TPU v7x, 128 devices: a whole 4x4x4 slice. The times are simulated.
128 devices in a mesh: seq: 32 (over x, y, core), head: 4 (over z).
Axes of the slice: x: 4, y: 4, z: 4, core: 2. Of those that a mesh axis runs over, the one named last changes fastest.
Arguments:
- group_of: int32 [32], replicated, may hold values from 0 to 31, as said below
- soft_query: bfloat16 [8192, 1536], P('seq', 'head'), may hold values from -8 to 8
- soft_key: bfloat16 [8192, 1536], P('seq', 'head'), may hold values from -8 to 8
- soft_value: bfloat16 [8192, 1536], P('seq', 'head'), may hold values from -6 to 6
- soft_grad: bfloat16 [8192, 1536], P('seq', 'head'), may hold values from -6 to 6
- lin_query: bfloat16 [8192, 1536], P('seq', 'head'), may hold values from -6 to 6
- lin_key: bfloat16 [8192, 1536], P('seq', 'head'), may hold values from -0.59765625 to 0.59765625
- lin_value: bfloat16 [8192, 1536], P('seq', 'head'), may hold values from -40 to 40
- log_decay: float32 [8192, 12], P('seq', 'head'), may hold values from -1 to 0
- lin_grad: bfloat16 [8192, 1536], P('seq', 'head'), may hold values from -6 to 6
Outputs:
- soft_out: bfloat16 [8192, 1536], P('seq', 'head')
- soft_dq: bfloat16 [8192, 1536], P('seq', 'head')
- soft_dk: bfloat16 [8192, 1536], P('seq', 'head')
- soft_dv: bfloat16 [8192, 1536], P('seq', 'head')
- lin_out: float32 [8192, 1536], P('seq', 'head')
- lin_dq: float32 [8192, 1536], P('seq', 'head')
- lin_dk: float32 [8192, 1536], P('seq', 'head')
- lin_dv: float32 [8192, 1536], P('seq', 'head')
Inputs may be any that keep to these rules, and one draw needn't show every extreme that they name: group_of[d] = (group_of[0] + d) mod 32: the indices of seq hold the sequence's blocks in order around the axis, from a drawn first index.
All inputs are finite; a program needn't handle non-finite values.
Results may differ from a plain program's by a relative error of at most 0.017.
Values may be sent and summed in bfloat16 or wider, within the bound.
No kernel may reach another device: no remote copies, remote signals or barrier semaphores. Data moves between devices by JAX's collectives and lax.ppermute only.
A program may use at most 128 MiB of HBM per device.

v0:
```python
import functools

import jax
import jax.numpy as jnp
from jax import lax
from jax.experimental import pallas as pl
from jax.experimental.pallas import tpu as pltpu
from jax.sharding import Mesh
from jax.sharding import PartitionSpec as P


HEAD_TOTAL = 12
HEAD_DIM = 128
HEADS = 3
WIDTH = HEADS * HEAD_DIM
TOK = 256
NX, NY, NC, NZ = 4, 4, 2, 4
LINE = NY * NC
EPS = 1e-06
SCALE = HEAD_DIM ** (-0.5)
LOG2E = 1.4426950408889634
NEG = -1e30
F32 = jnp.float32
BF16 = jnp.bfloat16
HIGHEST = lax.Precision.HIGHEST
SEQ = ("x", "y", "c")
OFFSETS = (1, 3, 2)
STATE_ROW = TOK
LOG_ROW = STATE_ROW + HEAD_DIM
PACK_ROWS = LOG_ROW + 16
ANY = pl.BlockSpec(memory_space=pl.ANY)


def send(block, axis, size, offset):
    return lax.ppermute(block, axis, [(i, (i + offset) % size) for i in range(size)])


def fetch(block, axis, size, offset):
    return send(block, axis, size, -offset)


def dot(a, b, dim_a, dim_b, precision=None):
    return lax.dot_general(
        a, b, (((dim_a,), (dim_b,)), ((), ())), precision=precision, preferred_element_type=F32
    )


def head_cols(h):
    return pl.ds(h * HEAD_DIM, HEAD_DIM)


def shaped(*dims, dtype=F32):
    return jax.ShapeDtypeStruct(dims, dtype)


def call(kernel, out_shape, flops, args, vmem=40, **kwargs):
    return pl.pallas_call(
        kernel,
        out_shape=out_shape,
        cost_estimate=pl.CostEstimate(flops=flops, transcendentals=2**18, bytes_accessed=2 * 2**20),
        compiler_params=pltpu.CompilerParams(vmem_limit_bytes=vmem * 2**20),
        **kwargs,
    )(*args)


def placed(in_specs, out_specs, scratch=(), grid=()):
    return {
        "grid_spec": pltpu.PrefetchScalarGridSpec(
            num_scalar_prefetch=2,
            grid=grid,
            in_specs=in_specs,
            out_specs=out_specs,
            scratch_shapes=list(scratch),
        )
    }


def position(group_ref, index_ref, along_x, side, along_y):
    index = index_ref[0]
    x, y, c = (index >> 3) + along_x, ((index >> 1) & 3) + along_y, (index & 1) + side
    return group_ref[(x & 3) * LINE + (y & 3) * NC + (c & 1)]


def flag(condition):
    return jnp.where(condition, 1, 0)


def key_scores(k, q, limit=None):
    s = dot(k, q, 1, 1) * (SCALE * LOG2E)
    if limit is not None:
        key_row = lax.broadcasted_iota(jnp.int32, s.shape, 0)
        query_col = lax.broadcasted_iota(jnp.int32, s.shape, 1)
        s = jnp.where(key_row - query_col <= limit, s, NEG)
    return s


def forward_kernel(
    side, group_ref, index_ref, q_ref, kv_0, kv_1, kv_2, kv_3, out_ref, stat_ref, k_ref, vt_ref
):
    h = pl.program_id(0)
    for o, kv_ref in enumerate((kv_0, kv_1, kv_2, kv_3)):
        k_ref[o] = kv_ref[0]
        vt_ref[o] = kv_ref[1].T
    key_pos = [position(group_ref, index_ref, o, 0, 0) for o in range(NX)]
    first = (4 - (key_pos[0] >> 3)) & 3

    @pl.when(h == 0)
    def _():
        stat_ref[...] = jnp.zeros_like(stat_ref)

    @pl.loop(0, NY)
    def _(i):
        query_pos = position(group_ref, index_ref, 0, side, i)
        count = sum(flag(p <= query_pos) for p in key_pos)
        limit = jnp.where(key_pos[0] == query_pos, 0, TOK)

        @pl.when(count == 0)
        def _():
            out_ref[i] = jnp.zeros((TOK, HEAD_DIM), BF16)
            stat_ref[i, pl.ds(h, 1)] = jnp.full((1, TOK), NEG, F32)

        for n in range(1, NX + 1):

            @pl.when(count == n)
            def _():
                q = q_ref[i]
                slots = [(first + m) & 3 for m in range(n)]
                parts = [
                    key_scores(k_ref[o], q, limit if m == n - 1 else None)
                    for m, o in enumerate(slots)
                ]
                top = jnp.max(parts[0], axis=0, keepdims=True)
                for s in parts[1:]:
                    top = jnp.maximum(top, jnp.max(s, axis=0, keepdims=True))
                total = jnp.zeros((1, TOK), F32)
                acc = jnp.zeros((HEAD_DIM, TOK), F32)
                for m, o in enumerate(slots):
                    p = jnp.exp2(parts[m] - top)
                    total = total + jnp.sum(p, axis=0, keepdims=True)
                    acc = acc + dot(vt_ref[o], p.astype(BF16), 1, 0)
                out_ref[i] = (acc / total).T.astype(BF16)
                stat_ref[i, pl.ds(h, 1)] = top + jnp.log(total) * LOG2E


def rows_spec(first=0):
    return pl.BlockSpec((NY, TOK, HEAD_DIM), lambda h, *_: (0, 0, h + first))


def pair_spec(first=0):
    return pl.BlockSpec((2, TOK, HEAD_DIM), lambda h, *_: (0, 0, h + first))


def soft_forward(place, side, q, kvs):
    return call(
        functools.partial(forward_kernel, side),
        [shaped(NY, TOK, WIDTH, dtype=BF16), shaped(NY, 8, TOK)],
        NY * NX * HEADS * 4 * TOK * TOK * HEAD_DIM,
        (*place, q, *kvs),
        **placed(
            [rows_spec()] + [pair_spec()] * NX,
            [rows_spec(), pl.BlockSpec((NY, 8, TOK), lambda h, *_: (0, 0, 0))],
            [pltpu.VMEM((NX, TOK, HEAD_DIM), BF16), pltpu.VMEM((NX, HEAD_DIM, TOK), BF16)],
            (HEADS,),
        ),
    )


def delta_kernel(g_a, g_b, out_a, out_b, stat_a, stat_b, part_ref):
    h = pl.program_id(0)

    @pl.when(h == 0)
    def _():
        part_ref[0] = stat_a[...]
        part_ref[1] = stat_b[...]

    for side, (g_ref, o_ref) in enumerate(((g_a, out_a), (g_b, out_b))):
        for i in range(NY):
            product = o_ref[i].astype(F32) * g_ref[i].astype(F32)
            part_ref[side, i, pl.ds(h + 4, 1)] = jnp.sum(product.T, axis=0, keepdims=True)


def tile_backward(k, v, kt, q, g, lse, delta, limit=None):
    p = jnp.exp2(key_scores(k, q, limit) - lse)
    ds = (p * (dot(v, g, 1, 1) - delta)).astype(BF16)
    return dot(ds, q, 1, 0), dot(p.astype(BF16), g, 1, 0), dot(kt, ds, 1, 0)


def far_kernel(
    first_head, group_ref, index_ref, qa_ref, qb_ref, ga_ref, gb_ref, kv_1, kv_2, kv_3, stat_ref,
    *refs,
):
    dqa_ref, dqb_ref, dkv_ref, k_ref, v_ref, kt_ref, acc_ref = refs[-7:]
    h = pl.program_id(0) + first_head
    for o, kv_ref in enumerate((kv_1, kv_2, kv_3)):
        k_ref[o] = kv_ref[0]
        v_ref[o] = kv_ref[1]
        kt_ref[o] = kv_ref[0].T
    acc_ref[...] = jnp.zeros_like(acc_ref)
    key_pos = [position(group_ref, index_ref, o, 0, 0) for o in range(NX)]
    first, own_rank = (4 - (key_pos[0] >> 3)) & 3, key_pos[0] >> 3

    def one_block(q_ref, g_ref, dq_ref, side, b):
        query_pos = position(group_ref, index_ref, 0, side, b)
        count = sum(flag(p <= query_pos) for p in key_pos[1:])

        @pl.when(count == 0)
        def _():
            dq_ref[b] = jnp.zeros((TOK, HEAD_DIM), F32)

        for n in range(1, NX):

            @pl.when(count == n)
            def _():
                q, g = q_ref[b], g_ref[b]
                lse = stat_ref[side, b, pl.ds(h, 1)]
                delta = stat_ref[side, b, pl.ds(h + 4, 1)]
                dqt = jnp.zeros((HEAD_DIM, TOK), F32)
                for m in range(n):
                    o = ((first + m + flag(own_rank <= m)) & 3) - 1
                    dk, dv, dq = tile_backward(k_ref[o], v_ref[o], kt_ref[o], q, g, lse, delta)
                    acc_ref[o, 0] += dk
                    acc_ref[o, 1] += dv
                    dqt = dqt + dq
                dq_ref[b] = dqt.T

    pl.loop(0, NY)(lambda b: one_block(qa_ref, ga_ref, dqa_ref, 0, b))
    pl.loop(0, NY)(lambda b: one_block(qb_ref, gb_ref, dqb_ref, 1, b))
    for o in range(NX - 1):
        dkv_ref[o, 0] = (acc_ref[o, 0] * SCALE).astype(BF16)
        dkv_ref[o, 1] = acc_ref[o, 1].astype(BF16)


STAT_SPEC = pl.BlockSpec((2, NY, 8, TOK), lambda h, *_: (0, 0, 0, 0))


def far_backward(place, first, heads, qa, qb, ga, gb, kvs, stats, earlier=()):
    rows, pair = rows_spec(first), pair_spec(first)
    kwargs = placed(
        [rows] * 4 + [pair] * (NX - 1) + [STAT_SPEC] + [ANY] * len(earlier),
        [
            rows,
            rows,
            pl.BlockSpec((NX - 1, 2, TOK, HEAD_DIM), lambda h, *_: (0, 0, 0, h + first)),
        ],
        [
            pltpu.VMEM((NX - 1, TOK, HEAD_DIM), BF16),
            pltpu.VMEM((NX - 1, TOK, HEAD_DIM), BF16),
            pltpu.VMEM((NX - 1, HEAD_DIM, TOK), BF16),
            pltpu.VMEM((NX - 1, 2, TOK, HEAD_DIM), F32),
        ],
        (heads,),
    )
    return call(
        functools.partial(far_kernel, first),
        [shaped(NY, TOK, WIDTH), shaped(NY, TOK, WIDTH), shaped(NX - 1, 2, TOK, WIDTH, dtype=BF16)],
        2 * NY * (NX - 1) * heads * 10 * TOK * TOK * HEAD_DIM,
        (*place, qa, qb, ga, gb, *kvs, stats, *earlier),
        input_output_aliases={10 + i: i for i in range(len(earlier))},
        **kwargs,
    )


def near_kernel(
    group_ref, index_ref, qa_ref, qb_ref, ga_ref, gb_ref, kv_ref, stat_ref, dqa_in, dqb_in,
    dqa_ref, dqb_ref, dkv_ref, kt_ref,
):
    h = pl.program_id(0)
    kt_ref[...] = kv_ref[0].T
    dkv_ref[...] = jnp.zeros_like(dkv_ref)
    own = position(group_ref, index_ref, 0, 0, 0)
    sides = ((qa_ref, ga_ref, dqa_in, dqa_ref), (qb_ref, gb_ref, dqb_in, dqb_ref))
    for side, (q_ref, g_ref, dq_in, dq_ref) in enumerate(sides):
        where = [position(group_ref, index_ref, 0, side, b) for b in range(NY)]
        count = sum(flag(p >= own) for p in where)

        @pl.when(count == 0)
        def _():
            for b in range(NY):
                dq_ref[b] = (dq_in[b] * SCALE).astype(BF16)

        @pl.when(count > 0)
        def _():
            dk_sum = jnp.zeros((TOK, HEAD_DIM), F32)
            dv_sum = jnp.zeros((TOK, HEAD_DIM), F32)
            for b in range(NY):
                limit = jnp.where(where[b] == own, 0, jnp.where(where[b] > own, TOK, -TOK))
                dk, dv, dq = tile_backward(
                    kv_ref[0], kv_ref[1], kt_ref[...], q_ref[b], g_ref[b],
                    stat_ref[side, b, pl.ds(h, 1)], stat_ref[side, b, pl.ds(h + 4, 1)], limit,
                )
                dk_sum = dk_sum + dk
                dv_sum = dv_sum + dv
                dq_ref[b] = ((dq_in[b] + dq.T) * SCALE).astype(BF16)
            dkv_ref[0] += dk_sum * SCALE
            dkv_ref[1] += dv_sum


def near_backward(place, qa, qb, ga, gb, kv, stats, dqa, dqb):
    rows, pair = rows_spec(), pair_spec()
    return call(
        near_kernel,
        [
            shaped(NY, TOK, WIDTH, dtype=BF16),
            shaped(NY, TOK, WIDTH, dtype=BF16),
            shaped(2, TOK, WIDTH),
        ],
        2 * NY * HEADS * 10 * TOK * TOK * HEAD_DIM,
        (*place, qa, qb, ga, gb, kv, stats, dqa, dqb),
        **placed(
            [rows] * 4 + [pair, STAT_SPEC, rows, rows],
            [rows, rows, pair],
            [pltpu.VMEM((HEAD_DIM, TOK), BF16)],
            (HEADS,),
        ),
    )


def merged(stats_a, stats_b):
    lse_a, lse_b = stats_a[..., :4, :], stats_b[..., :4, :]
    top = jnp.maximum(lse_a, lse_b)
    weight_a, weight_b = jnp.exp2(lse_a - top), jnp.exp2(lse_b - top)
    total = weight_a + weight_b
    delta = (weight_a * stats_a[..., 4:, :] + weight_b * stats_b[..., 4:, :]) / total
    return jnp.concatenate([top + jnp.log(total) * LOG2E, delta], axis=-2)


def chip_kernel(part_ref, other_ref, out_ref):
    for side in range(2):
        out_ref[side] = merged(part_ref[side], other_ref[1 - side])


def line_kernel(
    part_ref, chip_ref, from_1, from_2, from_3, out_a_ref, out_b_ref, read_ref,
    stat_ref, mine_ref, theirs_ref,
):
    for side, o_ref in enumerate((out_a_ref, out_b_ref)):
        for i in range(NY):
            stats = chip_ref[side, i]
            for o, other in ((1, from_1), (2, from_2), (3, from_3)):
                stats = merged(stats, other[side, (i - o) % NY])
            stat_ref[side, i] = stats
            weight = jnp.exp2(part_ref[side, i, :4] - stats[:4])
            weight = jnp.concatenate([weight] * (HEAD_DIM // 4), axis=0).T
            for h in range(HEADS):
                scaled = o_ref[i, :, head_cols(h)].astype(F32) * weight[:, h : h + 1]
                if side == 0:
                    mine_ref[i, :, head_cols(h)] = scaled
                else:
                    theirs_ref[pl.ds(i * TOK, TOK), head_cols(h)] = scaled.astype(BF16)
    theirs_ref[pl.ds(NY * TOK, HEAD_DIM)] = read_ref[...]


def join_kernel(mine_ref, core_ref, read_ref, own_ref, pay_1, pay_2, pay_3):
    own_ref[...] = mine_ref[0] + core_ref[pl.ds(0, TOK)].astype(F32)
    for o, pay in ((1, pay_1), (2, pay_2), (3, pay_3)):
        total = mine_ref[o] + core_ref[pl.ds(o * TOK, TOK)].astype(F32)
        pay[pl.ds(0, TOK)] = total.astype(BF16)
        pay[pl.ds(TOK, HEAD_DIM)] = read_ref[...]
        pay[pl.ds(TOK + HEAD_DIM, HEAD_DIM)] = core_ref[pl.ds(NY * TOK, HEAD_DIM)]


def triangle(upper):
    row = lax.broadcasted_iota(jnp.int32, (TOK, TOK), 0)
    col = lax.broadcasted_iota(jnp.int32, (TOK, TOK), 1)
    return row <= col if upper else row >= col


def decay_columns(decay_ref):
    return dot(triangle(False).astype(F32), decay_ref[...], 1, 1, HIGHEST)


def pack_kernel(q_ref, key_ref, value_ref, decay_ref, out_ref):
    cumulative = decay_columns(decay_ref)
    total = cumulative[TOK - 1 : TOK]
    tail = jnp.exp(total - cumulative)
    out_ref[pl.ds(0, TOK)] = q_ref[...]
    row = lax.broadcasted_iota(jnp.int32, (16, HEAD_DIM), 0)
    for h in range(HEADS):
        keys = key_ref[:, head_cols(h)].astype(F32) * tail[:, h : h + 1]
        state = dot(keys.astype(BF16), value_ref[:, head_cols(h)], 0, 0)
        out_ref[pl.ds(STATE_ROW, HEAD_DIM), head_cols(h)] = state.astype(BF16)
        log = jnp.broadcast_to(total[:, h : h + 1], (16, HEAD_DIM))
        high = log.astype(BF16).astype(F32)
        middle = (log - high).astype(BF16).astype(F32)
        low = log - high - middle
        piece = jnp.where(row == 0, high, jnp.where(row == 1, middle, jnp.where(row == 2, low, 0.0)))
        out_ref[pl.ds(LOG_ROW, 16), head_cols(h)] = piece.astype(BF16)


def least(values):
    return functools.reduce(jnp.minimum, values)


def chain_keys(group_ref, index_ref, along_x, forward):
    found = [
        position(group_ref, index_ref, along_x, side, j) for side in range(NC) for j in range(NY)
    ]
    return found if forward else [31 - p for p in found]


def chain_members(keys):
    apart = -least([-k for k in keys]) - least(keys) > LINE - 1
    handed = [flag(jnp.logical_or(k < LINE, jnp.logical_not(apart))) for k in keys]
    whole = flag(jnp.logical_not(apart))
    same = [jnp.maximum(whole, flag(flag(k < LINE) == flag(keys[0] < LINE))) for k in keys]
    return handed, same


def line_sums(keys, logs, states):
    handed, same = chain_members(keys)
    before = [s * flag(k < keys[0]) for s, k in zip(same, keys)]

    def weighted(members):
        total = jnp.zeros((HEAD_DIM, WIDTH), F32)
        for j in range(LINE):
            exponent = jnp.zeros((1, WIDTH), F32)
            for i in range(LINE):
                if i != j:
                    between = members[i] * flag(keys[i] > keys[j])
                    exponent = exponent + logs[i] * between.astype(F32)
            weight = jnp.exp(exponent) * members[j].astype(F32)
            total = total + weight * states[j]()
        return total

    prefix = sum(log * b.astype(F32) for log, b in zip(logs, before))
    return weighted(handed), weighted(before), prefix


def total_sums(group_ref, index_ref, forward, totals, line_logs, prefix):
    lines = [chain_keys(group_ref, index_ref, o, forward) for o in range(NX)]
    starts = [least(keys) for keys in lines]
    same = chain_members(lines[0])[1]
    own_start = least([jnp.where(s > 0, k, 99) for s, k in zip(same, lines[0])])
    earlier = [flag(s < own_start) for s in starts]
    result = jnp.zeros((HEAD_DIM, WIDTH), F32)
    for o in range(NX):
        exponent = prefix
        for i in range(NX):
            if i != o:
                between = earlier[i] * flag(starts[i] > starts[o])
                exponent = exponent + line_logs[i] * between.astype(F32)
        result = result + jnp.exp(exponent) * earlier[o].astype(F32) * totals[o]
    return result


def states_kernel(group_ref, index_ref, qa_ref, qb_ref, handed_ref, entry_ref, log_ref):
    logs, states = [], []
    for ref in (qa_ref, qb_ref):
        for i in range(NY):
            rows = ref[i, pl.ds(LOG_ROW, 16)].astype(F32)
            logs.append(rows[0:1] + rows[1:2] + rows[2:3])
            states.append(
                functools.partial(
                    lambda ref, i: ref[i, pl.ds(STATE_ROW, HEAD_DIM)].astype(F32), ref, i
                )
            )
    keys = chain_keys(group_ref, index_ref, 0, True)
    handed, entry, prefix = line_sums(keys, logs, states)
    handed_ref[pl.ds(0, HEAD_DIM)] = handed
    handed_ref[pl.ds(HEAD_DIM, 8)] = jnp.broadcast_to(sum(logs), (8, WIDTH))
    entry_ref[pl.ds(0, HEAD_DIM)] = entry
    entry_ref[pl.ds(HEAD_DIM, 8)] = jnp.broadcast_to(prefix, (8, WIDTH))
    for j in range(LINE):
        log_ref[pl.ds(j, 1)] = logs[j]


def inner_terms(q, k, decay_ref, cumulative, h):
    rows = dot(decay_ref[...], triangle(True).astype(F32), 1, 0, HIGHEST)
    gap = cumulative[:, h : h + 1] - rows[h : h + 1]
    decay = jnp.where(triangle(False), jnp.exp(jnp.minimum(gap, 0.0)), 0.0)
    return decay, (dot(q, k, 1, 1) * decay).astype(BF16)


def read_kernel(
    group_ref, index_ref, q_ref, k_ref, v_ref, g_ref, decay_ref, part_ref, own, from_1, from_2,
    from_3, raw_ref, sum_ref, entry_ref, log_ref,
):
    all_totals = (own, from_1, from_2, from_3)
    line_logs = [t[pl.ds(HEAD_DIM, 1)] for t in all_totals]
    for o in range(NX):
        log_ref[pl.ds(o, 1)] = line_logs[o]
    log_ref[pl.ds(NX, 4)] = jnp.zeros((4, WIDTH), F32)
    entry = part_ref[pl.ds(0, HEAD_DIM)] + total_sums(
        group_ref, index_ref, True, [t[pl.ds(0, HEAD_DIM)] for t in all_totals], line_logs,
        part_ref[pl.ds(HEAD_DIM, 1)],
    )
    entry_ref[...] = entry.astype(BF16)
    cumulative = decay_columns(decay_ref)
    squares = jnp.zeros((TOK, 1), F32)
    inner = jnp.zeros((TOK, 1), F32)
    for h in range(HEADS):
        cols = head_cols(h)
        q = q_ref[:, cols]
        scores = inner_terms(q, k_ref[:, cols], decay_ref, cumulative, h)[1]
        carried = dot(q, entry_ref[:, cols], 1, 0)
        raw = dot(scores, v_ref[:, cols], 1, 0) + jnp.exp(cumulative[:, h : h + 1]) * carried
        raw_ref[:, cols] = raw
        squares = squares + jnp.sum(raw * raw, axis=1, keepdims=True)
        inner = inner + jnp.sum(raw * g_ref[:, cols].astype(F32), axis=1, keepdims=True)
    lane = lax.broadcasted_iota(jnp.int32, (TOK, HEAD_DIM), 1)
    sums = jnp.where(lane == 0, squares, jnp.where(lane == 1, inner, 0.0))
    sum_ref[...] = sums.T[:8]


def grad_kernel(
    q_ref, k_ref, v_ref, g_ref, decay_ref, entry_ref, raw_ref, sum_0, sum_1, sum_2, sum_3,
    out_ref, dq_ref, dk_ref, dv_ref, read_ref,
):
    cumulative = decay_columns(decay_ref)
    sums = (sum_0[...] + sum_1[...]) + (sum_2[...] + sum_3[...])
    sums = jnp.concatenate([sums] * (HEAD_DIM // 8), axis=0).T
    inverse = 1.0 / jnp.sqrt(sums[:, 0:1] * (1.0 / (HEAD_TOTAL * HEAD_DIM)) + EPS)
    aligned = sums[:, 1:2] * inverse * (1.0 / (HEAD_TOTAL * HEAD_DIM))
    for h in range(HEADS):
        cols = head_cols(h)
        q, k = q_ref[:, cols], k_ref[:, cols]
        out = raw_ref[:, cols] * inverse
        out_ref[:, cols] = out
        raw_grad = ((g_ref[:, cols].astype(F32) - out * aligned) * inverse).astype(BF16)
        decay, scores = inner_terms(q, k, decay_ref, cumulative, h)
        head_decay = jnp.exp(cumulative[:, h : h + 1])
        inner_grad = (dot(raw_grad, v_ref[:, cols], 1, 1) * decay).astype(BF16)
        carried = dot(raw_grad, entry_ref[:, cols], 1, 1)
        dq_ref[:, cols] = dot(inner_grad, k, 1, 0) + head_decay * carried
        dk_ref[:, cols] = dot(inner_grad, q, 0, 0)
        dv_ref[:, cols] = dot(scores, raw_grad, 0, 0)
        scaled = (q.astype(F32) * head_decay).astype(BF16)
        read_ref[:, cols] = dot(scaled, raw_grad, 0, 0).astype(BF16)


def back_kernel(
    group_ref, index_ref, log_ref, read_ref, core_ref, from_1, from_2, from_3, handed_ref, part_ref
):
    logs = [log_ref[pl.ds(j, 1)] for j in range(LINE)]
    sources = [(read_ref, 0), (from_1, TOK), (from_2, TOK), (from_3, TOK)]
    sources += [(core_ref, NY * TOK)]
    sources += [(ref, TOK + HEAD_DIM) for ref in (from_1, from_2, from_3)]
    states = [
        functools.partial(lambda ref, row: ref[pl.ds(row, HEAD_DIM)].astype(F32), ref, row)
        for ref, row in sources
    ]
    keys = chain_keys(group_ref, index_ref, 0, False)
    handed, part, prefix = line_sums(keys, logs, states)
    handed_ref[...] = handed
    part_ref[pl.ds(0, HEAD_DIM)] = part
    part_ref[pl.ds(HEAD_DIM, 8)] = jnp.broadcast_to(prefix, (8, WIDTH))


def write_kernel(
    group_ref, index_ref, k_ref, v_ref, decay_ref, part_ref, log_ref, own, from_1, from_2, from_3,
    dk_in, dv_in, dk_ref, dv_ref,
):
    leave_all = part_ref[pl.ds(0, HEAD_DIM)] + total_sums(
        group_ref, index_ref, False, [t[...] for t in (own, from_1, from_2, from_3)],
        [log_ref[pl.ds(o, 1)] for o in range(NX)], part_ref[pl.ds(HEAD_DIM, 1)],
    )
    cumulative = decay_columns(decay_ref)
    tail = jnp.exp(cumulative[TOK - 1 : TOK] - cumulative)
    for h in range(HEADS):
        cols = head_cols(h)
        leave = leave_all[:, h * HEAD_DIM : (h + 1) * HEAD_DIM].astype(BF16)
        scale = tail[:, h : h + 1]
        dk_ref[:, cols] = dk_in[:, cols] + scale * dot(v_ref[:, cols], leave, 1, 1)
        dv_ref[:, cols] = dv_in[:, cols] + scale * dot(k_ref[:, cols], leave, 1, 0)


def in_vmem(n):
    return [pl.BlockSpec(memory_space=pltpu.VMEM)] * n


def on_device(
    group_of, soft_query, soft_key, soft_value, soft_grad,
    lin_query, lin_key, lin_value, log_decay, lin_grad,
):
    place = (group_of, lax.axis_index(SEQ).reshape(1))
    decay = log_decay.T

    kv_own = jnp.stack([soft_key, soft_value])
    kv = {0: kv_own, **{o: fetch(kv_own, "x", NX, o) for o in OFFSETS}}
    kvs = [kv[o] for o in range(NX)]
    packed = call(
        pack_kernel,
        shaped(PACK_ROWS, WIDTH, dtype=BF16),
        2**26,
        (soft_query, lin_key, lin_value, decay),
        vmem=60,
    )
    q_from = {0: packed, **{o: fetch(packed, "y", NY, o) for o in OFFSETS}}
    g_from = {0: soft_grad, **{o: fetch(soft_grad, "y", NY, o) for o in OFFSETS}}
    qa = jnp.stack([q_from[o] for o in range(NY)])
    qb = fetch(qa, "c", NC, 1)
    ga = jnp.stack([g_from[o] for o in range(NY)])
    gb = fetch(ga, "c", NC, 1)

    out_a, stat_a = soft_forward(place, 0, qa, kvs)
    handed, entry_part, logs = call(
        states_kernel,
        [shaped(HEAD_DIM + 8, WIDTH), shaped(HEAD_DIM + 8, WIDTH), shaped(8, WIDTH)],
        2**24,
        (*place, qa, qb),
        **placed(in_vmem(2), in_vmem(3)),
    )
    totals = [handed, *(fetch(handed, "x", NX, o) for o in (1, 2, 3))]
    out_b, stat_b = soft_forward(place, 1, qb, kvs)
    part = call(
        delta_kernel,
        shaped(2, NY, 8, TOK),
        2**25,
        (ga, gb, out_a, out_b, stat_a, stat_b),
        grid=(HEADS,),
        in_specs=[rows_spec()] * 4 + [pl.BlockSpec((NY, 8, TOK), lambda h: (0, 0, 0))] * 2,
        out_specs=pl.BlockSpec((2, NY, 8, TOK), lambda h: (0, 0, 0, 0)),
    )
    other = fetch(part, "c", NC, 1)

    rows = shaped(TOK, WIDTH)
    raw, sums, entry, line_logs = call(
        read_kernel,
        [rows, shaped(8, TOK), shaped(HEAD_DIM, WIDTH, dtype=BF16), shaped(8, WIDTH)],
        2**27,
        (*place, lin_query, lin_key, lin_value, lin_grad, decay, entry_part, *totals),
        **placed(in_vmem(10), in_vmem(4)),
    )
    all_sums = [sums, *(fetch(sums, "head", NZ, o) for o in (1, 2, 3))]
    chip = call(chip_kernel, shaped(2, NY, 8, TOK), 2**20, (part, other))
    received = {o: fetch(chip, "y", NY, o) for o in OFFSETS}
    lin_out, lin_dq, dk_local, dv_local, read_grad = call(
        grad_kernel,
        [rows] * 4 + [shaped(HEAD_DIM, WIDTH, dtype=BF16)],
        2**28,
        (lin_query, lin_key, lin_value, lin_grad, decay, entry, raw, *all_sums),
    )
    stats, mine, theirs = call(
        line_kernel,
        [
            shaped(2, NY, 8, TOK),
            shaped(NY, TOK, WIDTH),
            shaped(NY * TOK + HEAD_DIM, WIDTH, dtype=BF16),
        ],
        2**22,
        (part, chip, received[1], received[2], received[3], out_a, out_b, read_grad),
    )
    from_core = fetch(theirs, "c", NC, 1)

    grads = far_backward(place, 0, 1, qa, qb, ga, gb, kvs[1:], stats)
    own_out, *pays = call(
        join_kernel,
        [rows] + [shaped(2 * TOK, WIDTH, dtype=BF16)] * 3,
        2**22,
        (mine, from_core, read_grad),
    )
    sent_out = {o: send(pays[o - 1], "y", NY, o) for o in OFFSETS}
    dq_a, dq_b, far_dkv = far_backward(place, 1, 2, qa, qb, ga, gb, kvs[1:], stats, tuple(grads))
    sent_dkv = [send(far_dkv[o - 1], "x", NX, o) for o in OFFSETS]
    dq_a, dq_b, near_dkv = near_backward(place, qa, qb, ga, gb, kvs[0], stats, dq_a, dq_b)
    dq_core = fetch(dq_b, "c", NC, 1)

    back_handed, leave_part = call(
        back_kernel,
        [shaped(HEAD_DIM, WIDTH), shaped(HEAD_DIM + 8, WIDTH)],
        2**24,
        (*place, logs, read_grad, from_core, *(sent_out[NY - o] for o in (1, 2, 3))),
        **placed(in_vmem(6), in_vmem(2)),
    )
    back_totals = [back_handed, *(fetch(back_handed, "x", NX, o) for o in (1, 2, 3))]
    chip_dq = dq_a.astype(F32) + dq_core.astype(F32)
    soft_dq = chip_dq[0]
    for o in OFFSETS:
        soft_dq = soft_dq + send(chip_dq[o].astype(BF16), "y", NY, o).astype(F32)
    lin_dk, lin_dv = call(
        write_kernel,
        [rows, rows],
        2**26,
        (*place, lin_key, lin_value, decay, leave_part, line_logs, *back_totals, dk_local, dv_local),
        **placed(in_vmem(11), in_vmem(2)),
    )
    soft_out = own_out
    for o in OFFSETS:
        soft_out = soft_out + sent_out[o][:TOK].astype(F32)
    dkv = near_dkv
    for sent in sent_dkv:
        dkv = dkv + sent.astype(F32)
    return (
        soft_out.astype(BF16), soft_dq.astype(BF16), dkv[0].astype(BF16), dkv[1].astype(BF16),
        lin_out, lin_dq, lin_dk, lin_dv,
    )


def solution(mesh):
    grid = Mesh(mesh.devices.reshape(NX, NY, NC, NZ), (*SEQ, "head"))
    block = P(SEQ, "head")

    return jax.shard_map(
        on_device,
        mesh=grid,
        in_specs=(P(),) + (block,) * 9,
        out_specs=(block,) * 8,
        check_vma=False,
    )
```

profile of v0, /device:TPU:8, one launch (start us, length us, event | category | flops | bytes accessed | tf_op | source)
XLA Modules:
  0.0 216.5 jit_solution(2284642226532173855)
XLA Ops:
  0.6 2.7 %shard_map.161 = bf16[400,384]{1,0:T(8,128)(2,1)} custom-call(bf16[256,384]{1,0:T(8,128)(2,1)} %q_ref.3, bf16[256,384]{1,0:T(8,128)(2,1)} %k_ref.5, bf16[256,384]{1,0:T(8,128)(2,1)} %v_ref.5, f32[3,256]{1,0:T(4,128)} %bitcast.38), custom_call_target="tpu_custom_call" | custom-call | flops 67108864 | bytes 2097152 | tf_op jit(solution)/shard_map/pallas_call | solution.py:57
  3.3 1.6 collective-permute-start.6
  5.7 2.5 %collective-permute-start.4 = (bf16[400,384]{1,0:T(8,128)(2,1)}, bf16[400,384]{1,0:T(8,128)(2,1)S(1)}, u32[]{:S(2)}, u32[]{:S(2)}) collective-permute-start(bf16[400,384]{1,0:T(8,128)(2,1)} %shard_map.161), channel_id=1, source_target_pairs={{0,24},{8,0},{16,8},{24,16},{1,25},{9,1},{17,9},{25,17},{2,26},{10... | collective-permute-start | bytes 921608 | tf_op jit(solution)/shard_map/ppermute | solution.py:35
  8.2 5.4 %collective-permute-done.6 = bf16[400,384]{1,0:T(8,128)(2,1)S(1)} collective-permute-done((bf16[400,384]{1,0:T(8,128)(2,1)}, bf16[400,384]{1,0:T(8,128)(2,1)S(1)}, u32[]{:S(2)}, u32[]{:S(2)}) %collective-permute-start.6) | collective-permute-done | bytes 307232 | tf_op jit(solution)/shard_map/ppermute | solution.py:35
  13.6 3.1 %collective-permute-done.5 = bf16[400,384]{1,0:T(8,128)(2,1)S(1)} collective-permute-done((bf16[400,384]{1,0:T(8,128)(2,1)}, bf16[400,384]{1,0:T(8,128)(2,1)S(1)}, u32[]{:S(2)}, u32[]{:S(2)}) %collective-permute-start.5) | collective-permute-done | bytes 307232 | tf_op jit(solution)/shard_map/ppermute | solution.py:35
  16.7 4.4 %collective-permute-done.4 = bf16[400,384]{1,0:T(8,128)(2,1)S(1)} collective-permute-done((bf16[400,384]{1,0:T(8,128)(2,1)}, bf16[400,384]{1,0:T(8,128)(2,1)S(1)}, u32[]{:S(2)}, u32[]{:S(2)}) %collective-permute-start.4) | collective-permute-done | bytes 307232 | tf_op jit(solution)/shard_map/ppermute | solution.py:35
  24.6 3.0 %collective-permute-start.1 = (bf16[256,384]{1,0:T(8,128)(2,1)S(1)}, bf16[256,384]{1,0:T(8,128)(2,1)S(1)}, u32[]{:S(2)}, u32[]{:S(2)}) collective-permute-start(bf16[256,384]{1,0:T(8,128)(2,1)S(1)} %copy-done.6), channel_id=1, source_target_pairs={{0,16},{8,24},{16,0},{24,8},{1,17},{9,25},{17,1},{25,9},{2,18},{10... | collective-permute-start | bytes 589832 | tf_op jit(solution)/shard_map/ppermute | solution.py:35
  27.5 2.2 %collective-permute-done = bf16[256,384]{1,0:T(8,128)(2,1)S(1)} collective-permute-done((bf16[256,384]{1,0:T(8,128)(2,1)S(1)}, bf16[256,384]{1,0:T(8,128)(2,1)S(1)}, u32[]{:S(2)}, u32[]{:S(2)}) %collective-permute-start) | collective-permute-done | bytes 196640 | tf_op jit(solution)/shard_map/ppermute | solution.py:35
  29.8 1.5 collective-permute-done.2
  31.2 3.6 %collective-permute-done.1 = bf16[256,384]{1,0:T(8,128)(2,1)S(1)} collective-permute-done((bf16[256,384]{1,0:T(8,128)(2,1)S(1)}, bf16[256,384]{1,0:T(8,128)(2,1)S(1)}, u32[]{:S(2)}, u32[]{:S(2)}) %collective-permute-start.1) | collective-permute-done | bytes 196640 | tf_op jit(solution)/shard_map/ppermute | solution.py:35
  35.8 1.5 collective-permute-start.9
  37.3 2.7 %collective-permute-start.8 = (bf16[2,256,384]{2,1,0:T(8,128)(2,1)}, bf16[2,256,384]{2,1,0:T(8,128)(2,1)}, u32[]{:S(2)}, u32[]{:S(2)}) collective-permute-start(bf16[2,256,384]{2,1,0:T(8,128)(2,1)} %pad_maximum_fusion.2.kv_0.kv_ref), channel_id=1, source_target_pairs={{0,64},{32,96},{64,0},{96,32},{1,65},{33,97},{65,1},{97,33},{2,66}... | collective-permute-start | bytes 1179656 | tf_op jit(solution)/shard_map/ppermute | solution.py:35
  40.0 1.4 collective-permute-start.7
  41.5 7.4 %collective-permute-done.9.kv_3 = bf16[2,256,384]{2,1,0:T(8,128)(2,1)} collective-permute-done((bf16[2,256,384]{2,1,0:T(8,128)(2,1)}, bf16[2,256,384]{2,1,0:T(8,128)(2,1)}, u32[]{:S(2)}, u32[]{:S(2)}) %collective-permute-start.9) | collective-permute-done | bytes 393248 | tf_op jit(solution)/shard_map/ppermute | solution.py:35
  48.9 9.4 %collective-permute-done.8.kv_2 = bf16[2,256,384]{2,1,0:T(8,128)(2,1)} collective-permute-done((bf16[2,256,384]{2,1,0:T(8,128)(2,1)}, bf16[2,256,384]{2,1,0:T(8,128)(2,1)}, u32[]{:S(2)}, u32[]{:S(2)}) %collective-permute-start.8) | collective-permute-done | bytes 393248 | tf_op jit(solution)/shard_map/ppermute | solution.py:35
  58.3 11.0 %shard_map.162 = (bf16[4,256,384]{2,1,0:T(8,128)(2,1)S(1)}, f32[4,8,256]{2,1,0:T(8,128)S(1)}) custom-call(s32[32]{0:T(128)S(1)} %copy-done.5, s32[1]{0:T(128)} %bitcast.4.index_ref, bf16[4,400,384]{2,1,0:T(8,128)(2,1)S(1)} %pad_maximum_fusion.q_ref.qa_ref, bf16[2,256,384]{2,1,0:T(8,128)(2,1)} %pad_maximum_fusion.2.kv_0.kv_ref, ...), custom_call_target="tpu_custom_call" | custom-call | flops 1610612736 | bytes 2097152 | tf_op jit(solution)/shard_map/pallas_call | solution.py:57
  70.3 3.1 %collective-permute-start.17 = (f32[136,384]{1,0:T(8,128)S(1)}, f32[136,384]{1,0:T(8,128)S(1)}, u32[]{:S(2)}, u32[]{:S(2)}) collective-permute-start(f32[136,384]{1,0:T(8,128)S(1)} %get-tuple-element.49.own), channel_id=1, source_target_pairs={{0,32},{32,64},{64,96},{96,0},{1,33},{33,65},{65,97},{97,1},{2,34}... | collective-permute-start | bytes 626696 | tf_op jit(solution)/shard_map/ppermute | solution.py:35
  73.4 2.8 %collective-permute-start.15 = (f32[136,384]{1,0:T(8,128)S(1)}, f32[136,384]{1,0:T(8,128)S(1)}, u32[]{:S(2)}, u32[]{:S(2)}) collective-permute-start(f32[136,384]{1,0:T(8,128)S(1)} %get-tuple-element.49.own), channel_id=1, source_target_pairs={{0,96},{32,0},{64,32},{96,64},{1,97},{33,1},{65,33},{97,65},{2,98}... | collective-permute-start | bytes 626696 | tf_op jit(solution)/shard_map/ppermute | solution.py:35
  76.2 11.0 %shard_map.163 = (bf16[4,256,384]{2,1,0:T(8,128)(2,1)S(1)}, f32[4,8,256]{2,1,0:T(8,128)S(1)}) custom-call(s32[32]{0:T(128)S(1)} %copy-done.5, s32[1]{0:T(128)} %bitcast.4.index_ref, bf16[4,400,384]{2,1,0:T(8,128)(2,1)S(1)} %collective-permute-done.10.q_ref.qb_ref, bf16[2,256,384]{2,1,0:T(8,128)(2,1)} %pad_maximum_fusion.2.kv_0.kv_ref, ...), custom_call_target="tpu_custom_call" | custom-call | flops 1610612736 | bytes 2097152 | tf_op jit(solution)/shard_map/pallas_call | solution.py:57
  87.3 2.9 %shard_map.164.part_ref = f32[2,4,8,256]{3,2,1,0:T(8,128)S(1)} custom-call(bf16[4,256,384]{2,1,0:T(8,128)(2,1)S(1)} %pad_maximum_fusion.1.g_a.ga_ref, bf16[4,256,384]{2,1,0:T(8,128)(2,1)} %collective-permute-done.3.g_b.gb_ref, bf16[4,256,384]{2,1,0:T(8,128)(2,1)S(1)} %get-tuple-element.44.out_a.out_a_ref, ...), custom_call_target="tpu_custom_call" | custom-call | flops 33554432 | bytes 2097152 | tf_op jit(solution)/shard_map/pallas_call | solution.py:57
  92.4 5.0 %collective-permute-start.13 = (f32[2,4,8,256]{3,2,1,0:T(8,128)S(1)}, f32[2,4,8,256]{3,2,1,0:T(8,128)S(1)}, u32[]{:S(2)}, u32[]{:S(2)}) collective-permute-start(f32[2,4,8,256]{3,2,1,0:T(8,128)S(1)} %shard_map.165.chip_ref), channel_id=1, source_target_pairs={{0,16},{8,24},{16,0},{24,8},{1,17},{9,25},{17,1},{25,9},{2,18},{10... | collective-permute-start | bytes 196616 | tf_op jit(solution)/shard_map/ppermute | solution.py:35
  97.5 2.2 %shard_map.167 = (f32[256,384]{1,0:T(8,128)S(1)}, f32[8,256]{1,0:T(8,128)S(1)}, bf16[128,384]{1,0:T(8,128)(2,1)S(1)}, f32[8,384]{1,0:T(8,128)S(1)}) custom-call(s32[32]{0:T(128)S(1)} %copy-done.5, s32[1]{0:T(128)} %bitcast.4.index_ref, bf16[256,384]{1,0:T(8,128)(2,1)S(1)} %copy-done.2, bf16[256,384]{1,0:T(8,128)(2,1)S(1)} %copy-done, ...), custom_call_target="tpu_custom_call" | custom-call | flops 134217728 | bytes 2097152 | tf_op jit(solution)/shard_map/pallas_call | solution.py:57
  99.7 2.0 collective-permute-start.20
  101.7 3.6 %collective-permute-start.19 = (f32[8,256]{1,0:T(8,128)S(1)}, f32[8,256]{1,0:T(8,128)S(1)}, u32[]{:S(2)}, u32[]{:S(2)}) collective-permute-start(f32[8,256]{1,0:T(8,128)S(1)} %get-tuple-element.52.sum_0), channel_id=1, source_target_pairs={{0,2},{1,3},{2,0},{3,1},{4,6},{5,7},{6,4},{7,5},{8,10},{9,11},{10,... | collective-permute-start | bytes 24584 | tf_op jit(solution)/shard_map/ppermute | solution.py:35
  105.4 2.0 collective-permute-start.18
  107.5 1.6 collective-permute-done.18.sum_1
  109.1 2.5 %shard_map.168 = (f32[256,384]{1,0:T(8,128)}, f32[256,384]{1,0:T(8,128)}, f32[256,384]{1,0:T(8,128)S(1)}, f32[256,384]{1,0:T(8,128)S(1)}, bf16[128,384]{1,0:T(8,128)(2,1)S(1)}) custom-call(bf16[256,384]{1,0:T(8,128)(2,1)S(1)} %copy-done.2, bf16[256,384]{1,0:T(8,128)(2,1)S(1)} %copy-done, bf16[256,384]{1,0:T(8,128)(2,1)S(1)} %copy-done.1, ...), custom_call_target="tpu_custom_call" | custom-call | flops 268435456 | bytes 2097152 | tf_op jit(solution)/shard_map/pallas_call | solution.py:57
  111.6 1.3 shard_map.169
  112.9 8.4 %shard_map.171 = (f32[4,256,384]{2,1,0:T(8,128)S(1)}, f32[4,256,384]{2,1,0:T(8,128)S(1)}, bf16[3,2,256,384]{3,2,1,0:T(8,128)(2,1)S(1)}) custom-call(s32[32]{0:T(128)S(1)} %copy-done.5, s32[1]{0:T(128)} %bitcast.4.index_ref, bf16[4,400,384]{2,1,0:T(8,128)(2,1)S(1)} %pad_maximum_fusion.q_ref.qa_ref, ...), custom_call_target="tpu_custom_call" | custom-call | flops 2013265920 | bytes 2097152 | tf_op jit(solution)/shard_map/pallas_call | solution.py:57
  121.3 15.2 %shard_map.172 = (f32[4,256,384]{2,1,0:T(8,128)S(1)}, f32[4,256,384]{2,1,0:T(8,128)S(1)}, bf16[3,2,256,384]{3,2,1,0:T(8,128)(2,1)S(1)}) custom-call(s32[32]{0:T(128)S(1)} %copy-done.5, s32[1]{0:T(128)} %bitcast.4.index_ref, bf16[4,400,384]{2,1,0:T(8,128)(2,1)S(1)} %pad_maximum_fusion.q_ref.qa_ref, ...), custom_call_target="tpu_custom_call", output_to_operand_aliasing={{0}: (10, {}), {1}: (11, {}), {2}: (12, {})} | custom-call | flops 4026531840 | bytes 2097152 | tf_op jit(solution)/shard_map/pallas_call | solution.py:57
  136.5 9.8 %shard_map.173 = (bf16[4,256,384]{2,1,0:T(8,128)(2,1)S(1)}, bf16[4,256,384]{2,1,0:T(8,128)(2,1)S(1)}, f32[2,256,384]{2,1,0:T(8,128)S(1)}) custom-call(s32[32]{0:T(128)S(1)} %copy-done.5, s32[1]{0:T(128)} %bitcast.4.index_ref, bf16[4,400,384]{2,1,0:T(8,128)(2,1)S(1)} %pad_maximum_fusion.q_ref.qa_ref, ...), custom_call_target="tpu_custom_call" | custom-call | flops 2013265920 | bytes 2097152 | tf_op jit(solution)/shard_map/pallas_call | solution.py:57
  147.0 6.5 %collective-permute-start.29 = (bf16[2,256,384]{2,1,0:T(8,128)(2,1)S(1)}, bf16[2,256,384]{2,1,0:T(8,128)(2,1)S(1)}, u32[]{:S(2)}, u32[]{:S(2)}) collective-permute-start(bf16[2,256,384]{2,1,0:T(8,128)(2,1)S(1)} %get-tuple-element.82), channel_id=1, source_target_pairs={{0,32},{32,64},{64,96},{96,0},{1,33},{33,65},{65,97},{97,1},{2,34}... | collective-permute-start | bytes 1179656 | tf_op jit(solution)/shard_map/ppermute | solution.py:35
  153.5 2.8 %collective-permute-start.30 = (bf16[2,256,384]{2,1,0:T(8,128)(2,1)S(1)}, bf16[2,256,384]{2,1,0:T(8,128)(2,1)S(1)}, u32[]{:S(2)}, u32[]{:S(2)}) collective-permute-start(bf16[2,256,384]{2,1,0:T(8,128)(2,1)S(1)} %get-tuple-element.84), channel_id=1, source_target_pairs={{0,96},{32,0},{64,32},{96,64},{1,97},{33,1},{65,33},{97,65},{2,98}... | collective-permute-start | bytes 1179656 | tf_op jit(solution)/shard_map/ppermute | solution.py:35
  156.6 2.3 %collective-permute-start.26 = (bf16[256,384]{1,0:T(8,128)(2,1)S(1)}, bf16[256,384]{1,0:T(8,128)(2,1)S(1)}, u32[]{:S(2)}, u32[]{:S(2)}) collective-permute-start(bf16[256,384]{1,0:T(8,128)(2,1)S(1)} %get-tuple-element.85), channel_id=1, source_target_pairs={{0,8},{8,16},{16,24},{24,0},{1,9},{9,17},{17,25},{25,1},{2,10},{10... | collective-permute-start | bytes 589832 | tf_op jit(solution)/shard_map/ppermute | solution.py:35
  158.9 8.9 %collective-permute-done.29 = bf16[2,256,384]{2,1,0:T(8,128)(2,1)S(1)} collective-permute-done((bf16[2,256,384]{2,1,0:T(8,128)(2,1)S(1)}, bf16[2,256,384]{2,1,0:T(8,128)(2,1)S(1)}, u32[]{:S(2)}, u32[]{:S(2)}) %collective-permute-start.29) | collective-permute-done | bytes 393248 | tf_op jit(solution)/shard_map/ppermute | solution.py:35
  167.8 2.8 %collective-permute-done.31 = bf16[2,256,384]{2,1,0:T(8,128)(2,1)S(1)} collective-permute-done((bf16[2,256,384]{2,1,0:T(8,128)(2,1)S(1)}, bf16[2,256,384]{2,1,0:T(8,128)(2,1)S(1)}, u32[]{:S(2)}, u32[]{:S(2)}) %collective-permute-start.31) | collective-permute-done | bytes 393248 | tf_op jit(solution)/shard_map/ppermute | solution.py:35
  172.7 3.2 %collective-permute-start.27 = (bf16[256,384]{1,0:T(8,128)(2,1)S(1)}, bf16[256,384]{1,0:T(8,128)(2,1)S(1)}, u32[]{:S(2)}, u32[]{:S(2)}) collective-permute-start(bf16[256,384]{1,0:T(8,128)(2,1)S(1)} %get-tuple-element.87), channel_id=1, source_target_pairs={{0,24},{8,0},{16,8},{24,16},{1,25},{9,1},{17,9},{25,17},{2,26},{10... | collective-permute-start | bytes 589832 | tf_op jit(solution)/shard_map/ppermute | solution.py:35
  176.2 2.0 collective-permute-start.23
  179.6 1.4 collective-permute-done.28
  181.0 2.9 %collective-permute-done.27 = bf16[256,384]{1,0:T(8,128)(2,1)S(1)} collective-permute-done((bf16[256,384]{1,0:T(8,128)(2,1)S(1)}, bf16[256,384]{1,0:T(8,128)(2,1)S(1)}, u32[]{:S(2)}, u32[]{:S(2)}) %collective-permute-start.27) | collective-permute-done | bytes 196640 | tf_op jit(solution)/shard_map/ppermute | solution.py:35
  184.6 5.4 %collective-permute-done.22.from_3 = bf16[512,384]{1,0:T(8,128)(2,1)S(1)} collective-permute-done((bf16[512,384]{1,0:T(8,128)(2,1)S(1)}, bf16[512,384]{1,0:T(8,128)(2,1)S(1)}, u32[]{:S(2)}, u32[]{:S(2)}) %collective-permute-start.22) | collective-permute-done | bytes 393248 | tf_op jit(solution)/shard_map/ppermute | solution.py:35
  190.0 1.8 collective-permute-done.23.from_1
  191.8 8.8 %collective-permute-done.24.from_2 = bf16[512,384]{1,0:T(8,128)(2,1)S(1)} collective-permute-done((bf16[512,384]{1,0:T(8,128)(2,1)S(1)}, bf16[512,384]{1,0:T(8,128)(2,1)S(1)}, u32[]{:S(2)}, u32[]{:S(2)}) %collective-permute-start.24) | collective-permute-done | bytes 393248 | tf_op jit(solution)/shard_map/ppermute | solution.py:35
  201.6 2.9 %collective-permute-start.34 = (f32[128,384]{1,0:T(8,128)S(1)}, f32[128,384]{1,0:T(8,128)S(1)}, u32[]{:S(2)}, u32[]{:S(2)}) collective-permute-start(f32[128,384]{1,0:T(8,128)S(1)} %get-tuple-element.75.own), channel_id=1, source_target_pairs={{0,32},{32,64},{64,96},{96,0},{1,33},{33,65},{65,97},{97,1},{2,34}... | collective-permute-start | bytes 589832 | tf_op jit(solution)/shard_map/ppermute | solution.py:35
  204.6 1.7 collective-permute-start.33
  206.3 1.6 collective-permute-start.32
  209.8 4.6 %collective-permute-done.33.from_2 = f32[128,384]{1,0:T(8,128)S(1)} collective-permute-done((f32[128,384]{1,0:T(8,128)S(1)}, f32[128,384]{1,0:T(8,128)S(1)}, u32[]{:S(2)}, u32[]{:S(2)}) %collective-permute-start.33) | collective-permute-done | bytes 196640 | tf_op jit(solution)/shard_map/ppermute | solution.py:35
  214.5 2.0 shard_map.175
  (65 shorter events, 17.2 us)
Async XLA Ops:
  3.3 10.4 %collective-permute-start.6 = (bf16[400,384]{1,0:T(8,128)(2,1)}, bf16[400,384]{1,0:T(8,128)(2,1)S(1)}, u32[]{:S(2)}, u32[]{:S(2)}) collective-permute-start(bf16[400,384]{1,0:T(8,128)(2,1)} %shard_map.161), channel_id=1, source_target_pairs={{0,8},{8,16},{16,24},{24,0},{1,9},{9,17},{17,25},{25,1},{2,10},{10... | collective-permute-start | bytes 921608 | tf_op jit(solution)/shard_map/ppermute | solution.py:35
  4.9 11.9 %collective-permute-start.5 = (bf16[400,384]{1,0:T(8,128)(2,1)}, bf16[400,384]{1,0:T(8,128)(2,1)S(1)}, u32[]{:S(2)}, u32[]{:S(2)}) collective-permute-start(bf16[400,384]{1,0:T(8,128)(2,1)} %shard_map.161), channel_id=1, source_target_pairs={{0,16},{8,24},{16,0},{24,8},{1,17},{9,25},{17,1},{25,9},{2,18},{10... | collective-permute-start | bytes 921608 | tf_op jit(solution)/shard_map/ppermute | solution.py:35
  5.7 15.4 %collective-permute-start.4 = (bf16[400,384]{1,0:T(8,128)(2,1)}, bf16[400,384]{1,0:T(8,128)(2,1)S(1)}, u32[]{:S(2)}, u32[]{:S(2)}) collective-permute-start(bf16[400,384]{1,0:T(8,128)(2,1)} %shard_map.161), channel_id=1, source_target_pairs={{0,24},{8,0},{16,8},{24,16},{1,25},{9,1},{17,9},{25,17},{2,26},{10... | collective-permute-start | bytes 921608 | tf_op jit(solution)/shard_map/ppermute | solution.py:35
  21.1 1.3 copy-start.6
  22.3 12.7 %copy-start.7 = (bf16[256,384]{1,0:T(8,128)(2,1)S(1)}, bf16[256,384]{1,0:T(8,128)(2,1)}, u32[]{:S(2)}) copy-start(bf16[256,384]{1,0:T(8,128)(2,1)} %param.13) | copy-start | bytes 589828
  22.3 12.7 %copy-start.8 = (bf16[256,384]{1,0:T(8,128)(2,1)S(1)}, bf16[256,384]{1,0:T(8,128)(2,1)}, u32[]{:S(2)}) copy-start(bf16[256,384]{1,0:T(8,128)(2,1)} %param.12) | copy-start | bytes 589828
  22.3 35.9 %copy-start.5 = (s32[32]{0:T(128)S(1)}, s32[32]{0:T(128)}, u32[]{:S(2)}) copy-start(s32[32]{0:T(128)} %group_ref.17) | copy-start | bytes 388
  22.4 46.9 %collective-permute-start.10 = (bf16[4,400,384]{2,1,0:T(8,128)(2,1)S(1)}, bf16[4,400,384]{2,1,0:T(8,128)(2,1)S(1)}, u32[]{:S(2)}, u32[]{:S(2)}) collective-permute-start(bf16[4,400,384]{2,1,0:T(8,128)(2,1)S(1)} %pad_maximum_fusion.q_ref.qa_ref), channel_id=1, source_target_pairs={{0,4},{4,0},{1,5},{5,1},{2,6},{6,2},{3,7},{7,3},{8,12},{12,8},{9,1... | collective-permute-start | bytes 3686408 | tf_op jit(solution)/shard_map/ppermute | solution.py:35
  22.5 7.3 %collective-permute-start = (bf16[256,384]{1,0:T(8,128)(2,1)S(1)}, bf16[256,384]{1,0:T(8,128)(2,1)S(1)}, u32[]{:S(2)}, u32[]{:S(2)}) collective-permute-start(bf16[256,384]{1,0:T(8,128)(2,1)S(1)} %copy-done.6), channel_id=1, source_target_pairs={{0,24},{8,0},{16,8},{24,16},{1,25},{9,1},{17,9},{25,17},{2,26},{10... | collective-permute-start | bytes 589832 | tf_op jit(solution)/shard_map/ppermute | solution.py:35
  23.4 7.8 %collective-permute-start.2 = (bf16[256,384]{1,0:T(8,128)(2,1)S(1)}, bf16[256,384]{1,0:T(8,128)(2,1)S(1)}, u32[]{:S(2)}, u32[]{:S(2)}) collective-permute-start(bf16[256,384]{1,0:T(8,128)(2,1)S(1)} %copy-done.6), channel_id=1, source_target_pairs={{0,8},{8,16},{16,24},{24,0},{1,9},{9,17},{17,25},{25,1},{2,10},{10... | collective-permute-start | bytes 589832 | tf_op jit(solution)/shard_map/ppermute | solution.py:35
  24.6 10.2 %collective-permute-start.1 = (bf16[256,384]{1,0:T(8,128)(2,1)S(1)}, bf16[256,384]{1,0:T(8,128)(2,1)S(1)}, u32[]{:S(2)}, u32[]{:S(2)}) collective-permute-start(bf16[256,384]{1,0:T(8,128)(2,1)S(1)} %copy-done.6), channel_id=1, source_target_pairs={{0,16},{8,24},{16,0},{24,8},{1,17},{9,25},{17,1},{25,9},{2,18},{10... | collective-permute-start | bytes 589832 | tf_op jit(solution)/shard_map/ppermute | solution.py:35
  34.9 52.3 %collective-permute-start.3 = (bf16[4,256,384]{2,1,0:T(8,128)(2,1)S(1)}, bf16[4,256,384]{2,1,0:T(8,128)(2,1)}, u32[]{:S(2)}, u32[]{:S(2)}) collective-permute-start(bf16[4,256,384]{2,1,0:T(8,128)(2,1)S(1)} %pad_maximum_fusion.1.g_a.ga_ref), channel_id=1, source_target_pairs={{0,4},{4,0},{1,5},{5,1},{2,6},{6,2},{3,7},{7,3},{8,12},{12,8},{9,1... | collective-permute-start | bytes 2359304 | tf_op jit(solution)/shard_map/ppermute | solution.py:35
  35.8 13.0 %collective-permute-start.9 = (bf16[2,256,384]{2,1,0:T(8,128)(2,1)}, bf16[2,256,384]{2,1,0:T(8,128)(2,1)}, u32[]{:S(2)}, u32[]{:S(2)}) collective-permute-start(bf16[2,256,384]{2,1,0:T(8,128)(2,1)} %pad_maximum_fusion.2.kv_0.kv_ref), channel_id=1, source_target_pairs={{0,32},{32,64},{64,96},{96,0},{1,33},{33,65},{65,97},{97,1},{2,34}... | collective-permute-start | bytes 1179656 | tf_op jit(solution)/shard_map/ppermute | solution.py:35
  37.3 20.9 %collective-permute-start.8 = (bf16[2,256,384]{2,1,0:T(8,128)(2,1)}, bf16[2,256,384]{2,1,0:T(8,128)(2,1)}, u32[]{:S(2)}, u32[]{:S(2)}) collective-permute-start(bf16[2,256,384]{2,1,0:T(8,128)(2,1)} %pad_maximum_fusion.2.kv_0.kv_ref), channel_id=1, source_target_pairs={{0,64},{32,96},{64,0},{96,32},{1,65},{33,97},{65,1},{97,33},{2,66}... | collective-permute-start | bytes 1179656 | tf_op jit(solution)/shard_map/ppermute | solution.py:35
  40.0 18.2 %collective-permute-start.7 = (bf16[2,256,384]{2,1,0:T(8,128)(2,1)}, bf16[2,256,384]{2,1,0:T(8,128)(2,1)}, u32[]{:S(2)}, u32[]{:S(2)}) collective-permute-start(bf16[2,256,384]{2,1,0:T(8,128)(2,1)} %pad_maximum_fusion.2.kv_0.kv_ref), channel_id=1, source_target_pairs={{0,96},{32,0},{64,32},{96,64},{1,97},{33,1},{65,33},{97,65},{2,98}... | collective-permute-start | bytes 1179656 | tf_op jit(solution)/shard_map/ppermute | solution.py:35
  70.3 27.1 %collective-permute-start.17 = (f32[136,384]{1,0:T(8,128)S(1)}, f32[136,384]{1,0:T(8,128)S(1)}, u32[]{:S(2)}, u32[]{:S(2)}) collective-permute-start(f32[136,384]{1,0:T(8,128)S(1)} %get-tuple-element.49.own), channel_id=1, source_target_pairs={{0,32},{32,64},{64,96},{96,0},{1,33},{33,65},{65,97},{97,1},{2,34}... | collective-permute-start | bytes 626696 | tf_op jit(solution)/shard_map/ppermute | solution.py:35
  73.4 24.0 %collective-permute-start.16 = (f32[136,384]{1,0:T(8,128)S(1)}, f32[136,384]{1,0:T(8,128)S(1)}, u32[]{:S(2)}, u32[]{:S(2)}) collective-permute-start(f32[136,384]{1,0:T(8,128)S(1)} %get-tuple-element.49.own), channel_id=1, source_target_pairs={{0,64},{32,96},{64,0},{96,32},{1,65},{33,97},{65,1},{97,33},{2,66}... | collective-permute-start | bytes 626696 | tf_op jit(solution)/shard_map/ppermute | solution.py:35
  73.4 24.0 %collective-permute-start.15 = (f32[136,384]{1,0:T(8,128)S(1)}, f32[136,384]{1,0:T(8,128)S(1)}, u32[]{:S(2)}, u32[]{:S(2)}) collective-permute-start(f32[136,384]{1,0:T(8,128)S(1)} %get-tuple-element.49.own), channel_id=1, source_target_pairs={{0,96},{32,0},{64,32},{96,64},{1,97},{33,1},{65,33},{97,65},{2,98}... | collective-permute-start | bytes 626696 | tf_op jit(solution)/shard_map/ppermute | solution.py:35
  87.2 10.3 %copy-start = (bf16[256,384]{1,0:T(8,128)(2,1)S(1)}, bf16[256,384]{1,0:T(8,128)(2,1)}, u32[]{:S(2)}) copy-start(bf16[256,384]{1,0:T(8,128)(2,1)} %k_ref.5) | copy-start | bytes 589828
  87.2 10.3 %copy-start.1 = (bf16[256,384]{1,0:T(8,128)(2,1)S(1)}, bf16[256,384]{1,0:T(8,128)(2,1)}, u32[]{:S(2)}) copy-start(bf16[256,384]{1,0:T(8,128)(2,1)} %v_ref.5) | copy-start | bytes 589828
  87.2 10.2 %copy-start.2 = (bf16[256,384]{1,0:T(8,128)(2,1)S(1)}, bf16[256,384]{1,0:T(8,128)(2,1)}, u32[]{:S(2)}) copy-start(bf16[256,384]{1,0:T(8,128)(2,1)} %q_ref.5) | copy-start | bytes 589828
  87.2 10.2 %copy-start.3 = (bf16[256,384]{1,0:T(8,128)(2,1)S(1)}, bf16[256,384]{1,0:T(8,128)(2,1)}, u32[]{:S(2)}) copy-start(bf16[256,384]{1,0:T(8,128)(2,1)} %g_ref.3) | copy-start | bytes 589828
  87.3 10.2 %copy-start.4 = (f32[256,3]{0,1:T(4,128)S(1)}, f32[256,3]{0,1:T(4,128)}, u32[]{:S(2)}) copy-start(f32[256,3]{0,1:T(4,128)} %param.18) | copy-start | bytes 9220
  90.2 1.3 collective-permute-start.11
  91.6 20.1 %collective-permute-start.14 = (f32[2,4,8,256]{3,2,1,0:T(8,128)S(1)}, f32[2,4,8,256]{3,2,1,0:T(8,128)S(1)}, u32[]{:S(2)}, u32[]{:S(2)}) collective-permute-start(f32[2,4,8,256]{3,2,1,0:T(8,128)S(1)} %shard_map.165.chip_ref), channel_id=1, source_target_pairs={{0,8},{8,16},{16,24},{24,0},{1,9},{9,17},{17,25},{25,1},{2,10},{10... | collective-permute-start | bytes 196616 | tf_op jit(solution)/shard_map/ppermute | solution.py:35
  92.4 19.2 %collective-permute-start.13 = (f32[2,4,8,256]{3,2,1,0:T(8,128)S(1)}, f32[2,4,8,256]{3,2,1,0:T(8,128)S(1)}, u32[]{:S(2)}, u32[]{:S(2)}) collective-permute-start(f32[2,4,8,256]{3,2,1,0:T(8,128)S(1)} %shard_map.165.chip_ref), channel_id=1, source_target_pairs={{0,16},{8,24},{16,0},{24,8},{1,17},{9,25},{17,1},{25,9},{2,18},{10... | collective-permute-start | bytes 196616 | tf_op jit(solution)/shard_map/ppermute | solution.py:35
  97.4 14.2 %collective-permute-start.12 = (f32[2,4,8,256]{3,2,1,0:T(8,128)S(1)}, f32[2,4,8,256]{3,2,1,0:T(8,128)S(1)}, u32[]{:S(2)}, u32[]{:S(2)}) collective-permute-start(f32[2,4,8,256]{3,2,1,0:T(8,128)S(1)} %shard_map.165.chip_ref), channel_id=1, source_target_pairs={{0,24},{8,0},{16,8},{24,16},{1,25},{9,1},{17,9},{25,17},{2,26},{10... | collective-permute-start | bytes 196616 | tf_op jit(solution)/shard_map/ppermute | solution.py:35
  99.7 5.7 %collective-permute-start.20 = (f32[8,256]{1,0:T(8,128)S(1)}, f32[8,256]{1,0:T(8,128)S(1)}, u32[]{:S(2)}, u32[]{:S(2)}) collective-permute-start(f32[8,256]{1,0:T(8,128)S(1)} %get-tuple-element.52.sum_0), channel_id=1, source_target_pairs={{0,1},{1,2},{2,3},{3,0},{4,5},{5,6},{6,7},{7,4},{8,9},{9,10},{10,1... | collective-permute-start | bytes 24584 | tf_op jit(solution)/shard_map/ppermute | solution.py:35
  101.7 5.8 %collective-permute-start.19 = (f32[8,256]{1,0:T(8,128)S(1)}, f32[8,256]{1,0:T(8,128)S(1)}, u32[]{:S(2)}, u32[]{:S(2)}) collective-permute-start(f32[8,256]{1,0:T(8,128)S(1)} %get-tuple-element.52.sum_0), channel_id=1, source_target_pairs={{0,2},{1,3},{2,0},{3,1},{4,6},{5,7},{6,4},{7,5},{8,10},{9,11},{10,... | collective-permute-start | bytes 24584 | tf_op jit(solution)/shard_map/ppermute | solution.py:35
  105.4 3.7 %collective-permute-start.18 = (f32[8,256]{1,0:T(8,128)S(1)}, f32[8,256]{1,0:T(8,128)S(1)}, u32[]{:S(2)}, u32[]{:S(2)}) collective-permute-start(f32[8,256]{1,0:T(8,128)S(1)} %get-tuple-element.52.sum_0), channel_id=1, source_target_pairs={{0,3},{1,0},{2,1},{3,2},{4,7},{5,4},{6,5},{7,6},{8,11},{9,8},{10,9... | collective-permute-start | bytes 24584 | tf_op jit(solution)/shard_map/ppermute | solution.py:35
  146.3 10.0 %collective-permute-start.25 = (bf16[4,256,384]{2,1,0:T(8,128)(2,1)S(1)}, bf16[4,256,384]{2,1,0:T(8,128)(2,1)S(1)}, u32[]{:S(2)}, u32[]{:S(2)}) collective-permute-start(bf16[4,256,384]{2,1,0:T(8,128)(2,1)S(1)} %get-tuple-element.67), channel_id=1, source_target_pairs={{0,4},{4,0},{1,5},{5,1},{2,6},{6,2},{3,7},{7,3},{8,12},{12,8},{9,1... | collective-permute-start | bytes 2359304 | tf_op jit(solution)/shard_map/ppermute | solution.py:35
  146.4 29.5 %collective-permute-start.21 = (bf16[1152,384]{1,0:T(8,128)(2,1)S(1)}, bf16[1152,384]{1,0:T(8,128)(2,1)S(1)}, u32[]{:S(2)}, u32[]{:S(2)}) collective-permute-start(bf16[1152,384]{1,0:T(8,128)(2,1)S(1)} %get-tuple-element.55), channel_id=1, source_target_pairs={{0,4},{4,0},{1,5},{5,1},{2,6},{6,2},{3,7},{7,3},{8,12},{12,8},{9,1... | collective-permute-start | bytes 2654216 | tf_op jit(solution)/shard_map/ppermute | solution.py:35
  147.0 20.8 %collective-permute-start.29 = (bf16[2,256,384]{2,1,0:T(8,128)(2,1)S(1)}, bf16[2,256,384]{2,1,0:T(8,128)(2,1)S(1)}, u32[]{:S(2)}, u32[]{:S(2)}) collective-permute-start(bf16[2,256,384]{2,1,0:T(8,128)(2,1)S(1)} %get-tuple-element.82), channel_id=1, source_target_pairs={{0,32},{32,64},{64,96},{96,0},{1,33},{33,65},{65,97},{97,1},{2,34}... | collective-permute-start | bytes 1179656 | tf_op jit(solution)/shard_map/ppermute | solution.py:35
  153.5 17.1 %collective-permute-start.31 = (bf16[2,256,384]{2,1,0:T(8,128)(2,1)S(1)}, bf16[2,256,384]{2,1,0:T(8,128)(2,1)S(1)}, u32[]{:S(2)}, u32[]{:S(2)}) collective-permute-start(bf16[2,256,384]{2,1,0:T(8,128)(2,1)S(1)} %get-tuple-element.83), channel_id=1, source_target_pairs={{0,64},{32,96},{64,0},{96,32},{1,65},{33,97},{65,1},{97,33},{2,66}... | collective-permute-start | bytes 1179656 | tf_op jit(solution)/shard_map/ppermute | solution.py:35
  153.5 17.9 %collective-permute-start.30 = (bf16[2,256,384]{2,1,0:T(8,128)(2,1)S(1)}, bf16[2,256,384]{2,1,0:T(8,128)(2,1)S(1)}, u32[]{:S(2)}, u32[]{:S(2)}) collective-permute-start(bf16[2,256,384]{2,1,0:T(8,128)(2,1)S(1)} %get-tuple-element.84), channel_id=1, source_target_pairs={{0,96},{32,0},{64,32},{96,64},{1,97},{33,1},{65,33},{97,65},{2,98}... | collective-permute-start | bytes 1179656 | tf_op jit(solution)/shard_map/ppermute | solution.py:35
  156.6 21.6 %collective-permute-start.26 = (bf16[256,384]{1,0:T(8,128)(2,1)S(1)}, bf16[256,384]{1,0:T(8,128)(2,1)S(1)}, u32[]{:S(2)}, u32[]{:S(2)}) collective-permute-start(bf16[256,384]{1,0:T(8,128)(2,1)S(1)} %get-tuple-element.85), channel_id=1, source_target_pairs={{0,8},{8,16},{16,24},{24,0},{1,9},{9,17},{17,25},{25,1},{2,10},{10... | collective-permute-start | bytes 589832 | tf_op jit(solution)/shard_map/ppermute | solution.py:35
  171.6 9.4 %collective-permute-start.28 = (bf16[256,384]{1,0:T(8,128)(2,1)S(1)}, bf16[256,384]{1,0:T(8,128)(2,1)S(1)}, u32[]{:S(2)}, u32[]{:S(2)}) collective-permute-start(bf16[256,384]{1,0:T(8,128)(2,1)S(1)} %get-tuple-element.86), channel_id=1, source_target_pairs={{0,16},{8,24},{16,0},{24,8},{1,17},{9,25},{17,1},{25,9},{2,18},{10... | collective-permute-start | bytes 589832 | tf_op jit(solution)/shard_map/ppermute | solution.py:35
  172.7 11.2 %collective-permute-start.27 = (bf16[256,384]{1,0:T(8,128)(2,1)S(1)}, bf16[256,384]{1,0:T(8,128)(2,1)S(1)}, u32[]{:S(2)}, u32[]{:S(2)}) collective-permute-start(bf16[256,384]{1,0:T(8,128)(2,1)S(1)} %get-tuple-element.87), channel_id=1, source_target_pairs={{0,24},{8,0},{16,8},{24,16},{1,25},{9,1},{17,9},{25,17},{2,26},{10... | collective-permute-start | bytes 589832 | tf_op jit(solution)/shard_map/ppermute | solution.py:35
  176.1 14.0 %collective-permute-start.22 = (bf16[512,384]{1,0:T(8,128)(2,1)S(1)}, bf16[512,384]{1,0:T(8,128)(2,1)S(1)}, u32[]{:S(2)}, u32[]{:S(2)}) collective-permute-start(bf16[512,384]{1,0:T(8,128)(2,1)S(1)} %get-tuple-element.57), channel_id=1, source_target_pairs={{0,8},{8,16},{16,24},{24,0},{1,9},{9,17},{17,25},{25,1},{2,10},{10... | collective-permute-start | bytes 1179656 | tf_op jit(solution)/shard_map/ppermute | solution.py:35
  176.2 15.7 %collective-permute-start.23 = (bf16[512,384]{1,0:T(8,128)(2,1)S(1)}, bf16[512,384]{1,0:T(8,128)(2,1)S(1)}, u32[]{:S(2)}, u32[]{:S(2)}) collective-permute-start(bf16[512,384]{1,0:T(8,128)(2,1)S(1)} %get-tuple-element.58), channel_id=1, source_target_pairs={{0,24},{8,0},{16,8},{24,16},{1,25},{9,1},{17,9},{25,17},{2,26},{10... | collective-permute-start | bytes 1179656 | tf_op jit(solution)/shard_map/ppermute | solution.py:35
  178.2 22.5 %collective-permute-start.24 = (bf16[512,384]{1,0:T(8,128)(2,1)S(1)}, bf16[512,384]{1,0:T(8,128)(2,1)S(1)}, u32[]{:S(2)}, u32[]{:S(2)}) collective-permute-start(bf16[512,384]{1,0:T(8,128)(2,1)S(1)} %get-tuple-element.59), channel_id=1, source_target_pairs={{0,16},{8,24},{16,0},{24,8},{1,17},{9,25},{17,1},{25,9},{2,18},{10... | collective-permute-start | bytes 1179656 | tf_op jit(solution)/shard_map/ppermute | solution.py:35
  201.6 8.2 %collective-permute-start.34 = (f32[128,384]{1,0:T(8,128)S(1)}, f32[128,384]{1,0:T(8,128)S(1)}, u32[]{:S(2)}, u32[]{:S(2)}) collective-permute-start(f32[128,384]{1,0:T(8,128)S(1)} %get-tuple-element.75.own), channel_id=1, source_target_pairs={{0,32},{32,64},{64,96},{96,0},{1,33},{33,65},{65,97},{97,1},{2,34}... | collective-permute-start | bytes 589832 | tf_op jit(solution)/shard_map/ppermute | solution.py:35
  204.6 9.9 %collective-permute-start.33 = (f32[128,384]{1,0:T(8,128)S(1)}, f32[128,384]{1,0:T(8,128)S(1)}, u32[]{:S(2)}, u32[]{:S(2)}) collective-permute-start(f32[128,384]{1,0:T(8,128)S(1)} %get-tuple-element.75.own), channel_id=1, source_target_pairs={{0,64},{32,96},{64,0},{96,32},{1,65},{33,97},{65,1},{97,33},{2,66}... | collective-permute-start | bytes 589832 | tf_op jit(solution)/shard_map/ppermute | solution.py:35
  206.3 8.2 %collective-permute-start.32 = (f32[128,384]{1,0:T(8,128)S(1)}, f32[128,384]{1,0:T(8,128)S(1)}, u32[]{:S(2)}, u32[]{:S(2)}) collective-permute-start(f32[128,384]{1,0:T(8,128)S(1)} %get-tuple-element.75.own), channel_id=1, source_target_pairs={{0,96},{32,0},{64,32},{96,64},{1,97},{33,1},{65,33},{97,65},{2,98}... | collective-permute-start | bytes 589832 | tf_op jit(solution)/shard_map/ppermute | solution.py:35
where the time goes:
time: 217 us
  waiting for transfers between devices  78.6 us (36%)
  Pallas kernels  71.2 us (33%)
  starting transfers between devices  60.6 us (28%)
  other arithmetic  4.03 us (2%)
    ppermute x35, waiting for transfers between devices, send(): lax.ppermute(block, axis, [(i, (i + offset) % size) for i in range(size)])  78.6 us
    pallas_call x15, Pallas kernels, call(): pl.pallas_call(kernel, out_shape=out_shape, cost_estimate=pl.CostEstimate...  71.2 us
    ppermute x35, starting transfers between devices, send(): lax.ppermute(block, axis, [(i, (i + offset) % size) for i in range(size)])  60.6 us
  transfers between devices with their start and end apart: 35, of which 21 were waited for; matrix products, arithmetic and copies ran while one was open for 2% of the time, Pallas kernels for 14%

commit v1 on v0

--- a/solution.py
+++ b/solution.py
@@ -85,13 +85,22 @@
     return jnp.where(condition, 1, 0)
 
 
-def key_scores(k, q, limit=None):
-    s = dot(k, q, 1, 1) * (SCALE * LOG2E)
-    if limit is not None:
-        key_row = lax.broadcasted_iota(jnp.int32, s.shape, 0)
-        query_col = lax.broadcasted_iota(jnp.int32, s.shape, 1)
-        s = jnp.where(key_row - query_col <= limit, s, NEG)
-    return s
+def causal(scores):
+    row = lax.broadcasted_iota(jnp.int32, scores.shape, 0)
+    col = lax.broadcasted_iota(jnp.int32, scores.shape, 1)
+    return jnp.where(row <= col, scores, NEG)
+
+
+def hidden(key_pos, query_pos):
+    return jnp.where(key_pos > query_pos, -NEG, 0.0)
+
+
+def staged(items, first, second):
+    current = first(items[0])
+    for i, item in enumerate(items):
+        following = first(items[i + 1]) if i + 1 < len(items) else None
+        second(item, current)
+        current = following
 
 
 def forward_kernel(
@@ -99,47 +108,37 @@
 ):
     h = pl.program_id(0)
     for o, kv_ref in enumerate((kv_0, kv_1, kv_2, kv_3)):
-        k_ref[o] = kv_ref[0]
-        vt_ref[o] = kv_ref[1].T
-    key_pos = [position(group_ref, index_ref, o, 0, 0) for o in range(NX)]
-    first = (4 - (key_pos[0] >> 3)) & 3
+        k_ref[pl.ds(o * TOK, TOK)] = kv_ref[0]
+        vt_ref[pl.ds(0, HEAD_DIM), pl.ds(o * TOK, TOK)] = kv_ref[1].T
 
     @pl.when(h == 0)
     def _():
         stat_ref[...] = jnp.zeros_like(stat_ref)
-
-    @pl.loop(0, NY)
-    def _(i):
+        vt_ref[pl.ds(HEAD_DIM, 16)] = jnp.ones((16, NX * TOK), BF16)
+
+    key_pos = [position(group_ref, index_ref, o, 0, 0) for o in range(NX)]
+
+    def scores(i):
+        return [dot(k_ref[pl.ds(o * TOK, TOK)], q_ref[i], 1, 1) for o in range(NX)]
+
+    def finish(i, parts):
         query_pos = position(group_ref, index_ref, 0, side, i)
-        count = sum(flag(p <= query_pos) for p in key_pos)
-        limit = jnp.where(key_pos[0] == query_pos, 0, TOK)
-
-        @pl.when(count == 0)
-        def _():
-            out_ref[i] = jnp.zeros((TOK, HEAD_DIM), BF16)
-            stat_ref[i, pl.ds(h, 1)] = jnp.full((1, TOK), NEG, F32)
-
-        for n in range(1, NX + 1):
-
-            @pl.when(count == n)
-            def _():
-                q = q_ref[i]
-                slots = [(first + m) & 3 for m in range(n)]
-                parts = [
-                    key_scores(k_ref[o], q, limit if m == n - 1 else None)
-                    for m, o in enumerate(slots)
-                ]
-                top = jnp.max(parts[0], axis=0, keepdims=True)
-                for s in parts[1:]:
-                    top = jnp.maximum(top, jnp.max(s, axis=0, keepdims=True))
-                total = jnp.zeros((1, TOK), F32)
-                acc = jnp.zeros((HEAD_DIM, TOK), F32)
-                for m, o in enumerate(slots):
-                    p = jnp.exp2(parts[m] - top)
-                    total = total + jnp.sum(p, axis=0, keepdims=True)
-                    acc = acc + dot(vt_ref[o], p.astype(BF16), 1, 0)
-                out_ref[i] = (acc / total).T.astype(BF16)
-                stat_ref[i, pl.ds(h, 1)] = top + jnp.log(total) * LOG2E
+        if side == 0 and i == 0:
+            parts = [causal(parts[0]), *parts[1:]]
+        hide = [hidden(p, query_pos) for p in key_pos]
+        tops = [jnp.max(s, axis=0, keepdims=True) - x for s, x in zip(parts, hide)]
+        top = functools.reduce(jnp.maximum, tops)
+        probs = [
+            jnp.exp2((s - (top + x)) * (SCALE * LOG2E)).astype(BF16) for s, x in zip(parts, hide)
+        ]
+        acc = dot(vt_ref[...], jnp.concatenate(probs), 1, 0)
+        total = acc[HEAD_DIM : HEAD_DIM + 1]
+        seen = top > 0.5 * NEG
+        out_ref[i] = jnp.where(seen, acc[:HEAD_DIM] * (1.0 / total), 0.0).T.astype(BF16)
+        log = top * (SCALE * LOG2E) + jnp.log(total) * LOG2E
+        stat_ref[i, pl.ds(h, 1)] = jnp.where(seen, log, NEG)
+
+    staged(range(NY), scores, finish)
 
 
 def rows_spec(first=0):
@@ -159,7 +158,10 @@
         **placed(
             [rows_spec()] + [pair_spec()] * NX,
             [rows_spec(), pl.BlockSpec((NY, 8, TOK), lambda h, *_: (0, 0, 0))],
-            [pltpu.VMEM((NX, TOK, HEAD_DIM), BF16), pltpu.VMEM((NX, HEAD_DIM, TOK), BF16)],
+            [
+                pltpu.VMEM((NX * TOK, HEAD_DIM), BF16),
+                pltpu.VMEM((HEAD_DIM + 16, NX * TOK), BF16),
+            ],
             (HEADS,),
         ),
     )
@@ -179,55 +181,48 @@
             part_ref[side, i, pl.ds(h + 4, 1)] = jnp.sum(product.T, axis=0, keepdims=True)
 
 
-def tile_backward(k, v, kt, q, g, lse, delta, limit=None):
-    p = jnp.exp2(key_scores(k, q, limit) - lse)
-    ds = (p * (dot(v, g, 1, 1) - delta)).astype(BF16)
-    return dot(ds, q, 1, 0), dot(p.astype(BF16), g, 1, 0), dot(kt, ds, 1, 0)
-
-
 def far_kernel(
     first_head, group_ref, index_ref, qa_ref, qb_ref, ga_ref, gb_ref, kv_1, kv_2, kv_3, stat_ref,
     *refs,
 ):
     dqa_ref, dqb_ref, dkv_ref, k_ref, v_ref, kt_ref, acc_ref = refs[-7:]
     h = pl.program_id(0) + first_head
-    for o, kv_ref in enumerate((kv_1, kv_2, kv_3)):
-        k_ref[o] = kv_ref[0]
-        v_ref[o] = kv_ref[1]
-        kt_ref[o] = kv_ref[0].T
+    tiles = [pl.ds(o * TOK, TOK) for o in range(NX - 1)]
+    for tile, kv_ref in zip(tiles, (kv_1, kv_2, kv_3)):
+        k_ref[tile] = kv_ref[0]
+        v_ref[tile] = kv_ref[1]
+        kt_ref[:, tile] = kv_ref[0].T
+    key_pos = [position(group_ref, index_ref, o, 0, 0) for o in range(1, NX)]
     acc_ref[...] = jnp.zeros_like(acc_ref)
-    key_pos = [position(group_ref, index_ref, o, 0, 0) for o in range(NX)]
-    first, own_rank = (4 - (key_pos[0] >> 3)) & 3, key_pos[0] >> 3
-
-    def one_block(q_ref, g_ref, dq_ref, side, b):
+
+    def products(item):
+        q_ref, g_ref, _, _, b = item
+        return (
+            [dot(k_ref[t], q_ref[b], 1, 1) for t in tiles],
+            [dot(v_ref[t], g_ref[b], 1, 1) for t in tiles],
+        )
+
+    def finish(item, found):
+        q_ref, g_ref, dq_ref, side, b = item
         query_pos = position(group_ref, index_ref, 0, side, b)
-        count = sum(flag(p <= query_pos) for p in key_pos[1:])
-
-        @pl.when(count == 0)
-        def _():
-            dq_ref[b] = jnp.zeros((TOK, HEAD_DIM), F32)
-
-        for n in range(1, NX):
-
-            @pl.when(count == n)
-            def _():
-                q, g = q_ref[b], g_ref[b]
-                lse = stat_ref[side, b, pl.ds(h, 1)]
-                delta = stat_ref[side, b, pl.ds(h + 4, 1)]
-                dqt = jnp.zeros((HEAD_DIM, TOK), F32)
-                for m in range(n):
-                    o = ((first + m + flag(own_rank <= m)) & 3) - 1
-                    dk, dv, dq = tile_backward(k_ref[o], v_ref[o], kt_ref[o], q, g, lse, delta)
-                    acc_ref[o, 0] += dk
-                    acc_ref[o, 1] += dv
-                    dqt = dqt + dq
-                dq_ref[b] = dqt.T
-
-    pl.loop(0, NY)(lambda b: one_block(qa_ref, ga_ref, dqa_ref, 0, b))
-    pl.loop(0, NY)(lambda b: one_block(qb_ref, gb_ref, dqb_ref, 1, b))
-    for o in range(NX - 1):
-        dkv_ref[o, 0] = (acc_ref[o, 0] * SCALE).astype(BF16)
-        dkv_ref[o, 1] = acc_ref[o, 1].astype(BF16)
+        lse = stat_ref[side, b, pl.ds(h, 1)]
+        delta = stat_ref[side, b, pl.ds(h + 4, 1)]
+        probs, grads = [], []
+        for x, s, dprobs in zip(key_pos, *found):
+            p = jnp.exp2(s * (SCALE * LOG2E) - (lse + hidden(x, query_pos)))
+            probs.append(p.astype(BF16))
+            grads.append((p * (dprobs - delta)).astype(BF16))
+        probs, grads = jnp.concatenate(probs), jnp.concatenate(grads)
+        acc_ref[0] += dot(grads, q_ref[b], 1, 0)
+        acc_ref[1] += dot(probs, g_ref[b], 1, 0)
+        dq_ref[b, 0] = dot(kt_ref[...], grads, 1, 0)
+
+    items = [(qa_ref, ga_ref, dqa_ref, 0, b) for b in range(NY)]
+    items += [(qb_ref, gb_ref, dqb_ref, 1, b) for b in range(NY)]
+    staged(items, products, finish)
+    for o, tile in enumerate(tiles):
+        dkv_ref[o, 0] = (acc_ref[0, tile] * SCALE).astype(BF16)
+        dkv_ref[o, 1] = acc_ref[1, tile].astype(BF16)
 
 
 STAT_SPEC = pl.BlockSpec((2, NY, 8, TOK), lambda h, *_: (0, 0, 0, 0))
@@ -235,24 +230,26 @@
 
 def far_backward(place, first, heads, qa, qb, ga, gb, kvs, stats, earlier=()):
     rows, pair = rows_spec(first), pair_spec(first)
+    turned = pl.BlockSpec((NY, 1, HEAD_DIM, TOK), lambda h, *_: (0, h + first, 0, 0))
+    dq_shape = shaped(NY, HEADS, HEAD_DIM, TOK)
     kwargs = placed(
         [rows] * 4 + [pair] * (NX - 1) + [STAT_SPEC] + [ANY] * len(earlier),
         [
-            rows,
-            rows,
+            turned,
+            turned,
             pl.BlockSpec((NX - 1, 2, TOK, HEAD_DIM), lambda h, *_: (0, 0, 0, h + first)),
         ],
         [
-            pltpu.VMEM((NX - 1, TOK, HEAD_DIM), BF16),
-            pltpu.VMEM((NX - 1, TOK, HEAD_DIM), BF16),
-            pltpu.VMEM((NX - 1, HEAD_DIM, TOK), BF16),
-            pltpu.VMEM((NX - 1, 2, TOK, HEAD_DIM), F32),
+            pltpu.VMEM(((NX - 1) * TOK, HEAD_DIM), BF16),
+            pltpu.VMEM(((NX - 1) * TOK, HEAD_DIM), BF16),
+            pltpu.VMEM((HEAD_DIM, (NX - 1) * TOK), BF16),
+            pltpu.VMEM((2, (NX - 1) * TOK, HEAD_DIM), F32),
         ],
         (heads,),
     )
     return call(
         functools.partial(far_kernel, first),
-        [shaped(NY, TOK, WIDTH), shaped(NY, TOK, WIDTH), shaped(NX - 1, 2, TOK, WIDTH, dtype=BF16)],
+        [dq_shape, dq_shape, shaped(NX - 1, 2, TOK, WIDTH, dtype=BF16)],
         2 * NY * (NX - 1) * heads * 10 * TOK * TOK * HEAD_DIM,
         (*place, qa, qb, ga, gb, *kvs, stats, *earlier),
         input_output_aliases={10 + i: i for i in range(len(earlier))},
@@ -266,37 +263,37 @@
 ):
     h = pl.program_id(0)
     kt_ref[...] = kv_ref[0].T
-    dkv_ref[...] = jnp.zeros_like(dkv_ref)
     own = position(group_ref, index_ref, 0, 0, 0)
+
+    def products(item):
+        q_ref, g_ref, b = item[0], item[1], item[-1]
+        return dot(kv_ref[0], q_ref[b], 1, 1), dot(kv_ref[1], g_ref[b], 1, 1)
+
+    def finish(item, found):
+        q_ref, g_ref, dq_in, dq_ref, side, b = item
+        s, dprobs = found
+        lse = stat_ref[side, b, pl.ds(h, 1)]
+        delta = stat_ref[side, b, pl.ds(h + 4, 1)]
+        s = s * (SCALE * LOG2E)
+        start = side == 0 and b == 0
+        if start:
+            s = causal(s)
+        p = jnp.exp2(s - (lse + hidden(own, position(group_ref, index_ref, 0, side, b))))
+        ds = (p * (dprobs - delta)).astype(BF16)
+        dq_sum = dq_in[b, 0] + dot(kt_ref[...], ds, 1, 0)
+        dq_ref[b] = (dq_sum * SCALE).T.astype(BF16)
+        dk, dv = dot(ds, q_ref[b], 1, 0) * SCALE, dot(p.astype(BF16), g_ref[b], 1, 0)
+        dkv_ref[0] = dk if start else dkv_ref[0] + dk
+        dkv_ref[1] = dv if start else dkv_ref[1] + dv
+
     sides = ((qa_ref, ga_ref, dqa_in, dqa_ref), (qb_ref, gb_ref, dqb_in, dqb_ref))
-    for side, (q_ref, g_ref, dq_in, dq_ref) in enumerate(sides):
-        where = [position(group_ref, index_ref, 0, side, b) for b in range(NY)]
-        count = sum(flag(p >= own) for p in where)
-
-        @pl.when(count == 0)
-        def _():
-            for b in range(NY):
-                dq_ref[b] = (dq_in[b] * SCALE).astype(BF16)
-
-        @pl.when(count > 0)
-        def _():
-            dk_sum = jnp.zeros((TOK, HEAD_DIM), F32)
-            dv_sum = jnp.zeros((TOK, HEAD_DIM), F32)
-            for b in range(NY):
-                limit = jnp.where(where[b] == own, 0, jnp.where(where[b] > own, TOK, -TOK))
-                dk, dv, dq = tile_backward(
-                    kv_ref[0], kv_ref[1], kt_ref[...], q_ref[b], g_ref[b],
-                    stat_ref[side, b, pl.ds(h, 1)], stat_ref[side, b, pl.ds(h + 4, 1)], limit,
-                )
-                dk_sum = dk_sum + dk
-                dv_sum = dv_sum + dv
-                dq_ref[b] = ((dq_in[b] + dq.T) * SCALE).astype(BF16)
-            dkv_ref[0] += dk_sum * SCALE
-            dkv_ref[1] += dv_sum
+    items = [(*refs, side, b) for side, refs in enumerate(sides) for b in range(NY)]
+    staged(items, products, finish)
 
 
 def near_backward(place, qa, qb, ga, gb, kv, stats, dqa, dqb):
     rows, pair = rows_spec(), pair_spec()
+    turned = pl.BlockSpec((NY, 1, HEAD_DIM, TOK), lambda h, *_: (0, h, 0, 0))
     return call(
         near_kernel,
         [
@@ -307,7 +304,7 @@
         2 * NY * HEADS * 10 * TOK * TOK * HEAD_DIM,
         (*place, qa, qb, ga, gb, kv, stats, dqa, dqb),
         **placed(
-            [rows] * 4 + [pair, STAT_SPEC, rows, rows],
+            [rows] * 4 + [pair, STAT_SPEC, turned, turned],
             [rows, rows, pair],
             [pltpu.VMEM((HEAD_DIM, TOK), BF16)],
             (HEADS,),
@@ -369,11 +366,11 @@
     return dot(triangle(False).astype(F32), decay_ref[...], 1, 1, HIGHEST)
 
 
-def pack_kernel(q_ref, key_ref, value_ref, decay_ref, out_ref):
+def pack_kernel(g_ref, key_ref, value_ref, decay_ref, out_ref):
     cumulative = decay_columns(decay_ref)
     total = cumulative[TOK - 1 : TOK]
     tail = jnp.exp(total - cumulative)
-    out_ref[pl.ds(0, TOK)] = q_ref[...]
+    out_ref[pl.ds(0, TOK)] = g_ref[...]
     row = lax.broadcasted_iota(jnp.int32, (16, HEAD_DIM), 0)
     for h in range(HEADS):
         keys = key_ref[:, head_cols(h)].astype(F32) * tail[:, h : h + 1]
@@ -443,9 +440,9 @@
     return result
 
 
-def states_kernel(group_ref, index_ref, qa_ref, qb_ref, handed_ref, entry_ref, log_ref):
+def states_kernel(group_ref, index_ref, ga_ref, gb_ref, handed_ref, entry_ref, log_ref):
     logs, states = [], []
-    for ref in (qa_ref, qb_ref):
+    for ref in (ga_ref, gb_ref):
         for i in range(NY):
             rows = ref[i, pl.ds(LOG_ROW, 16)].astype(F32)
             logs.append(rows[0:1] + rows[1:2] + rows[2:3])
@@ -582,11 +579,11 @@
         pack_kernel,
         shaped(PACK_ROWS, WIDTH, dtype=BF16),
         2**26,
-        (soft_query, lin_key, lin_value, decay),
+        (soft_grad, lin_key, lin_value, decay),
         vmem=60,
     )
-    q_from = {0: packed, **{o: fetch(packed, "y", NY, o) for o in OFFSETS}}
-    g_from = {0: soft_grad, **{o: fetch(soft_grad, "y", NY, o) for o in OFFSETS}}
+    q_from = {0: soft_query, **{o: fetch(soft_query, "y", NY, o) for o in OFFSETS}}
+    g_from = {0: packed, **{o: fetch(packed, "y", NY, o) for o in OFFSETS}}
     qa = jnp.stack([q_from[o] for o in range(NY)])
     qb = fetch(qa, "c", NC, 1)
     ga = jnp.stack([g_from[o] for o in range(NY)])
@@ -597,7 +594,7 @@
         states_kernel,
         [shaped(HEAD_DIM + 8, WIDTH), shaped(HEAD_DIM + 8, WIDTH), shaped(8, WIDTH)],
         2**24,
-        (*place, qa, qb),
+        (*place, ga, gb),
         **placed(in_vmem(2), in_vmem(3)),
     )
     totals = [handed, *(fetch(handed, "x", NX, o) for o in (1, 2, 3))]

time: 217 us -> 193 us (0.89)
  Pallas kernels: 71.2 us -> 52 us
  starting transfers between devices: 60.6 us -> 51.8 us
  waiting for transfers between devices: 78.6 us -> 82.4 us
    pallas_call x15, Pallas kernels: 71.2 us -> 52 us  [call(): pl.pallas_call(kernel, out_shape=out_shape, cost_estimate=pl.CostEstimate...]
    ppermute x35, starting transfers between devices: 60.6 us -> 51.8 us  [send(): lax.ppermute(block, axis, [(i, (i + offset) % size) for i in range(size)])]
    ppermute x35, waiting for transfers between devices: 78.6 us -> 82.4 us  [send(): lax.ppermute(block, axis, [(i, (i + offset) % size) for i in range(size)])]
  transfers between devices with their start and end apart: 35 -> 35, of which waited for: 21 -> 20; matrix products, arithmetic and copies ran while one was open for 2% -> 2% of each run, Pallas kernels for 14% -> 12%
where the time goes in v1:
time: 193 us; the launch traced here: 192 us
  waiting for transfers between devices  82.4 us (43%)
  Pallas kernels  52 us (27%)
  starting transfers between devices  51.8 us (27%)
  other arithmetic  4.06 us (2%)
    ppermute x35, waiting for transfers between devices, send(): lax.ppermute(block, axis, [(i, (i + offset) % size) for i in range(size)])  82.4 us
    pallas_call x15, Pallas kernels, call(): pl.pallas_call(kernel, out_shape=out_shape, cost_estimate=pl.CostEstimate...  52 us
    ppermute x35, starting transfers between devices, send(): lax.ppermute(block, axis, [(i, (i + offset) % size) for i in range(size)])  51.8 us
  transfers between devices with their start and end apart: 35, of which 20 were waited for; matrix products, arithmetic and copies ran while one was open for 2% of the time, Pallas kernels for 12%

profile of v1, /device:TPU:8, one launch (start us, length us, event | category | flops | bytes accessed | tf_op | source)
XLA Modules:
  0.0 192.2 jit_solution(11503695653583904536)
XLA Ops:
  0.6 2.7 %shard_map.161 = bf16[400,384]{1,0:T(8,128)(2,1)} custom-call(bf16[256,384]{1,0:T(8,128)(2,1)} %g_ref.3, bf16[256,384]{1,0:T(8,128)(2,1)} %k_ref.5, bf16[256,384]{1,0:T(8,128)(2,1)} %v_ref.5, f32[3,256]{1,0:T(4,128)} %bitcast.38), custom_call_target="tpu_custom_call" | custom-call | flops 67108864 | bytes 2097152 | tf_op jit(solution)/shard_map/pallas_call | solution.py:57
  3.3 1.6 collective-permute-start.2
  5.7 2.5 %collective-permute-start = (bf16[400,384]{1,0:T(8,128)(2,1)}, bf16[400,384]{1,0:T(8,128)(2,1)S(1)}, u32[]{:S(2)}, u32[]{:S(2)}) collective-permute-start(bf16[400,384]{1,0:T(8,128)(2,1)} %shard_map.161), channel_id=1, source_target_pairs={{0,24},{8,0},{16,8},{24,16},{1,25},{9,1},{17,9},{25,17},{2,26},{10... | collective-permute-start | bytes 921608 | tf_op jit(solution)/shard_map/ppermute | solution.py:35
  8.2 5.4 %collective-permute-done.2 = bf16[400,384]{1,0:T(8,128)(2,1)S(1)} collective-permute-done((bf16[400,384]{1,0:T(8,128)(2,1)}, bf16[400,384]{1,0:T(8,128)(2,1)S(1)}, u32[]{:S(2)}, u32[]{:S(2)}) %collective-permute-start.2) | collective-permute-done | bytes 307232 | tf_op jit(solution)/shard_map/ppermute | solution.py:35
  13.6 3.1 %collective-permute-done.1 = bf16[400,384]{1,0:T(8,128)(2,1)S(1)} collective-permute-done((bf16[400,384]{1,0:T(8,128)(2,1)}, bf16[400,384]{1,0:T(8,128)(2,1)S(1)}, u32[]{:S(2)}, u32[]{:S(2)}) %collective-permute-start.1) | collective-permute-done | bytes 307232 | tf_op jit(solution)/shard_map/ppermute | solution.py:35
  16.7 4.4 %collective-permute-done = bf16[400,384]{1,0:T(8,128)(2,1)S(1)} collective-permute-done((bf16[400,384]{1,0:T(8,128)(2,1)}, bf16[400,384]{1,0:T(8,128)(2,1)S(1)}, u32[]{:S(2)}, u32[]{:S(2)}) %collective-permute-start) | collective-permute-done | bytes 307232 | tf_op jit(solution)/shard_map/ppermute | solution.py:35
  24.6 3.0 %collective-permute-start.5 = (bf16[256,384]{1,0:T(8,128)(2,1)S(1)}, bf16[256,384]{1,0:T(8,128)(2,1)S(1)}, u32[]{:S(2)}, u32[]{:S(2)}) collective-permute-start(bf16[256,384]{1,0:T(8,128)(2,1)S(1)} %copy-done.6), channel_id=1, source_target_pairs={{0,16},{8,24},{16,0},{24,8},{1,17},{9,25},{17,1},{25,9},{2,18},{10... | collective-permute-start | bytes 589832 | tf_op jit(solution)/shard_map/ppermute | solution.py:35
  27.5 2.2 %collective-permute-done.4 = bf16[256,384]{1,0:T(8,128)(2,1)S(1)} collective-permute-done((bf16[256,384]{1,0:T(8,128)(2,1)S(1)}, bf16[256,384]{1,0:T(8,128)(2,1)S(1)}, u32[]{:S(2)}, u32[]{:S(2)}) %collective-permute-start.4) | collective-permute-done | bytes 196640 | tf_op jit(solution)/shard_map/ppermute | solution.py:35
  29.8 1.5 collective-permute-done.6
  31.2 3.6 %collective-permute-done.5 = bf16[256,384]{1,0:T(8,128)(2,1)S(1)} collective-permute-done((bf16[256,384]{1,0:T(8,128)(2,1)S(1)}, bf16[256,384]{1,0:T(8,128)(2,1)S(1)}, u32[]{:S(2)}, u32[]{:S(2)}) %collective-permute-start.5) | collective-permute-done | bytes 196640 | tf_op jit(solution)/shard_map/ppermute | solution.py:35
  35.8 1.5 collective-permute-start.9
  37.3 2.7 %collective-permute-start.8 = (bf16[2,256,384]{2,1,0:T(8,128)(2,1)}, bf16[2,256,384]{2,1,0:T(8,128)(2,1)}, u32[]{:S(2)}, u32[]{:S(2)}) collective-permute-start(bf16[2,256,384]{2,1,0:T(8,128)(2,1)} %pad_maximum_fusion.2.kv_0.kv_ref), channel_id=1, source_target_pairs={{0,64},{32,96},{64,0},{96,32},{1,65},{33,97},{65,1},{97,33},{2,66}... | collective-permute-start | bytes 1179656 | tf_op jit(solution)/shard_map/ppermute | solution.py:35
  40.0 1.4 collective-permute-start.7
  41.5 7.4 %collective-permute-done.9.kv_3 = bf16[2,256,384]{2,1,0:T(8,128)(2,1)} collective-permute-done((bf16[2,256,384]{2,1,0:T(8,128)(2,1)}, bf16[2,256,384]{2,1,0:T(8,128)(2,1)}, u32[]{:S(2)}, u32[]{:S(2)}) %collective-permute-start.9) | collective-permute-done | bytes 393248 | tf_op jit(solution)/shard_map/ppermute | solution.py:35
  48.9 9.4 %collective-permute-done.8.kv_2 = bf16[2,256,384]{2,1,0:T(8,128)(2,1)} collective-permute-done((bf16[2,256,384]{2,1,0:T(8,128)(2,1)}, bf16[2,256,384]{2,1,0:T(8,128)(2,1)}, u32[]{:S(2)}, u32[]{:S(2)}) %collective-permute-start.8) | collective-permute-done | bytes 393248 | tf_op jit(solution)/shard_map/ppermute | solution.py:35
  58.3 7.4 %shard_map.162 = (bf16[4,256,384]{2,1,0:T(8,128)(2,1)S(1)}, f32[4,8,256]{2,1,0:T(8,128)S(1)}) custom-call(s32[32]{0:T(128)S(1)} %copy-done.5, s32[1]{0:T(128)} %bitcast.5.index_ref, bf16[4,256,384]{2,1,0:T(8,128)(2,1)S(1)} %pad_maximum_fusion.1.q_ref.qa_ref, bf16[2,256,384]{2,1,0:T(8,128)(2,1)} %pad_maximum_fusion.2.kv_0.kv_ref, ...), custom_call_target="tpu_custom_call" | custom-call | flops 1610612736 | bytes 2097152 | tf_op jit(solution)/shard_map/pallas_call | solution.py:57
  66.7 1.4 collective-permute-start.17
  68.2 2.4 %collective-permute-start.16 = (f32[136,384]{1,0:T(8,128)S(1)}, f32[136,384]{1,0:T(8,128)S(1)}, u32[]{:S(2)}, u32[]{:S(2)}) collective-permute-start(f32[136,384]{1,0:T(8,128)S(1)} %get-tuple-element.49.own), channel_id=1, source_target_pairs={{0,64},{32,96},{64,0},{96,32},{1,65},{33,97},{65,1},{97,33},{2,66}... | collective-permute-start | bytes 626696 | tf_op jit(solution)/shard_map/ppermute | solution.py:35
  70.5 1.6 collective-permute-start.15
  72.1 7.4 %shard_map.163 = (bf16[4,256,384]{2,1,0:T(8,128)(2,1)S(1)}, f32[4,8,256]{2,1,0:T(8,128)S(1)}) custom-call(s32[32]{0:T(128)S(1)} %copy-done.5, s32[1]{0:T(128)} %bitcast.5.index_ref, bf16[4,256,384]{2,1,0:T(8,128)(2,1)} %collective-permute-done.10.q_ref.qb_ref, bf16[2,256,384]{2,1,0:T(8,128)(2,1)} %pad_maximum_fusion.2.kv_0.kv_ref, ...), custom_call_target="tpu_custom_call" | custom-call | flops 1610612736 | bytes 2097152 | tf_op jit(solution)/shard_map/pallas_call | solution.py:57
  79.5 1.7 shard_map.164.part_ref
  82.6 1.6 collective-permute-start.14
  84.3 3.6 %collective-permute-start.13 = (f32[2,4,8,256]{3,2,1,0:T(8,128)S(1)}, f32[2,4,8,256]{3,2,1,0:T(8,128)S(1)}, u32[]{:S(2)}, u32[]{:S(2)}) collective-permute-start(f32[2,4,8,256]{3,2,1,0:T(8,128)S(1)} %shard_map.165.chip_ref), channel_id=1, source_target_pairs={{0,16},{8,24},{16,0},{24,8},{1,17},{9,25},{17,1},{25,9},{2,18},{10... | collective-permute-start | bytes 196616 | tf_op jit(solution)/shard_map/ppermute | solution.py:35
  87.9 2.2 %shard_map.167 = (f32[256,384]{1,0:T(8,128)S(1)}, f32[8,256]{1,0:T(8,128)S(1)}, bf16[128,384]{1,0:T(8,128)(2,1)S(1)}, f32[8,384]{1,0:T(8,128)S(1)}) custom-call(s32[32]{0:T(128)S(1)} %copy-done.5, s32[1]{0:T(128)} %bitcast.5.index_ref, bf16[256,384]{1,0:T(8,128)(2,1)S(1)} %copy-done.2, bf16[256,384]{1,0:T(8,128)(2,1)S(1)} %copy-done, ...), custom_call_target="tpu_custom_call" | custom-call | flops 134217728 | bytes 2097152 | tf_op jit(solution)/shard_map/pallas_call | solution.py:57
  90.1 2.0 %collective-permute-start.20 = (f32[8,256]{1,0:T(8,128)S(1)}, f32[8,256]{1,0:T(8,128)S(1)}, u32[]{:S(2)}, u32[]{:S(2)}) collective-permute-start(f32[8,256]{1,0:T(8,128)S(1)} %get-tuple-element.52.sum_0), channel_id=1, source_target_pairs={{0,1},{1,2},{2,3},{3,0},{4,5},{5,6},{6,7},{7,4},{8,9},{9,10},{10,1... | collective-permute-start | bytes 24584 | tf_op jit(solution)/shard_map/ppermute | solution.py:35
  92.1 3.6 %collective-permute-start.19 = (f32[8,256]{1,0:T(8,128)S(1)}, f32[8,256]{1,0:T(8,128)S(1)}, u32[]{:S(2)}, u32[]{:S(2)}) collective-permute-start(f32[8,256]{1,0:T(8,128)S(1)} %get-tuple-element.52.sum_0), channel_id=1, source_target_pairs={{0,2},{1,3},{2,0},{3,1},{4,6},{5,7},{6,4},{7,5},{8,10},{9,11},{10,... | collective-permute-start | bytes 24584 | tf_op jit(solution)/shard_map/ppermute | solution.py:35
  95.8 2.0 %collective-permute-start.18 = (f32[8,256]{1,0:T(8,128)S(1)}, f32[8,256]{1,0:T(8,128)S(1)}, u32[]{:S(2)}, u32[]{:S(2)}) collective-permute-start(f32[8,256]{1,0:T(8,128)S(1)} %get-tuple-element.52.sum_0), channel_id=1, source_target_pairs={{0,3},{1,0},{2,1},{3,2},{4,7},{5,4},{6,5},{7,6},{8,11},{9,8},{10,9... | collective-permute-start | bytes 24584 | tf_op jit(solution)/shard_map/ppermute | solution.py:35
  97.9 1.6 collective-permute-done.18.sum_1
  99.5 2.5 %shard_map.168 = (f32[256,384]{1,0:T(8,128)}, f32[256,384]{1,0:T(8,128)}, f32[256,384]{1,0:T(8,128)S(1)}, f32[256,384]{1,0:T(8,128)S(1)}, bf16[128,384]{1,0:T(8,128)(2,1)S(1)}) custom-call(bf16[256,384]{1,0:T(8,128)(2,1)S(1)} %copy-done.2, bf16[256,384]{1,0:T(8,128)(2,1)S(1)} %copy-done, bf16[256,384]{1,0:T(8,128)(2,1)S(1)} %copy-done.1, ...), custom_call_target="tpu_custom_call" | custom-call | flops 268435456 | bytes 2097152 | tf_op jit(solution)/shard_map/pallas_call | solution.py:57
  102.0 1.3 shard_map.169
  103.3 5.7 %shard_map.171 = (f32[4,3,128,256]{3,2,1,0:T(8,128)S(1)}, f32[4,3,128,256]{3,2,1,0:T(8,128)S(1)}, bf16[3,2,256,384]{3,2,1,0:T(8,128)(2,1)S(1)}) custom-call(s32[32]{0:T(128)S(1)} %copy-done.5, s32[1]{0:T(128)} %bitcast.5.index_ref, bf16[4,256,384]{2,1,0:T(8,128)(2,1)S(1)} %pad_maximum_fusion.1.q_ref.qa_ref, ...), custom_call_target="tpu_custom_call" | custom-call | flops 2013265920 | bytes 2097152 | tf_op jit(solution)/shard_map/pallas_call | solution.py:57
  109.0 10.1 %shard_map.172 = (f32[4,3,128,256]{3,2,1,0:T(8,128)S(1)}, f32[4,3,128,256]{3,2,1,0:T(8,128)S(1)}, bf16[3,2,256,384]{3,2,1,0:T(8,128)(2,1)S(1)}) custom-call(s32[32]{0:T(128)S(1)} %copy-done.5, s32[1]{0:T(128)} %bitcast.5.index_ref, ...), custom_call_target="tpu_custom_call", output_to_operand_aliasing={{0}: (10, {}), {1}: (11, {}), {2}: (12, {})} | custom-call | flops 4026531840 | bytes 2097152 | tf_op jit(solution)/shard_map/pallas_call | solution.py:57
  119.1 6.7 %shard_map.173 = (bf16[4,256,384]{2,1,0:T(8,128)(2,1)S(1)}, bf16[4,256,384]{2,1,0:T(8,128)(2,1)S(1)}, f32[2,256,384]{2,1,0:T(8,128)S(1)}) custom-call(s32[32]{0:T(128)S(1)} %copy-done.5, s32[1]{0:T(128)} %bitcast.5.index_ref, bf16[4,256,384]{2,1,0:T(8,128)(2,1)S(1)} %pad_maximum_fusion.1.q_ref.qa_ref, ...), custom_call_target="tpu_custom_call" | custom-call | flops 2013265920 | bytes 2097152 | tf_op jit(solution)/shard_map/pallas_call | solution.py:57
  128.2 1.9 collective-permute-start.30
  130.4 2.1 %collective-permute-start.26 = (bf16[256,384]{1,0:T(8,128)(2,1)S(1)}, bf16[256,384]{1,0:T(8,128)(2,1)S(1)}, u32[]{:S(2)}, u32[]{:S(2)}) collective-permute-start(bf16[256,384]{1,0:T(8,128)(2,1)S(1)} %get-tuple-element.85), channel_id=1, source_target_pairs={{0,8},{8,16},{16,24},{24,0},{1,9},{9,17},{17,25},{25,1},{2,10},{10... | collective-permute-start | bytes 589832 | tf_op jit(solution)/shard_map/ppermute | solution.py:35
  132.5 14.9 %collective-permute-done.29 = bf16[2,256,384]{2,1,0:T(8,128)(2,1)S(1)} collective-permute-done((bf16[2,256,384]{2,1,0:T(8,128)(2,1)S(1)}, bf16[2,256,384]{2,1,0:T(8,128)(2,1)S(1)}, u32[]{:S(2)}, u32[]{:S(2)}) %collective-permute-start.29) | collective-permute-done | bytes 393248 | tf_op jit(solution)/shard_map/ppermute | solution.py:35
  149.2 3.1 %collective-permute-start.27 = (bf16[256,384]{1,0:T(8,128)(2,1)S(1)}, bf16[256,384]{1,0:T(8,128)(2,1)S(1)}, u32[]{:S(2)}, u32[]{:S(2)}) collective-permute-start(bf16[256,384]{1,0:T(8,128)(2,1)S(1)} %get-tuple-element.87), channel_id=1, source_target_pairs={{0,24},{8,0},{16,8},{24,16},{1,25},{9,1},{17,9},{25,17},{2,26},{10... | collective-permute-start | bytes 589832 | tf_op jit(solution)/shard_map/ppermute | solution.py:35
  152.7 2.0 %collective-permute-start.23 = (bf16[512,384]{1,0:T(8,128)(2,1)S(1)}, bf16[512,384]{1,0:T(8,128)(2,1)S(1)}, u32[]{:S(2)}, u32[]{:S(2)}) collective-permute-start(bf16[512,384]{1,0:T(8,128)(2,1)S(1)} %get-tuple-element.58), channel_id=1, source_target_pairs={{0,24},{8,0},{16,8},{24,16},{1,25},{9,1},{17,9},{25,17},{2,26},{10... | collective-permute-start | bytes 1179656 | tf_op jit(solution)/shard_map/ppermute | solution.py:35
  156.2 1.4 collective-permute-done.28
  157.6 2.3 %collective-permute-done.27 = bf16[256,384]{1,0:T(8,128)(2,1)S(1)} collective-permute-done((bf16[256,384]{1,0:T(8,128)(2,1)S(1)}, bf16[256,384]{1,0:T(8,128)(2,1)S(1)}, u32[]{:S(2)}, u32[]{:S(2)}) %collective-permute-start.27) | collective-permute-done | bytes 196640 | tf_op jit(solution)/shard_map/ppermute | solution.py:35
  160.7 5.9 %collective-permute-done.22.from_3 = bf16[512,384]{1,0:T(8,128)(2,1)S(1)} collective-permute-done((bf16[512,384]{1,0:T(8,128)(2,1)S(1)}, bf16[512,384]{1,0:T(8,128)(2,1)S(1)}, u32[]{:S(2)}, u32[]{:S(2)}) %collective-permute-start.22) | collective-permute-done | bytes 393248 | tf_op jit(solution)/shard_map/ppermute | solution.py:35
  166.6 1.9 collective-permute-done.23.from_1
  168.4 8.3 %collective-permute-done.24.from_2 = bf16[512,384]{1,0:T(8,128)(2,1)S(1)} collective-permute-done((bf16[512,384]{1,0:T(8,128)(2,1)S(1)}, bf16[512,384]{1,0:T(8,128)(2,1)S(1)}, u32[]{:S(2)}, u32[]{:S(2)}) %collective-permute-start.24) | collective-permute-done | bytes 393248 | tf_op jit(solution)/shard_map/ppermute | solution.py:35
  177.7 1.3 collective-permute-start.34
  179.0 3.3 %collective-permute-start.33 = (f32[128,384]{1,0:T(8,128)S(1)}, f32[128,384]{1,0:T(8,128)S(1)}, u32[]{:S(2)}, u32[]{:S(2)}) collective-permute-start(f32[128,384]{1,0:T(8,128)S(1)} %get-tuple-element.75.own), channel_id=1, source_target_pairs={{0,64},{32,96},{64,0},{96,32},{1,65},{33,97},{65,1},{97,33},{2,66}... | collective-permute-start | bytes 589832 | tf_op jit(solution)/shard_map/ppermute | solution.py:35
  183.1 2.6 %collective-permute-done.34.from_3 = f32[128,384]{1,0:T(8,128)S(1)} collective-permute-done((f32[128,384]{1,0:T(8,128)S(1)}, f32[128,384]{1,0:T(8,128)S(1)}, u32[]{:S(2)}, u32[]{:S(2)}) %collective-permute-start.34) | collective-permute-done | bytes 196640 | tf_op jit(solution)/shard_map/ppermute | solution.py:35
  185.7 4.5 %collective-permute-done.33.from_2 = f32[128,384]{1,0:T(8,128)S(1)} collective-permute-done((f32[128,384]{1,0:T(8,128)S(1)}, f32[128,384]{1,0:T(8,128)S(1)}, u32[]{:S(2)}, u32[]{:S(2)}) %collective-permute-start.33) | collective-permute-done | bytes 196640 | tf_op jit(solution)/shard_map/ppermute | solution.py:35
  190.2 2.0 %shard_map.175 = (f32[256,384]{1,0:T(8,128)}, f32[256,384]{1,0:T(8,128)}) custom-call(s32[32]{0:T(128)S(1)} %copy-done.5, s32[1]{0:T(128)} %bitcast.5.index_ref, bf16[256,384]{1,0:T(8,128)(2,1)S(1)} %copy-done, bf16[256,384]{1,0:T(8,128)(2,1)S(1)} %copy-done.1, f32[3,256]{1,0:T(4,128)S(1)} %bitcast.41, f32[136,384]{1,0:T(8,128)S(1)} %get-tuple-element.73.part_ref, ...), custom_call_target="tpu_custom_call" | custom-call | flops 67108864 | bytes 2097152 | tf_op jit(solution)/shard_map/pallas_call | solution.py:57
  (65 shorter events, 16.6 us)
Async XLA Ops:
  3.3 10.4 %collective-permute-start.2 = (bf16[400,384]{1,0:T(8,128)(2,1)}, bf16[400,384]{1,0:T(8,128)(2,1)S(1)}, u32[]{:S(2)}, u32[]{:S(2)}) collective-permute-start(bf16[400,384]{1,0:T(8,128)(2,1)} %shard_map.161), channel_id=1, source_target_pairs={{0,8},{8,16},{16,24},{24,0},{1,9},{9,17},{17,25},{25,1},{2,10},{10... | collective-permute-start | bytes 921608 | tf_op jit(solution)/shard_map/ppermute | solution.py:35
  4.9 11.9 %collective-permute-start.1 = (bf16[400,384]{1,0:T(8,128)(2,1)}, bf16[400,384]{1,0:T(8,128)(2,1)S(1)}, u32[]{:S(2)}, u32[]{:S(2)}) collective-permute-start(bf16[400,384]{1,0:T(8,128)(2,1)} %shard_map.161), channel_id=1, source_target_pairs={{0,16},{8,24},{16,0},{24,8},{1,17},{9,25},{17,1},{25,9},{2,18},{10... | collective-permute-start | bytes 921608 | tf_op jit(solution)/shard_map/ppermute | solution.py:35
  5.7 15.4 %collective-permute-start = (bf16[400,384]{1,0:T(8,128)(2,1)}, bf16[400,384]{1,0:T(8,128)(2,1)S(1)}, u32[]{:S(2)}, u32[]{:S(2)}) collective-permute-start(bf16[400,384]{1,0:T(8,128)(2,1)} %shard_map.161), channel_id=1, source_target_pairs={{0,24},{8,0},{16,8},{24,16},{1,25},{9,1},{17,9},{25,17},{2,26},{10... | collective-permute-start | bytes 921608 | tf_op jit(solution)/shard_map/ppermute | solution.py:35
  21.1 1.3 copy-start.6
  22.3 12.7 %copy-start.7 = (bf16[256,384]{1,0:T(8,128)(2,1)S(1)}, bf16[256,384]{1,0:T(8,128)(2,1)}, u32[]{:S(2)}) copy-start(bf16[256,384]{1,0:T(8,128)(2,1)} %param.13) | copy-start | bytes 589828
  22.3 12.7 %copy-start.8 = (bf16[256,384]{1,0:T(8,128)(2,1)S(1)}, bf16[256,384]{1,0:T(8,128)(2,1)}, u32[]{:S(2)}) copy-start(bf16[256,384]{1,0:T(8,128)(2,1)} %param.12) | copy-start | bytes 589828
  22.3 35.9 %copy-start.5 = (s32[32]{0:T(128)S(1)}, s32[32]{0:T(128)}, u32[]{:S(2)}) copy-start(s32[32]{0:T(128)} %group_ref.17) | copy-start | bytes 388
  22.4 43.3 %collective-permute-start.3 = (bf16[4,400,384]{2,1,0:T(8,128)(2,1)S(1)}, bf16[4,400,384]{2,1,0:T(8,128)(2,1)S(1)}, u32[]{:S(2)}, u32[]{:S(2)}) collective-permute-start(bf16[4,400,384]{2,1,0:T(8,128)(2,1)S(1)} %pad_maximum_fusion.g_a.ga_ref), channel_id=1, source_target_pairs={{0,4},{4,0},{1,5},{5,1},{2,6},{6,2},{3,7},{7,3},{8,12},{12,8},{9,1... | collective-permute-start | bytes 3686408 | tf_op jit(solution)/shard_map/ppermute | solution.py:35
  22.5 7.3 %collective-permute-start.4 = (bf16[256,384]{1,0:T(8,128)(2,1)S(1)}, bf16[256,384]{1,0:T(8,128)(2,1)S(1)}, u32[]{:S(2)}, u32[]{:S(2)}) collective-permute-start(bf16[256,384]{1,0:T(8,128)(2,1)S(1)} %copy-done.6), channel_id=1, source_target_pairs={{0,24},{8,0},{16,8},{24,16},{1,25},{9,1},{17,9},{25,17},{2,26},{10... | collective-permute-start | bytes 589832 | tf_op jit(solution)/shard_map/ppermute | solution.py:35
  23.4 7.8 %collective-permute-start.6 = (bf16[256,384]{1,0:T(8,128)(2,1)S(1)}, bf16[256,384]{1,0:T(8,128)(2,1)S(1)}, u32[]{:S(2)}, u32[]{:S(2)}) collective-permute-start(bf16[256,384]{1,0:T(8,128)(2,1)S(1)} %copy-done.6), channel_id=1, source_target_pairs={{0,8},{8,16},{16,24},{24,0},{1,9},{9,17},{17,25},{25,1},{2,10},{10... | collective-permute-start | bytes 589832 | tf_op jit(solution)/shard_map/ppermute | solution.py:35
  24.6 10.2 %collective-permute-start.5 = (bf16[256,384]{1,0:T(8,128)(2,1)S(1)}, bf16[256,384]{1,0:T(8,128)(2,1)S(1)}, u32[]{:S(2)}, u32[]{:S(2)}) collective-permute-start(bf16[256,384]{1,0:T(8,128)(2,1)S(1)} %copy-done.6), channel_id=1, source_target_pairs={{0,16},{8,24},{16,0},{24,8},{1,17},{9,25},{17,1},{25,9},{2,18},{10... | collective-permute-start | bytes 589832 | tf_op jit(solution)/shard_map/ppermute | solution.py:35
  34.9 37.2 %collective-permute-start.10 = (bf16[4,256,384]{2,1,0:T(8,128)(2,1)S(1)}, bf16[4,256,384]{2,1,0:T(8,128)(2,1)}, u32[]{:S(2)}, u32[]{:S(2)}) collective-permute-start(bf16[4,256,384]{2,1,0:T(8,128)(2,1)S(1)} %pad_maximum_fusion.1.q_ref.qa_ref), channel_id=1, source_target_pairs={{0,4},{4,0},{1,5},{5,1},{2,6},{6,2},{3,7},{7,3},{8,12},{12,8},{9,1... | collective-permute-start | bytes 2359304 | tf_op jit(solution)/shard_map/ppermute | solution.py:35
  35.8 13.0 %collective-permute-start.9 = (bf16[2,256,384]{2,1,0:T(8,128)(2,1)}, bf16[2,256,384]{2,1,0:T(8,128)(2,1)}, u32[]{:S(2)}, u32[]{:S(2)}) collective-permute-start(bf16[2,256,384]{2,1,0:T(8,128)(2,1)} %pad_maximum_fusion.2.kv_0.kv_ref), channel_id=1, source_target_pairs={{0,32},{32,64},{64,96},{96,0},{1,33},{33,65},{65,97},{97,1},{2,34}... | collective-permute-start | bytes 1179656 | tf_op jit(solution)/shard_map/ppermute | solution.py:35
  37.3 20.9 %collective-permute-start.8 = (bf16[2,256,384]{2,1,0:T(8,128)(2,1)}, bf16[2,256,384]{2,1,0:T(8,128)(2,1)}, u32[]{:S(2)}, u32[]{:S(2)}) collective-permute-start(bf16[2,256,384]{2,1,0:T(8,128)(2,1)} %pad_maximum_fusion.2.kv_0.kv_ref), channel_id=1, source_target_pairs={{0,64},{32,96},{64,0},{96,32},{1,65},{33,97},{65,1},{97,33},{2,66}... | collective-permute-start | bytes 1179656 | tf_op jit(solution)/shard_map/ppermute | solution.py:35
  40.0 18.2 %collective-permute-start.7 = (bf16[2,256,384]{2,1,0:T(8,128)(2,1)}, bf16[2,256,384]{2,1,0:T(8,128)(2,1)}, u32[]{:S(2)}, u32[]{:S(2)}) collective-permute-start(bf16[2,256,384]{2,1,0:T(8,128)(2,1)} %pad_maximum_fusion.2.kv_0.kv_ref), channel_id=1, source_target_pairs={{0,96},{32,0},{64,32},{96,64},{1,97},{33,1},{65,33},{97,65},{2,98}... | collective-permute-start | bytes 1179656 | tf_op jit(solution)/shard_map/ppermute | solution.py:35
  66.7 21.1 %collective-permute-start.17 = (f32[136,384]{1,0:T(8,128)S(1)}, f32[136,384]{1,0:T(8,128)S(1)}, u32[]{:S(2)}, u32[]{:S(2)}) collective-permute-start(f32[136,384]{1,0:T(8,128)S(1)} %get-tuple-element.49.own), channel_id=1, source_target_pairs={{0,32},{32,64},{64,96},{96,0},{1,33},{33,65},{65,97},{97,1},{2,34}... | collective-permute-start | bytes 626696 | tf_op jit(solution)/shard_map/ppermute | solution.py:35
  68.2 19.7 %collective-permute-start.16 = (f32[136,384]{1,0:T(8,128)S(1)}, f32[136,384]{1,0:T(8,128)S(1)}, u32[]{:S(2)}, u32[]{:S(2)}) collective-permute-start(f32[136,384]{1,0:T(8,128)S(1)} %get-tuple-element.49.own), channel_id=1, source_target_pairs={{0,64},{32,96},{64,0},{96,32},{1,65},{33,97},{65,1},{97,33},{2,66}... | collective-permute-start | bytes 626696 | tf_op jit(solution)/shard_map/ppermute | solution.py:35
  70.5 17.3 %collective-permute-start.15 = (f32[136,384]{1,0:T(8,128)S(1)}, f32[136,384]{1,0:T(8,128)S(1)}, u32[]{:S(2)}, u32[]{:S(2)}) collective-permute-start(f32[136,384]{1,0:T(8,128)S(1)} %get-tuple-element.49.own), channel_id=1, source_target_pairs={{0,96},{32,0},{64,32},{96,64},{1,97},{33,1},{65,33},{97,65},{2,98}... | collective-permute-start | bytes 626696 | tf_op jit(solution)/shard_map/ppermute | solution.py:35
  79.5 8.4 %copy-start = (bf16[256,384]{1,0:T(8,128)(2,1)S(1)}, bf16[256,384]{1,0:T(8,128)(2,1)}, u32[]{:S(2)}) copy-start(bf16[256,384]{1,0:T(8,128)(2,1)} %k_ref.5) | copy-start | bytes 589828
  79.5 8.4 %copy-start.1 = (bf16[256,384]{1,0:T(8,128)(2,1)S(1)}, bf16[256,384]{1,0:T(8,128)(2,1)}, u32[]{:S(2)}) copy-start(bf16[256,384]{1,0:T(8,128)(2,1)} %v_ref.5) | copy-start | bytes 589828
  79.5 8.4 %copy-start.2 = (bf16[256,384]{1,0:T(8,128)(2,1)S(1)}, bf16[256,384]{1,0:T(8,128)(2,1)}, u32[]{:S(2)}) copy-start(bf16[256,384]{1,0:T(8,128)(2,1)} %q_ref.3) | copy-start | bytes 589828
  79.5 8.4 %copy-start.3 = (bf16[256,384]{1,0:T(8,128)(2,1)S(1)}, bf16[256,384]{1,0:T(8,128)(2,1)}, u32[]{:S(2)}) copy-start(bf16[256,384]{1,0:T(8,128)(2,1)} %g_ref.5) | copy-start | bytes 589828
  79.5 8.4 %copy-start.4 = (f32[256,3]{0,1:T(4,128)S(1)}, f32[256,3]{0,1:T(4,128)}, u32[]{:S(2)}) copy-start(f32[256,3]{0,1:T(4,128)} %param.18) | copy-start | bytes 9220
  81.2 1.3 collective-permute-start.11
  82.6 19.4 %collective-permute-start.14 = (f32[2,4,8,256]{3,2,1,0:T(8,128)S(1)}, f32[2,4,8,256]{3,2,1,0:T(8,128)S(1)}, u32[]{:S(2)}, u32[]{:S(2)}) collective-permute-start(f32[2,4,8,256]{3,2,1,0:T(8,128)S(1)} %shard_map.165.chip_ref), channel_id=1, source_target_pairs={{0,8},{8,16},{16,24},{24,0},{1,9},{9,17},{17,25},{25,1},{2,10},{10... | collective-permute-start | bytes 196616 | tf_op jit(solution)/shard_map/ppermute | solution.py:35
  84.3 17.8 %collective-permute-start.13 = (f32[2,4,8,256]{3,2,1,0:T(8,128)S(1)}, f32[2,4,8,256]{3,2,1,0:T(8,128)S(1)}, u32[]{:S(2)}, u32[]{:S(2)}) collective-permute-start(f32[2,4,8,256]{3,2,1,0:T(8,128)S(1)} %shard_map.165.chip_ref), channel_id=1, source_target_pairs={{0,16},{8,24},{16,0},{24,8},{1,17},{9,25},{17,1},{25,9},{2,18},{10... | collective-permute-start | bytes 196616 | tf_op jit(solution)/shard_map/ppermute | solution.py:35
  87.8 14.2 %collective-permute-start.12 = (f32[2,4,8,256]{3,2,1,0:T(8,128)S(1)}, f32[2,4,8,256]{3,2,1,0:T(8,128)S(1)}, u32[]{:S(2)}, u32[]{:S(2)}) collective-permute-start(f32[2,4,8,256]{3,2,1,0:T(8,128)S(1)} %shard_map.165.chip_ref), channel_id=1, source_target_pairs={{0,24},{8,0},{16,8},{24,16},{1,25},{9,1},{17,9},{25,17},{2,26},{10... | collective-permute-start | bytes 196616 | tf_op jit(solution)/shard_map/ppermute | solution.py:35
  90.1 5.7 %collective-permute-start.20 = (f32[8,256]{1,0:T(8,128)S(1)}, f32[8,256]{1,0:T(8,128)S(1)}, u32[]{:S(2)}, u32[]{:S(2)}) collective-permute-start(f32[8,256]{1,0:T(8,128)S(1)} %get-tuple-element.52.sum_0), channel_id=1, source_target_pairs={{0,1},{1,2},{2,3},{3,0},{4,5},{5,6},{6,7},{7,4},{8,9},{9,10},{10,1... | collective-permute-start | bytes 24584 | tf_op jit(solution)/shard_map/ppermute | solution.py:35
  92.1 5.8 %collective-permute-start.19 = (f32[8,256]{1,0:T(8,128)S(1)}, f32[8,256]{1,0:T(8,128)S(1)}, u32[]{:S(2)}, u32[]{:S(2)}) collective-permute-start(f32[8,256]{1,0:T(8,128)S(1)} %get-tuple-element.52.sum_0), channel_id=1, source_target_pairs={{0,2},{1,3},{2,0},{3,1},{4,6},{5,7},{6,4},{7,5},{8,10},{9,11},{10,... | collective-permute-start | bytes 24584 | tf_op jit(solution)/shard_map/ppermute | solution.py:35
  95.8 3.7 %collective-permute-start.18 = (f32[8,256]{1,0:T(8,128)S(1)}, f32[8,256]{1,0:T(8,128)S(1)}, u32[]{:S(2)}, u32[]{:S(2)}) collective-permute-start(f32[8,256]{1,0:T(8,128)S(1)} %get-tuple-element.52.sum_0), channel_id=1, source_target_pairs={{0,3},{1,0},{2,1},{3,2},{4,7},{5,4},{6,5},{7,6},{8,11},{9,8},{10,9... | collective-permute-start | bytes 24584 | tf_op jit(solution)/shard_map/ppermute | solution.py:35
  125.8 4.3 %collective-permute-start.25 = (bf16[4,256,384]{2,1,0:T(8,128)(2,1)S(1)}, bf16[4,256,384]{2,1,0:T(8,128)(2,1)S(1)}, u32[]{:S(2)}, u32[]{:S(2)}) collective-permute-start(bf16[4,256,384]{2,1,0:T(8,128)(2,1)S(1)} %get-tuple-element.67), channel_id=1, source_target_pairs={{0,4},{4,0},{1,5},{5,1},{2,6},{6,2},{3,7},{7,3},{8,12},{12,8},{9,1... | collective-permute-start | bytes 2359304 | tf_op jit(solution)/shard_map/ppermute | solution.py:35
  125.9 26.4 %collective-permute-start.21 = (bf16[1152,384]{1,0:T(8,128)(2,1)S(1)}, bf16[1152,384]{1,0:T(8,128)(2,1)S(1)}, u32[]{:S(2)}, u32[]{:S(2)}) collective-permute-start(bf16[1152,384]{1,0:T(8,128)(2,1)S(1)} %get-tuple-element.55), channel_id=1, source_target_pairs={{0,4},{4,0},{1,5},{5,1},{2,6},{6,2},{3,7},{7,3},{8,12},{12,8},{9,1... | collective-permute-start | bytes 2654216 | tf_op jit(solution)/shard_map/ppermute | solution.py:35
  126.6 20.8 %collective-permute-start.29 = (bf16[2,256,384]{2,1,0:T(8,128)(2,1)S(1)}, bf16[2,256,384]{2,1,0:T(8,128)(2,1)S(1)}, u32[]{:S(2)}, u32[]{:S(2)}) collective-permute-start(bf16[2,256,384]{2,1,0:T(8,128)(2,1)S(1)} %get-tuple-element.82), channel_id=1, source_target_pairs={{0,32},{32,64},{64,96},{96,0},{1,33},{33,65},{65,97},{97,1},{2,34}... | collective-permute-start | bytes 1179656 | tf_op jit(solution)/shard_map/ppermute | solution.py:35
  127.1 20.3 %collective-permute-start.31 = (bf16[2,256,384]{2,1,0:T(8,128)(2,1)S(1)}, bf16[2,256,384]{2,1,0:T(8,128)(2,1)S(1)}, u32[]{:S(2)}, u32[]{:S(2)}) collective-permute-start(bf16[2,256,384]{2,1,0:T(8,128)(2,1)S(1)} %get-tuple-element.83), channel_id=1, source_target_pairs={{0,64},{32,96},{64,0},{96,32},{1,65},{33,97},{65,1},{97,33},{2,66}... | collective-permute-start | bytes 1179656 | tf_op jit(solution)/shard_map/ppermute | solution.py:35
  128.2 19.8 %collective-permute-start.30 = (bf16[2,256,384]{2,1,0:T(8,128)(2,1)S(1)}, bf16[2,256,384]{2,1,0:T(8,128)(2,1)S(1)}, u32[]{:S(2)}, u32[]{:S(2)}) collective-permute-start(bf16[2,256,384]{2,1,0:T(8,128)(2,1)S(1)} %get-tuple-element.84), channel_id=1, source_target_pairs={{0,96},{32,0},{64,32},{96,64},{1,97},{33,1},{65,33},{97,65},{2,98}... | collective-permute-start | bytes 1179656 | tf_op jit(solution)/shard_map/ppermute | solution.py:35
  130.4 24.3 %collective-permute-start.26 = (bf16[256,384]{1,0:T(8,128)(2,1)S(1)}, bf16[256,384]{1,0:T(8,128)(2,1)S(1)}, u32[]{:S(2)}, u32[]{:S(2)}) collective-permute-start(bf16[256,384]{1,0:T(8,128)(2,1)S(1)} %get-tuple-element.85), channel_id=1, source_target_pairs={{0,8},{8,16},{16,24},{24,0},{1,9},{9,17},{17,25},{25,1},{2,10},{10... | collective-permute-start | bytes 589832 | tf_op jit(solution)/shard_map/ppermute | solution.py:35
  148.2 9.4 %collective-permute-start.28 = (bf16[256,384]{1,0:T(8,128)(2,1)S(1)}, bf16[256,384]{1,0:T(8,128)(2,1)S(1)}, u32[]{:S(2)}, u32[]{:S(2)}) collective-permute-start(bf16[256,384]{1,0:T(8,128)(2,1)S(1)} %get-tuple-element.86), channel_id=1, source_target_pairs={{0,16},{8,24},{16,0},{24,8},{1,17},{9,25},{17,1},{25,9},{2,18},{10... | collective-permute-start | bytes 589832 | tf_op jit(solution)/shard_map/ppermute | solution.py:35
  149.2 10.7 %collective-permute-start.27 = (bf16[256,384]{1,0:T(8,128)(2,1)S(1)}, bf16[256,384]{1,0:T(8,128)(2,1)S(1)}, u32[]{:S(2)}, u32[]{:S(2)}) collective-permute-start(bf16[256,384]{1,0:T(8,128)(2,1)S(1)} %get-tuple-element.87), channel_id=1, source_target_pairs={{0,24},{8,0},{16,8},{24,16},{1,25},{9,1},{17,9},{25,17},{2,26},{10... | collective-permute-start | bytes 589832 | tf_op jit(solution)/shard_map/ppermute | solution.py:35
  152.6 13.9 %collective-permute-start.22 = (bf16[512,384]{1,0:T(8,128)(2,1)S(1)}, bf16[512,384]{1,0:T(8,128)(2,1)S(1)}, u32[]{:S(2)}, u32[]{:S(2)}) collective-permute-start(bf16[512,384]{1,0:T(8,128)(2,1)S(1)} %get-tuple-element.57), channel_id=1, source_target_pairs={{0,8},{8,16},{16,24},{24,0},{1,9},{9,17},{17,25},{25,1},{2,10},{10... | collective-permute-start | bytes 1179656 | tf_op jit(solution)/shard_map/ppermute | solution.py:35
  152.7 15.7 %collective-permute-start.23 = (bf16[512,384]{1,0:T(8,128)(2,1)S(1)}, bf16[512,384]{1,0:T(8,128)(2,1)S(1)}, u32[]{:S(2)}, u32[]{:S(2)}) collective-permute-start(bf16[512,384]{1,0:T(8,128)(2,1)S(1)} %get-tuple-element.58), channel_id=1, source_target_pairs={{0,24},{8,0},{16,8},{24,16},{1,25},{9,1},{17,9},{25,17},{2,26},{10... | collective-permute-start | bytes 1179656 | tf_op jit(solution)/shard_map/ppermute | solution.py:35
  154.7 22.0 %collective-permute-start.24 = (bf16[512,384]{1,0:T(8,128)(2,1)S(1)}, bf16[512,384]{1,0:T(8,128)(2,1)S(1)}, u32[]{:S(2)}, u32[]{:S(2)}) collective-permute-start(bf16[512,384]{1,0:T(8,128)(2,1)S(1)} %get-tuple-element.59), channel_id=1, source_target_pairs={{0,16},{8,24},{16,0},{24,8},{1,17},{9,25},{17,1},{25,9},{2,18},{10... | collective-permute-start | bytes 1179656 | tf_op jit(solution)/shard_map/ppermute | solution.py:35
  177.7 8.0 %collective-permute-start.34 = (f32[128,384]{1,0:T(8,128)S(1)}, f32[128,384]{1,0:T(8,128)S(1)}, u32[]{:S(2)}, u32[]{:S(2)}) collective-permute-start(f32[128,384]{1,0:T(8,128)S(1)} %get-tuple-element.75.own), channel_id=1, source_target_pairs={{0,32},{32,64},{64,96},{96,0},{1,33},{33,65},{65,97},{97,1},{2,34}... | collective-permute-start | bytes 589832 | tf_op jit(solution)/shard_map/ppermute | solution.py:35
  179.0 11.2 %collective-permute-start.33 = (f32[128,384]{1,0:T(8,128)S(1)}, f32[128,384]{1,0:T(8,128)S(1)}, u32[]{:S(2)}, u32[]{:S(2)}) collective-permute-start(f32[128,384]{1,0:T(8,128)S(1)} %get-tuple-element.75.own), channel_id=1, source_target_pairs={{0,64},{32,96},{64,0},{96,32},{1,65},{33,97},{65,1},{97,33},{2,66}... | collective-permute-start | bytes 589832 | tf_op jit(solution)/shard_map/ppermute | solution.py:35
  182.3 7.9 %collective-permute-start.32 = (f32[128,384]{1,0:T(8,128)S(1)}, f32[128,384]{1,0:T(8,128)S(1)}, u32[]{:S(2)}, u32[]{:S(2)}) collective-permute-start(f32[128,384]{1,0:T(8,128)S(1)} %get-tuple-element.75.own), channel_id=1, source_target_pairs={{0,96},{32,0},{64,32},{96,64},{1,97},{33,1},{65,33},{97,65},{2,98}... | collective-permute-start | bytes 589832 | tf_op jit(solution)/shard_map/ppermute | solution.py:35

commit v2 on v1

--- a/solution.py
+++ b/solution.py
@@ -366,22 +366,32 @@
     return dot(triangle(False).astype(F32), decay_ref[...], 1, 1, HIGHEST)
 
 
+def log_pieces(log):
+    log = jnp.broadcast_to(log, (16, log.shape[1]))
+    row = lax.broadcasted_iota(jnp.int32, log.shape, 0)
+    high = log.astype(BF16).astype(F32)
+    middle = (log - high).astype(BF16).astype(F32)
+    low = log - high - middle
+    piece = jnp.where(row == 0, high, jnp.where(row == 1, middle, jnp.where(row == 2, low, 0.0)))
+    return piece.astype(BF16)
+
+
+def whole_log(pieces):
+    pieces = pieces.astype(F32)
+    return pieces[0:1] + pieces[1:2] + pieces[2:3]
+
+
 def pack_kernel(g_ref, key_ref, value_ref, decay_ref, out_ref):
     cumulative = decay_columns(decay_ref)
     total = cumulative[TOK - 1 : TOK]
     tail = jnp.exp(total - cumulative)
     out_ref[pl.ds(0, TOK)] = g_ref[...]
-    row = lax.broadcasted_iota(jnp.int32, (16, HEAD_DIM), 0)
     for h in range(HEADS):
         keys = key_ref[:, head_cols(h)].astype(F32) * tail[:, h : h + 1]
         state = dot(keys.astype(BF16), value_ref[:, head_cols(h)], 0, 0)
         out_ref[pl.ds(STATE_ROW, HEAD_DIM), head_cols(h)] = state.astype(BF16)
-        log = jnp.broadcast_to(total[:, h : h + 1], (16, HEAD_DIM))
-        high = log.astype(BF16).astype(F32)
-        middle = (log - high).astype(BF16).astype(F32)
-        low = log - high - middle
-        piece = jnp.where(row == 0, high, jnp.where(row == 1, middle, jnp.where(row == 2, low, 0.0)))
-        out_ref[pl.ds(LOG_ROW, 16), head_cols(h)] = piece.astype(BF16)
+        log = jnp.broadcast_to(total[:, h : h + 1], (1, HEAD_DIM))
+        out_ref[pl.ds(LOG_ROW, 16), head_cols(h)] = log_pieces(log)
 
 
 def least(values):
@@ -436,7 +446,7 @@
             if i != o:
                 between = earlier[i] * flag(starts[i] > starts[o])
                 exponent = exponent + line_logs[i] * between.astype(F32)
-        result = result + jnp.exp(exponent) * earlier[o].astype(F32) * totals[o]
+        result = result + jnp.exp(exponent) * earlier[o].astype(F32) * totals[o].astype(F32)
     return result
 
 
@@ -444,8 +454,7 @@
     logs, states = [], []
     for ref in (ga_ref, gb_ref):
         for i in range(NY):
-            rows = ref[i, pl.ds(LOG_ROW, 16)].astype(F32)
-            logs.append(rows[0:1] + rows[1:2] + rows[2:3])
+            logs.append(whole_log(ref[i, pl.ds(LOG_ROW, 16)]))
             states.append(
                 functools.partial(
                     lambda ref, i: ref[i, pl.ds(STATE_ROW, HEAD_DIM)].astype(F32), ref, i
@@ -453,16 +462,19 @@
             )
     keys = chain_keys(group_ref, index_ref, 0, True)
     handed, entry, prefix = line_sums(keys, logs, states)
-    handed_ref[pl.ds(0, HEAD_DIM)] = handed
-    handed_ref[pl.ds(HEAD_DIM, 8)] = jnp.broadcast_to(sum(logs), (8, WIDTH))
+    handed_ref[pl.ds(0, HEAD_DIM)] = handed.astype(BF16)
+    handed_ref[pl.ds(HEAD_DIM, 16)] = log_pieces(sum(logs))
     entry_ref[pl.ds(0, HEAD_DIM)] = entry
     entry_ref[pl.ds(HEAD_DIM, 8)] = jnp.broadcast_to(prefix, (8, WIDTH))
     for j in range(LINE):
         log_ref[pl.ds(j, 1)] = logs[j]
 
 
-def inner_terms(q, k, decay_ref, cumulative, h):
-    rows = dot(decay_ref[...], triangle(True).astype(F32), 1, 0, HIGHEST)
+def decay_rows(decay_ref):
+    return dot(decay_ref[...], triangle(True).astype(F32), 1, 0, HIGHEST)
+
+
+def inner_terms(q, k, rows, cumulative, h):
     gap = cumulative[:, h : h + 1] - rows[h : h + 1]
     decay = jnp.where(triangle(False), jnp.exp(jnp.minimum(gap, 0.0)), 0.0)
     return decay, (dot(q, k, 1, 1) * decay).astype(BF16)
@@ -473,7 +485,7 @@
     from_3, raw_ref, sum_ref, entry_ref, log_ref,
 ):
     all_totals = (own, from_1, from_2, from_3)
-    line_logs = [t[pl.ds(HEAD_DIM, 1)] for t in all_totals]
+    line_logs = [whole_log(t[pl.ds(HEAD_DIM, 16)]) for t in all_totals]
     for o in range(NX):
         log_ref[pl.ds(o, 1)] = line_logs[o]
     log_ref[pl.ds(NX, 4)] = jnp.zeros((4, WIDTH), F32)
@@ -482,13 +494,13 @@
         part_ref[pl.ds(HEAD_DIM, 1)],
     )
     entry_ref[...] = entry.astype(BF16)
-    cumulative = decay_columns(decay_ref)
+    cumulative, decay_in_rows = decay_columns(decay_ref), decay_rows(decay_ref)
     squares = jnp.zeros((TOK, 1), F32)
     inner = jnp.zeros((TOK, 1), F32)
     for h in range(HEADS):
         cols = head_cols(h)
         q = q_ref[:, cols]
-        scores = inner_terms(q, k_ref[:, cols], decay_ref, cumulative, h)[1]
+        scores = inner_terms(q, k_ref[:, cols], decay_in_rows, cumulative, h)[1]
         carried = dot(q, entry_ref[:, cols], 1, 0)
         raw = dot(scores, v_ref[:, cols], 1, 0) + jnp.exp(cumulative[:, h : h + 1]) * carried
         raw_ref[:, cols] = raw
@@ -503,7 +515,7 @@
     q_ref, k_ref, v_ref, g_ref, decay_ref, entry_ref, raw_ref, sum_0, sum_1, sum_2, sum_3,
     out_ref, dq_ref, dk_ref, dv_ref, read_ref,
 ):
-    cumulative = decay_columns(decay_ref)
+    cumulative, decay_in_rows = decay_columns(decay_ref), decay_rows(decay_ref)
     sums = (sum_0[...] + sum_1[...]) + (sum_2[...] + sum_3[...])
     sums = jnp.concatenate([sums] * (HEAD_DIM // 8), axis=0).T
     inverse = 1.0 / jnp.sqrt(sums[:, 0:1] * (1.0 / (HEAD_TOTAL * HEAD_DIM)) + EPS)
@@ -514,7 +526,7 @@
         out = raw_ref[:, cols] * inverse
         out_ref[:, cols] = out
         raw_grad = ((g_ref[:, cols].astype(F32) - out * aligned) * inverse).astype(BF16)
-        decay, scores = inner_terms(q, k, decay_ref, cumulative, h)
+        decay, scores = inner_terms(q, k, decay_in_rows, cumulative, h)
         head_decay = jnp.exp(cumulative[:, h : h + 1])
         inner_grad = (dot(raw_grad, v_ref[:, cols], 1, 1) * decay).astype(BF16)
         carried = dot(raw_grad, entry_ref[:, cols], 1, 1)
@@ -538,7 +550,7 @@
     ]
     keys = chain_keys(group_ref, index_ref, 0, False)
     handed, part, prefix = line_sums(keys, logs, states)
-    handed_ref[...] = handed
+    handed_ref[...] = handed.astype(BF16)
     part_ref[pl.ds(0, HEAD_DIM)] = part
     part_ref[pl.ds(HEAD_DIM, 8)] = jnp.broadcast_to(prefix, (8, WIDTH))
 
@@ -580,7 +592,6 @@
         shaped(PACK_ROWS, WIDTH, dtype=BF16),
         2**26,
         (soft_grad, lin_key, lin_value, decay),
-        vmem=60,
     )
     q_from = {0: soft_query, **{o: fetch(soft_query, "y", NY, o) for o in OFFSETS}}
     g_from = {0: packed, **{o: fetch(packed, "y", NY, o) for o in OFFSETS}}
@@ -592,7 +603,11 @@
     out_a, stat_a = soft_forward(place, 0, qa, kvs)
     handed, entry_part, logs = call(
         states_kernel,
-        [shaped(HEAD_DIM + 8, WIDTH), shaped(HEAD_DIM + 8, WIDTH), shaped(8, WIDTH)],
+        [
+            shaped(HEAD_DIM + 16, WIDTH, dtype=BF16),
+            shaped(HEAD_DIM + 8, WIDTH),
+            shaped(8, WIDTH),
+        ],
         2**24,
         (*place, ga, gb),
         **placed(in_vmem(2), in_vmem(3)),
@@ -654,7 +669,7 @@
 
     back_handed, leave_part = call(
         back_kernel,
-        [shaped(HEAD_DIM, WIDTH), shaped(HEAD_DIM + 8, WIDTH)],
+        [shaped(HEAD_DIM, WIDTH, dtype=BF16), shaped(HEAD_DIM + 8, WIDTH)],
         2**24,
         (*place, logs, read_grad, from_core, *(sent_out[NY - o] for o in (1, 2, 3))),
         **placed(in_vmem(6), in_vmem(2)),

time: 193 us -> 189 us (0.979)
  local copies, waits for them, and re-layouts: 1.02 us -> 5.08 us
  waiting for transfers between devices: 82.4 us -> 78.4 us
  Pallas kernels: 52 us -> 49.3 us
    unnamed x18 -> x26, local copies, waits for them, and re-layouts: 0.05 us -> 4.11 us
    ppermute x35, waiting for transfers between devices: 82.4 us -> 78.4 us  [send(): lax.ppermute(block, axis, [(i, (i + offset) % size) for i in range(size)])]
    pallas_call x15, Pallas kernels: 52 us -> 49.3 us  [call(): pl.pallas_call(kernel, out_shape=out_shape, cost_estimate=pl.CostEstimate...]
  transfers between devices with their start and end apart: 35 -> 35, of which waited for: 20 -> 21; matrix products, arithmetic and copies ran while one was open for 2% -> 2% of each run, Pallas kernels for 12% -> 11%
where the time goes in v2:
time: 189 us
  waiting for transfers between devices  78.4 us (41%)
  starting transfers between devices  52 us (28%)
  Pallas kernels  49.3 us (26%)
  local copies, waits for them, and re-layouts  5.08 us (3%)
  other arithmetic  3.06 us (2%)
    ppermute x35, waiting for transfers between devices, send(): lax.ppermute(block, axis, [(i, (i + offset) % size) for i in range(size)])  78.4 us
    ppermute x35, starting transfers between devices, send(): lax.ppermute(block, axis, [(i, (i + offset) % size) for i in range(size)])  52 us
    pallas_call x15, Pallas kernels, call(): pl.pallas_call(kernel, out_shape=out_shape, cost_estimate=pl.CostEstimate...  49.3 us
    unnamed x26, local copies, waits for them, and re-layouts  4.11 us
  transfers between devices with their start and end apart: 35, of which 21 were waited for; matrix products, arithmetic and copies ran while one was open for 2% of the time, Pallas kernels for 11%

profile of v2, /device:TPU:8, one launch (start us, length us, event | category | flops | bytes accessed | tf_op | source)
XLA Modules:
  0.0 188.7 jit_solution(4331191602904334887)
XLA Ops:
  4.9 1.6 collective-permute-start.2
  7.4 2.5 %collective-permute-start = (bf16[400,384]{1,0:T(8,128)(2,1)S(1)}, bf16[400,384]{1,0:T(8,128)(2,1)S(1)}, u32[]{:S(2)}, u32[]{:S(2)}) collective-permute-start(bf16[400,384]{1,0:T(8,128)(2,1)S(1)} %shard_map.161), channel_id=1, source_target_pairs={{0,24},{8,0},{16,8},{24,16},{1,25},{9,1},{17,9},{25,17},{2,26},{10... | collective-permute-start | bytes 921608 | tf_op jit(solution)/shard_map/ppermute | solution.py:35
  9.9 5.2 %collective-permute-done.2 = bf16[400,384]{1,0:T(8,128)(2,1)S(1)} collective-permute-done((bf16[400,384]{1,0:T(8,128)(2,1)S(1)}, bf16[400,384]{1,0:T(8,128)(2,1)S(1)}, u32[]{:S(2)}, u32[]{:S(2)}) %collective-permute-start.2) | collective-permute-done | bytes 307232 | tf_op jit(solution)/shard_map/ppermute | solution.py:35
  15.1 3.1 %collective-permute-done.1 = bf16[400,384]{1,0:T(8,128)(2,1)S(1)} collective-permute-done((bf16[400,384]{1,0:T(8,128)(2,1)S(1)}, bf16[400,384]{1,0:T(8,128)(2,1)S(1)}, u32[]{:S(2)}, u32[]{:S(2)}) %collective-permute-start.1) | collective-permute-done | bytes 307232 | tf_op jit(solution)/shard_map/ppermute | solution.py:35
  18.2 4.5 %collective-permute-done = bf16[400,384]{1,0:T(8,128)(2,1)S(1)} collective-permute-done((bf16[400,384]{1,0:T(8,128)(2,1)S(1)}, bf16[400,384]{1,0:T(8,128)(2,1)S(1)}, u32[]{:S(2)}, u32[]{:S(2)}) %collective-permute-start) | collective-permute-done | bytes 307232 | tf_op jit(solution)/shard_map/ppermute | solution.py:35
  25.6 3.0 %collective-permute-start.5 = (bf16[256,384]{1,0:T(8,128)(2,1)S(1)}, bf16[256,384]{1,0:T(8,128)(2,1)S(1)}, u32[]{:S(2)}, u32[]{:S(2)}) collective-permute-start(bf16[256,384]{1,0:T(8,128)(2,1)S(1)} %copy-done.10), channel_id=1, source_target_pairs={{0,16},{8,24},{16,0},{24,8},{1,17},{9,25},{17,1},{25,9},{2,18},{10... | collective-permute-start | bytes 589832 | tf_op jit(solution)/shard_map/ppermute | solution.py:35
  28.6 2.0 %collective-permute-done.4 = bf16[256,384]{1,0:T(8,128)(2,1)S(1)} collective-permute-done((bf16[256,384]{1,0:T(8,128)(2,1)S(1)}, bf16[256,384]{1,0:T(8,128)(2,1)S(1)}, u32[]{:S(2)}, u32[]{:S(2)}) %collective-permute-start.4) | collective-permute-done | bytes 196640 | tf_op jit(solution)/shard_map/ppermute | solution.py:35
  30.6 1.7 collective-permute-done.6
  32.3 3.0 %collective-permute-done.5 = bf16[256,384]{1,0:T(8,128)(2,1)S(1)} collective-permute-done((bf16[256,384]{1,0:T(8,128)(2,1)S(1)}, bf16[256,384]{1,0:T(8,128)(2,1)S(1)}, u32[]{:S(2)}, u32[]{:S(2)}) %collective-permute-start.5) | collective-permute-done | bytes 196640 | tf_op jit(solution)/shard_map/ppermute | solution.py:35
  36.3 1.5 collective-permute-start.9
  37.8 2.7 %collective-permute-start.8 = (bf16[2,256,384]{2,1,0:T(8,128)(2,1)}, bf16[2,256,384]{2,1,0:T(8,128)(2,1)}, u32[]{:S(2)}, u32[]{:S(2)}) collective-permute-start(bf16[2,256,384]{2,1,0:T(8,128)(2,1)} %pad_maximum_fusion.2.kv_0.kv_ref), channel_id=1, source_target_pairs={{0,64},{32,96},{64,0},{96,32},{1,65},{33,97},{65,1},{97,33},{2,66}... | collective-permute-start | bytes 1179656 | tf_op jit(solution)/shard_map/ppermute | solution.py:35
  40.5 1.4 collective-permute-start.7
  42.0 7.4 %collective-permute-done.9.kv_3 = bf16[2,256,384]{2,1,0:T(8,128)(2,1)} collective-permute-done((bf16[2,256,384]{2,1,0:T(8,128)(2,1)}, bf16[2,256,384]{2,1,0:T(8,128)(2,1)}, u32[]{:S(2)}, u32[]{:S(2)}) %collective-permute-start.9) | collective-permute-done | bytes 393248 | tf_op jit(solution)/shard_map/ppermute | solution.py:35
  49.3 9.4 %collective-permute-done.8.kv_2 = bf16[2,256,384]{2,1,0:T(8,128)(2,1)} collective-permute-done((bf16[2,256,384]{2,1,0:T(8,128)(2,1)}, bf16[2,256,384]{2,1,0:T(8,128)(2,1)}, u32[]{:S(2)}, u32[]{:S(2)}) %collective-permute-start.8) | collective-permute-done | bytes 393248 | tf_op jit(solution)/shard_map/ppermute | solution.py:35
  58.8 7.4 %shard_map.162 = (bf16[4,256,384]{2,1,0:T(8,128)(2,1)S(1)}, f32[4,8,256]{2,1,0:T(8,128)S(1)}) custom-call(s32[32]{0:T(128)S(1)} %copy-done.9, s32[1]{0:T(128)} %bitcast.5.index_ref, bf16[4,256,384]{2,1,0:T(8,128)(2,1)S(1)} %pad_maximum_fusion.1.q_ref.qa_ref, bf16[2,256,384]{2,1,0:T(8,128)(2,1)} %pad_maximum_fusion.2.kv_0.kv_ref, ...), custom_call_target="tpu_custom_call" | custom-call | flops 1610612736 | bytes 2097152 | tf_op jit(solution)/shard_map/pallas_call | solution.py:57
  67.2 1.4 collective-permute-start.17
  68.6 2.4 %collective-permute-start.16 = (bf16[144,384]{1,0:T(8,128)(2,1)S(1)}, bf16[144,384]{1,0:T(8,128)(2,1)S(1)}, u32[]{:S(2)}, u32[]{:S(2)}) collective-permute-start(bf16[144,384]{1,0:T(8,128)(2,1)S(1)} %get-tuple-element.49.own), channel_id=1, source_target_pairs={{0,64},{32,96},{64,0},{96,32},{1,65},{33,97},{65,1},{97,33},{2,66}... | collective-permute-start | bytes 331784 | tf_op jit(solution)/shard_map/ppermute | solution.py:35
  71.0 1.6 collective-permute-start.15
  72.6 7.4 %shard_map.163 = (bf16[4,256,384]{2,1,0:T(8,128)(2,1)S(1)}, f32[4,8,256]{2,1,0:T(8,128)S(1)}) custom-call(s32[32]{0:T(128)S(1)} %copy-done.9, s32[1]{0:T(128)} %bitcast.5.index_ref, bf16[4,256,384]{2,1,0:T(8,128)(2,1)} %collective-permute-done.10.q_ref.qb_ref, bf16[2,256,384]{2,1,0:T(8,128)(2,1)} %pad_maximum_fusion.2.kv_0.kv_ref, ...), custom_call_target="tpu_custom_call" | custom-call | flops 1610612736 | bytes 2097152 | tf_op jit(solution)/shard_map/pallas_call | solution.py:57
  80.0 1.7 shard_map.164.part_ref
  81.8 1.2 collective-permute-done.11.other_ref
  83.1 1.8 collective-permute-start.14
  85.0 3.6 %collective-permute-start.13 = (f32[2,4,8,256]{3,2,1,0:T(8,128)S(1)}, f32[2,4,8,256]{3,2,1,0:T(8,128)S(1)}, u32[]{:S(2)}, u32[]{:S(2)}) collective-permute-start(f32[2,4,8,256]{3,2,1,0:T(8,128)S(1)} %shard_map.165.chip_ref), channel_id=1, source_target_pairs={{0,16},{8,24},{16,0},{24,8},{1,17},{9,25},{17,1},{25,9},{2,18},{10... | collective-permute-start | bytes 196616 | tf_op jit(solution)/shard_map/ppermute | solution.py:35
  88.6 1.7 shard_map.167
  90.3 2.0 %collective-permute-start.20 = (f32[8,256]{1,0:T(8,128)S(1)}, f32[8,256]{1,0:T(8,128)S(1)}, u32[]{:S(2)}, u32[]{:S(2)}) collective-permute-start(f32[8,256]{1,0:T(8,128)S(1)} %get-tuple-element.52.sum_0), channel_id=1, source_target_pairs={{0,1},{1,2},{2,3},{3,0},{4,5},{5,6},{6,7},{7,4},{8,9},{9,10},{10,1... | collective-permute-start | bytes 24584 | tf_op jit(solution)/shard_map/ppermute | solution.py:35
  92.3 3.6 %collective-permute-start.19 = (f32[8,256]{1,0:T(8,128)S(1)}, f32[8,256]{1,0:T(8,128)S(1)}, u32[]{:S(2)}, u32[]{:S(2)}) collective-permute-start(f32[8,256]{1,0:T(8,128)S(1)} %get-tuple-element.52.sum_0), channel_id=1, source_target_pairs={{0,2},{1,3},{2,0},{3,1},{4,6},{5,7},{6,4},{7,5},{8,10},{9,11},{10,... | collective-permute-start | bytes 24584 | tf_op jit(solution)/shard_map/ppermute | solution.py:35
  96.0 2.0 %collective-permute-start.18 = (f32[8,256]{1,0:T(8,128)S(1)}, f32[8,256]{1,0:T(8,128)S(1)}, u32[]{:S(2)}, u32[]{:S(2)}) collective-permute-start(f32[8,256]{1,0:T(8,128)S(1)} %get-tuple-element.52.sum_0), channel_id=1, source_target_pairs={{0,3},{1,0},{2,1},{3,2},{4,7},{5,4},{6,5},{7,6},{8,11},{9,8},{10,9... | collective-permute-start | bytes 24584 | tf_op jit(solution)/shard_map/ppermute | solution.py:35
  98.0 1.6 collective-permute-done.18.sum_1
  99.7 2.2 %shard_map.168 = (f32[256,384]{1,0:T(8,128)}, f32[256,384]{1,0:T(8,128)}, f32[256,384]{1,0:T(8,128)S(1)}, f32[256,384]{1,0:T(8,128)S(1)}, bf16[128,384]{1,0:T(8,128)(2,1)S(1)}) custom-call(bf16[256,384]{1,0:T(8,128)(2,1)S(1)} %copy-done.4, bf16[256,384]{1,0:T(8,128)(2,1)S(1)} %copy-done.1, bf16[256,384]{1,0:T(8,128)(2,1)S(1)} %copy-done.3, ...), custom_call_target="tpu_custom_call" | custom-call | flops 268435456 | bytes 2097152 | tf_op jit(solution)/shard_map/pallas_call | solution.py:57
  101.8 1.3 shard_map.169
  103.1 5.7 %shard_map.171 = (f32[4,3,128,256]{3,2,1,0:T(8,128)S(1)}, f32[4,3,128,256]{3,2,1,0:T(8,128)S(1)}, bf16[3,2,256,384]{3,2,1,0:T(8,128)(2,1)S(1)}) custom-call(s32[32]{0:T(128)S(1)} %copy-done.9, s32[1]{0:T(128)} %bitcast.5.index_ref, bf16[4,256,384]{2,1,0:T(8,128)(2,1)S(1)} %pad_maximum_fusion.1.q_ref.qa_ref, ...), custom_call_target="tpu_custom_call" | custom-call | flops 2013265920 | bytes 2097152 | tf_op jit(solution)/shard_map/pallas_call | solution.py:57
  108.8 10.1 %shard_map.172 = (f32[4,3,128,256]{3,2,1,0:T(8,128)S(1)}, f32[4,3,128,256]{3,2,1,0:T(8,128)S(1)}, bf16[3,2,256,384]{3,2,1,0:T(8,128)(2,1)S(1)}) custom-call(s32[32]{0:T(128)S(1)} %copy-done.9, s32[1]{0:T(128)} %bitcast.5.index_ref, ...), custom_call_target="tpu_custom_call", output_to_operand_aliasing={{0}: (10, {}), {1}: (11, {}), {2}: (12, {})} | custom-call | flops 4026531840 | bytes 2097152 | tf_op jit(solution)/shard_map/pallas_call | solution.py:57
  118.9 6.7 %shard_map.173 = (bf16[4,256,384]{2,1,0:T(8,128)(2,1)S(1)}, bf16[4,256,384]{2,1,0:T(8,128)(2,1)S(1)}, f32[2,256,384]{2,1,0:T(8,128)S(1)}) custom-call(s32[32]{0:T(128)S(1)} %copy-done.9, s32[1]{0:T(128)} %bitcast.5.index_ref, bf16[4,256,384]{2,1,0:T(8,128)(2,1)S(1)} %pad_maximum_fusion.1.q_ref.qa_ref, ...), custom_call_target="tpu_custom_call" | custom-call | flops 2013265920 | bytes 2097152 | tf_op jit(solution)/shard_map/pallas_call | solution.py:57
  128.0 1.9 %collective-permute-start.30 = (bf16[2,256,384]{2,1,0:T(8,128)(2,1)S(1)}, bf16[2,256,384]{2,1,0:T(8,128)(2,1)S(1)}, u32[]{:S(2)}, u32[]{:S(2)}) collective-permute-start(bf16[2,256,384]{2,1,0:T(8,128)(2,1)S(1)} %get-tuple-element.84), channel_id=1, source_target_pairs={{0,96},{32,0},{64,32},{96,64},{1,97},{33,1},{65,33},{97,65},{2,98}... | collective-permute-start | bytes 1179656 | tf_op jit(solution)/shard_map/ppermute | solution.py:35
  130.2 2.1 %collective-permute-start.26 = (bf16[256,384]{1,0:T(8,128)(2,1)S(1)}, bf16[256,384]{1,0:T(8,128)(2,1)S(1)}, u32[]{:S(2)}, u32[]{:S(2)}) collective-permute-start(bf16[256,384]{1,0:T(8,128)(2,1)S(1)} %get-tuple-element.85), channel_id=1, source_target_pairs={{0,8},{8,16},{16,24},{24,0},{1,9},{9,17},{17,25},{25,1},{2,10},{10... | collective-permute-start | bytes 589832 | tf_op jit(solution)/shard_map/ppermute | solution.py:35
  132.3 14.9 %collective-permute-done.29 = bf16[2,256,384]{2,1,0:T(8,128)(2,1)S(1)} collective-permute-done((bf16[2,256,384]{2,1,0:T(8,128)(2,1)S(1)}, bf16[2,256,384]{2,1,0:T(8,128)(2,1)S(1)}, u32[]{:S(2)}, u32[]{:S(2)}) %collective-permute-start.29) | collective-permute-done | bytes 393248 | tf_op jit(solution)/shard_map/ppermute | solution.py:35
  149.0 3.1 %collective-permute-start.27 = (bf16[256,384]{1,0:T(8,128)(2,1)S(1)}, bf16[256,384]{1,0:T(8,128)(2,1)S(1)}, u32[]{:S(2)}, u32[]{:S(2)}) collective-permute-start(bf16[256,384]{1,0:T(8,128)(2,1)S(1)} %get-tuple-element.87), channel_id=1, source_target_pairs={{0,24},{8,0},{16,8},{24,16},{1,25},{9,1},{17,9},{25,17},{2,26},{10... | collective-permute-start | bytes 589832 | tf_op jit(solution)/shard_map/ppermute | solution.py:35
  152.5 2.0 %collective-permute-start.23 = (bf16[512,384]{1,0:T(8,128)(2,1)S(1)}, bf16[512,384]{1,0:T(8,128)(2,1)S(1)}, u32[]{:S(2)}, u32[]{:S(2)}) collective-permute-start(bf16[512,384]{1,0:T(8,128)(2,1)S(1)} %get-tuple-element.58), channel_id=1, source_target_pairs={{0,24},{8,0},{16,8},{24,16},{1,25},{9,1},{17,9},{25,17},{2,26},{10... | collective-permute-start | bytes 1179656 | tf_op jit(solution)/shard_map/ppermute | solution.py:35
  156.0 1.4 collective-permute-done.28
  157.4 2.3 %collective-permute-done.27 = bf16[256,384]{1,0:T(8,128)(2,1)S(1)} collective-permute-done((bf16[256,384]{1,0:T(8,128)(2,1)S(1)}, bf16[256,384]{1,0:T(8,128)(2,1)S(1)}, u32[]{:S(2)}, u32[]{:S(2)}) %collective-permute-start.27) | collective-permute-done | bytes 196640 | tf_op jit(solution)/shard_map/ppermute | solution.py:35
  160.5 5.9 %collective-permute-done.22.from_3 = bf16[512,384]{1,0:T(8,128)(2,1)S(1)} collective-permute-done((bf16[512,384]{1,0:T(8,128)(2,1)S(1)}, bf16[512,384]{1,0:T(8,128)(2,1)S(1)}, u32[]{:S(2)}, u32[]{:S(2)}) %collective-permute-start.22) | collective-permute-done | bytes 393248 | tf_op jit(solution)/shard_map/ppermute | solution.py:35
  166.4 1.9 %collective-permute-done.23.from_1 = bf16[512,384]{1,0:T(8,128)(2,1)S(1)} collective-permute-done((bf16[512,384]{1,0:T(8,128)(2,1)S(1)}, bf16[512,384]{1,0:T(8,128)(2,1)S(1)}, u32[]{:S(2)}, u32[]{:S(2)}) %collective-permute-start.23) | collective-permute-done | bytes 393248 | tf_op jit(solution)/shard_map/ppermute | solution.py:35
  168.2 8.3 %collective-permute-done.24.from_2 = bf16[512,384]{1,0:T(8,128)(2,1)S(1)} collective-permute-done((bf16[512,384]{1,0:T(8,128)(2,1)S(1)}, bf16[512,384]{1,0:T(8,128)(2,1)S(1)}, u32[]{:S(2)}, u32[]{:S(2)}) %collective-permute-start.24) | collective-permute-done | bytes 393248 | tf_op jit(solution)/shard_map/ppermute | solution.py:35
  177.5 1.3 collective-permute-start.34
  178.8 3.3 %collective-permute-start.33 = (bf16[128,384]{1,0:T(8,128)(2,1)S(1)}, bf16[128,384]{1,0:T(8,128)(2,1)S(1)}, u32[]{:S(2)}, u32[]{:S(2)}) collective-permute-start(bf16[128,384]{1,0:T(8,128)(2,1)S(1)} %get-tuple-element.75.own), channel_id=1, source_target_pairs={{0,64},{32,96},{64,0},{96,32},{1,65},{33,97},{65,1},{97,33},{2,66}... | collective-permute-start | bytes 294920 | tf_op jit(solution)/shard_map/ppermute | solution.py:35
  182.9 1.6 collective-permute-done.34.from_3
  184.4 1.4 collective-permute-done.33.from_2
  186.7 2.0 %shard_map.175 = (f32[256,384]{1,0:T(8,128)}, f32[256,384]{1,0:T(8,128)}) custom-call(s32[32]{0:T(128)S(1)} %copy-done.9, s32[1]{0:T(128)} %bitcast.5.index_ref, bf16[256,384]{1,0:T(8,128)(2,1)S(1)} %copy-done.1, bf16[256,384]{1,0:T(8,128)(2,1)S(1)} %copy-done.3, f32[3,256]{1,0:T(4,128)S(1)} %bitcast.42, f32[136,384]{1,0:T(8,128)S(1)} %get-tuple-element.73.part_ref, ...), custom_call_target="tpu_custom_call" | custom-call | flops 67108864 | bytes 2097152 | tf_op jit(solution)/shard_map/pallas_call | solution.py:57
  (73 shorter events, 20.1 us)
Async XLA Ops:
  0.6 0.9 copy-start
  1.6 0.9 copy-start.2
  2.5 0.9 copy-start.6
  3.4 0.7 copy-start.7
  4.9 10.2 %collective-permute-start.2 = (bf16[400,384]{1,0:T(8,128)(2,1)S(1)}, bf16[400,384]{1,0:T(8,128)(2,1)S(1)}, u32[]{:S(2)}, u32[]{:S(2)}) collective-permute-start(bf16[400,384]{1,0:T(8,128)(2,1)S(1)} %shard_map.161), channel_id=1, source_target_pairs={{0,8},{8,16},{16,24},{24,0},{1,9},{9,17},{17,25},{25,1},{2,10},{10... | collective-permute-start | bytes 921608 | tf_op jit(solution)/shard_map/ppermute | solution.py:35
  6.6 11.6 %collective-permute-start.1 = (bf16[400,384]{1,0:T(8,128)(2,1)S(1)}, bf16[400,384]{1,0:T(8,128)(2,1)S(1)}, u32[]{:S(2)}, u32[]{:S(2)}) collective-permute-start(bf16[400,384]{1,0:T(8,128)(2,1)S(1)} %shard_map.161), channel_id=1, source_target_pairs={{0,16},{8,24},{16,0},{24,8},{1,17},{9,25},{17,1},{25,9},{2,18},{10... | collective-permute-start | bytes 921608 | tf_op jit(solution)/shard_map/ppermute | solution.py:35
  7.4 15.3 %collective-permute-start = (bf16[400,384]{1,0:T(8,128)(2,1)S(1)}, bf16[400,384]{1,0:T(8,128)(2,1)S(1)}, u32[]{:S(2)}, u32[]{:S(2)}) collective-permute-start(bf16[400,384]{1,0:T(8,128)(2,1)S(1)} %shard_map.161), channel_id=1, source_target_pairs={{0,24},{8,0},{16,8},{24,16},{1,25},{9,1},{17,9},{25,17},{2,26},{10... | collective-permute-start | bytes 921608 | tf_op jit(solution)/shard_map/ppermute | solution.py:35
  22.7 0.9 copy-start.10
  22.9 12.6 %copy-start.11 = (bf16[256,384]{1,0:T(8,128)(2,1)S(1)}, bf16[256,384]{1,0:T(8,128)(2,1)}, u32[]{:S(2)}) copy-start(bf16[256,384]{1,0:T(8,128)(2,1)} %param.13) | copy-start | bytes 589828
  22.9 12.6 %copy-start.12 = (bf16[256,384]{1,0:T(8,128)(2,1)S(1)}, bf16[256,384]{1,0:T(8,128)(2,1)}, u32[]{:S(2)}) copy-start(bf16[256,384]{1,0:T(8,128)(2,1)} %param.12) | copy-start | bytes 589828
  22.9 35.8 %copy-start.9 = (s32[32]{0:T(128)S(1)}, s32[32]{0:T(128)}, u32[]{:S(2)}) copy-start(s32[32]{0:T(128)} %group_ref.17) | copy-start | bytes 388
  22.9 43.3 %collective-permute-start.3 = (bf16[4,400,384]{2,1,0:T(8,128)(2,1)S(1)}, bf16[4,400,384]{2,1,0:T(8,128)(2,1)S(1)}, u32[]{:S(2)}, u32[]{:S(2)}) collective-permute-start(bf16[4,400,384]{2,1,0:T(8,128)(2,1)S(1)} %pad_maximum_fusion.g_a.ga_ref), channel_id=1, source_target_pairs={{0,4},{4,0},{1,5},{5,1},{2,6},{6,2},{3,7},{7,3},{8,12},{12,8},{9,1... | collective-permute-start | bytes 3686408 | tf_op jit(solution)/shard_map/ppermute | solution.py:35
  23.6 7.0 %collective-permute-start.4 = (bf16[256,384]{1,0:T(8,128)(2,1)S(1)}, bf16[256,384]{1,0:T(8,128)(2,1)S(1)}, u32[]{:S(2)}, u32[]{:S(2)}) collective-permute-start(bf16[256,384]{1,0:T(8,128)(2,1)S(1)} %copy-done.10), channel_id=1, source_target_pairs={{0,24},{8,0},{16,8},{24,16},{1,25},{9,1},{17,9},{25,17},{2,26},{10... | collective-permute-start | bytes 589832 | tf_op jit(solution)/shard_map/ppermute | solution.py:35
  24.4 7.9 %collective-permute-start.6 = (bf16[256,384]{1,0:T(8,128)(2,1)S(1)}, bf16[256,384]{1,0:T(8,128)(2,1)S(1)}, u32[]{:S(2)}, u32[]{:S(2)}) collective-permute-start(bf16[256,384]{1,0:T(8,128)(2,1)S(1)} %copy-done.10), channel_id=1, source_target_pairs={{0,8},{8,16},{16,24},{24,0},{1,9},{9,17},{17,25},{25,1},{2,10},{10... | collective-permute-start | bytes 589832 | tf_op jit(solution)/shard_map/ppermute | solution.py:35
  25.6 9.6 %collective-permute-start.5 = (bf16[256,384]{1,0:T(8,128)(2,1)S(1)}, bf16[256,384]{1,0:T(8,128)(2,1)S(1)}, u32[]{:S(2)}, u32[]{:S(2)}) collective-permute-start(bf16[256,384]{1,0:T(8,128)(2,1)S(1)} %copy-done.10), channel_id=1, source_target_pairs={{0,16},{8,24},{16,0},{24,8},{1,17},{9,25},{17,1},{25,9},{2,18},{10... | collective-permute-start | bytes 589832 | tf_op jit(solution)/shard_map/ppermute | solution.py:35
  35.4 37.2 %collective-permute-start.10 = (bf16[4,256,384]{2,1,0:T(8,128)(2,1)S(1)}, bf16[4,256,384]{2,1,0:T(8,128)(2,1)}, u32[]{:S(2)}, u32[]{:S(2)}) collective-permute-start(bf16[4,256,384]{2,1,0:T(8,128)(2,1)S(1)} %pad_maximum_fusion.1.q_ref.qa_ref), channel_id=1, source_target_pairs={{0,4},{4,0},{1,5},{5,1},{2,6},{6,2},{3,7},{7,3},{8,12},{12,8},{9,1... | collective-permute-start | bytes 2359304 | tf_op jit(solution)/shard_map/ppermute | solution.py:35
  36.3 13.0 %collective-permute-start.9 = (bf16[2,256,384]{2,1,0:T(8,128)(2,1)}, bf16[2,256,384]{2,1,0:T(8,128)(2,1)}, u32[]{:S(2)}, u32[]{:S(2)}) collective-permute-start(bf16[2,256,384]{2,1,0:T(8,128)(2,1)} %pad_maximum_fusion.2.kv_0.kv_ref), channel_id=1, source_target_pairs={{0,32},{32,64},{64,96},{96,0},{1,33},{33,65},{65,97},{97,1},{2,34}... | collective-permute-start | bytes 1179656 | tf_op jit(solution)/shard_map/ppermute | solution.py:35
  37.8 20.9 %collective-permute-start.8 = (bf16[2,256,384]{2,1,0:T(8,128)(2,1)}, bf16[2,256,384]{2,1,0:T(8,128)(2,1)}, u32[]{:S(2)}, u32[]{:S(2)}) collective-permute-start(bf16[2,256,384]{2,1,0:T(8,128)(2,1)} %pad_maximum_fusion.2.kv_0.kv_ref), channel_id=1, source_target_pairs={{0,64},{32,96},{64,0},{96,32},{1,65},{33,97},{65,1},{97,33},{2,66}... | collective-permute-start | bytes 1179656 | tf_op jit(solution)/shard_map/ppermute | solution.py:35
  40.5 18.2 %collective-permute-start.7 = (bf16[2,256,384]{2,1,0:T(8,128)(2,1)}, bf16[2,256,384]{2,1,0:T(8,128)(2,1)}, u32[]{:S(2)}, u32[]{:S(2)}) collective-permute-start(bf16[2,256,384]{2,1,0:T(8,128)(2,1)} %pad_maximum_fusion.2.kv_0.kv_ref), channel_id=1, source_target_pairs={{0,96},{32,0},{64,32},{96,64},{1,97},{33,1},{65,33},{97,65},{2,98}... | collective-permute-start | bytes 1179656 | tf_op jit(solution)/shard_map/ppermute | solution.py:35
  67.2 21.3 %collective-permute-start.17 = (bf16[144,384]{1,0:T(8,128)(2,1)S(1)}, bf16[144,384]{1,0:T(8,128)(2,1)S(1)}, u32[]{:S(2)}, u32[]{:S(2)}) collective-permute-start(bf16[144,384]{1,0:T(8,128)(2,1)S(1)} %get-tuple-element.49.own), channel_id=1, source_target_pairs={{0,32},{32,64},{64,96},{96,0},{1,33},{33,65},{65,97},{97,1},{2,34}... | collective-permute-start | bytes 331784 | tf_op jit(solution)/shard_map/ppermute | solution.py:35
  68.6 19.9 %collective-permute-start.16 = (bf16[144,384]{1,0:T(8,128)(2,1)S(1)}, bf16[144,384]{1,0:T(8,128)(2,1)S(1)}, u32[]{:S(2)}, u32[]{:S(2)}) collective-permute-start(bf16[144,384]{1,0:T(8,128)(2,1)S(1)} %get-tuple-element.49.own), channel_id=1, source_target_pairs={{0,64},{32,96},{64,0},{96,32},{1,65},{33,97},{65,1},{97,33},{2,66}... | collective-permute-start | bytes 331784 | tf_op jit(solution)/shard_map/ppermute | solution.py:35
  71.0 17.5 %collective-permute-start.15 = (bf16[144,384]{1,0:T(8,128)(2,1)S(1)}, bf16[144,384]{1,0:T(8,128)(2,1)S(1)}, u32[]{:S(2)}, u32[]{:S(2)}) collective-permute-start(bf16[144,384]{1,0:T(8,128)(2,1)S(1)} %get-tuple-element.49.own), channel_id=1, source_target_pairs={{0,96},{32,0},{64,32},{96,64},{1,97},{33,1},{65,33},{97,65},{2,98}... | collective-permute-start | bytes 331784 | tf_op jit(solution)/shard_map/ppermute | solution.py:35
  80.0 8.5 %copy-start.1 = (bf16[256,384]{1,0:T(8,128)(2,1)S(1)}, bf16[256,384]{1,0:T(8,128)(2,1)}, u32[]{:S(2)}) copy-start(bf16[256,384]{1,0:T(8,128)(2,1)} %k_ref.5) | copy-start | bytes 589828
  80.0 8.5 %copy-start.3 = (bf16[256,384]{1,0:T(8,128)(2,1)S(1)}, bf16[256,384]{1,0:T(8,128)(2,1)}, u32[]{:S(2)}) copy-start(bf16[256,384]{1,0:T(8,128)(2,1)} %v_ref.5) | copy-start | bytes 589828
  80.0 8.5 %copy-start.4 = (bf16[256,384]{1,0:T(8,128)(2,1)S(1)}, bf16[256,384]{1,0:T(8,128)(2,1)}, u32[]{:S(2)}) copy-start(bf16[256,384]{1,0:T(8,128)(2,1)} %q_ref.3) | copy-start | bytes 589828
  80.0 8.5 %copy-start.5 = (bf16[256,384]{1,0:T(8,128)(2,1)S(1)}, bf16[256,384]{1,0:T(8,128)(2,1)}, u32[]{:S(2)}) copy-start(bf16[256,384]{1,0:T(8,128)(2,1)} %g_ref.5) | copy-start | bytes 589828
  80.0 8.5 %copy-start.8 = (f32[256,3]{0,1:T(4,128)S(1)}, f32[256,3]{0,1:T(4,128)}, u32[]{:S(2)}) copy-start(f32[256,3]{0,1:T(4,128)} %param.18) | copy-start | bytes 9220
  81.7 1.3 collective-permute-start.11
  83.1 18.7 %collective-permute-start.14 = (f32[2,4,8,256]{3,2,1,0:T(8,128)S(1)}, f32[2,4,8,256]{3,2,1,0:T(8,128)S(1)}, u32[]{:S(2)}, u32[]{:S(2)}) collective-permute-start(f32[2,4,8,256]{3,2,1,0:T(8,128)S(1)} %shard_map.165.chip_ref), channel_id=1, source_target_pairs={{0,8},{8,16},{16,24},{24,0},{1,9},{9,17},{17,25},{25,1},{2,10},{10... | collective-permute-start | bytes 196616 | tf_op jit(solution)/shard_map/ppermute | solution.py:35
  85.0 16.9 %collective-permute-start.13 = (f32[2,4,8,256]{3,2,1,0:T(8,128)S(1)}, f32[2,4,8,256]{3,2,1,0:T(8,128)S(1)}, u32[]{:S(2)}, u32[]{:S(2)}) collective-permute-start(f32[2,4,8,256]{3,2,1,0:T(8,128)S(1)} %shard_map.165.chip_ref), channel_id=1, source_target_pairs={{0,16},{8,24},{16,0},{24,8},{1,17},{9,25},{17,1},{25,9},{2,18},{10... | collective-permute-start | bytes 196616 | tf_op jit(solution)/shard_map/ppermute | solution.py:35
  88.5 13.3 %collective-permute-start.12 = (f32[2,4,8,256]{3,2,1,0:T(8,128)S(1)}, f32[2,4,8,256]{3,2,1,0:T(8,128)S(1)}, u32[]{:S(2)}, u32[]{:S(2)}) collective-permute-start(f32[2,4,8,256]{3,2,1,0:T(8,128)S(1)} %shard_map.165.chip_ref), channel_id=1, source_target_pairs={{0,24},{8,0},{16,8},{24,16},{1,25},{9,1},{17,9},{25,17},{2,26},{10... | collective-permute-start | bytes 196616 | tf_op jit(solution)/shard_map/ppermute | solution.py:35
  90.3 5.7 %collective-permute-start.20 = (f32[8,256]{1,0:T(8,128)S(1)}, f32[8,256]{1,0:T(8,128)S(1)}, u32[]{:S(2)}, u32[]{:S(2)}) collective-permute-start(f32[8,256]{1,0:T(8,128)S(1)} %get-tuple-element.52.sum_0), channel_id=1, source_target_pairs={{0,1},{1,2},{2,3},{3,0},{4,5},{5,6},{6,7},{7,4},{8,9},{9,10},{10,1... | collective-permute-start | bytes 24584 | tf_op jit(solution)/shard_map/ppermute | solution.py:35
  92.3 5.8 %collective-permute-start.19 = (f32[8,256]{1,0:T(8,128)S(1)}, f32[8,256]{1,0:T(8,128)S(1)}, u32[]{:S(2)}, u32[]{:S(2)}) collective-permute-start(f32[8,256]{1,0:T(8,128)S(1)} %get-tuple-element.52.sum_0), channel_id=1, source_target_pairs={{0,2},{1,3},{2,0},{3,1},{4,6},{5,7},{6,4},{7,5},{8,10},{9,11},{10,... | collective-permute-start | bytes 24584 | tf_op jit(solution)/shard_map/ppermute | solution.py:35
  96.0 3.7 %collective-permute-start.18 = (f32[8,256]{1,0:T(8,128)S(1)}, f32[8,256]{1,0:T(8,128)S(1)}, u32[]{:S(2)}, u32[]{:S(2)}) collective-permute-start(f32[8,256]{1,0:T(8,128)S(1)} %get-tuple-element.52.sum_0), channel_id=1, source_target_pairs={{0,3},{1,0},{2,1},{3,2},{4,7},{5,4},{6,5},{7,6},{8,11},{9,8},{10,9... | collective-permute-start | bytes 24584 | tf_op jit(solution)/shard_map/ppermute | solution.py:35
  125.6 4.3 %collective-permute-start.25 = (bf16[4,256,384]{2,1,0:T(8,128)(2,1)S(1)}, bf16[4,256,384]{2,1,0:T(8,128)(2,1)S(1)}, u32[]{:S(2)}, u32[]{:S(2)}) collective-permute-start(bf16[4,256,384]{2,1,0:T(8,128)(2,1)S(1)} %get-tuple-element.67), channel_id=1, source_target_pairs={{0,4},{4,0},{1,5},{5,1},{2,6},{6,2},{3,7},{7,3},{8,12},{12,8},{9,1... | collective-permute-start | bytes 2359304 | tf_op jit(solution)/shard_map/ppermute | solution.py:35
  125.7 26.4 %collective-permute-start.21 = (bf16[1152,384]{1,0:T(8,128)(2,1)S(1)}, bf16[1152,384]{1,0:T(8,128)(2,1)S(1)}, u32[]{:S(2)}, u32[]{:S(2)}) collective-permute-start(bf16[1152,384]{1,0:T(8,128)(2,1)S(1)} %get-tuple-element.55), channel_id=1, source_target_pairs={{0,4},{4,0},{1,5},{5,1},{2,6},{6,2},{3,7},{7,3},{8,12},{12,8},{9,1... | collective-permute-start | bytes 2654216 | tf_op jit(solution)/shard_map/ppermute | solution.py:35
  126.4 20.8 %collective-permute-start.29 = (bf16[2,256,384]{2,1,0:T(8,128)(2,1)S(1)}, bf16[2,256,384]{2,1,0:T(8,128)(2,1)S(1)}, u32[]{:S(2)}, u32[]{:S(2)}) collective-permute-start(bf16[2,256,384]{2,1,0:T(8,128)(2,1)S(1)} %get-tuple-element.82), channel_id=1, source_target_pairs={{0,32},{32,64},{64,96},{96,0},{1,33},{33,65},{65,97},{97,1},{2,34}... | collective-permute-start | bytes 1179656 | tf_op jit(solution)/shard_map/ppermute | solution.py:35
  126.9 20.3 %collective-permute-start.31 = (bf16[2,256,384]{2,1,0:T(8,128)(2,1)S(1)}, bf16[2,256,384]{2,1,0:T(8,128)(2,1)S(1)}, u32[]{:S(2)}, u32[]{:S(2)}) collective-permute-start(bf16[2,256,384]{2,1,0:T(8,128)(2,1)S(1)} %get-tuple-element.83), channel_id=1, source_target_pairs={{0,64},{32,96},{64,0},{96,32},{1,65},{33,97},{65,1},{97,33},{2,66}... | collective-permute-start | bytes 1179656 | tf_op jit(solution)/shard_map/ppermute | solution.py:35
  128.0 19.8 %collective-permute-start.30 = (bf16[2,256,384]{2,1,0:T(8,128)(2,1)S(1)}, bf16[2,256,384]{2,1,0:T(8,128)(2,1)S(1)}, u32[]{:S(2)}, u32[]{:S(2)}) collective-permute-start(bf16[2,256,384]{2,1,0:T(8,128)(2,1)S(1)} %get-tuple-element.84), channel_id=1, source_target_pairs={{0,96},{32,0},{64,32},{96,64},{1,97},{33,1},{65,33},{97,65},{2,98}... | collective-permute-start | bytes 1179656 | tf_op jit(solution)/shard_map/ppermute | solution.py:35
  130.2 24.3 %collective-permute-start.26 = (bf16[256,384]{1,0:T(8,128)(2,1)S(1)}, bf16[256,384]{1,0:T(8,128)(2,1)S(1)}, u32[]{:S(2)}, u32[]{:S(2)}) collective-permute-start(bf16[256,384]{1,0:T(8,128)(2,1)S(1)} %get-tuple-element.85), channel_id=1, source_target_pairs={{0,8},{8,16},{16,24},{24,0},{1,9},{9,17},{17,25},{25,1},{2,10},{10... | collective-permute-start | bytes 589832 | tf_op jit(solution)/shard_map/ppermute | solution.py:35
  148.0 9.4 %collective-permute-start.28 = (bf16[256,384]{1,0:T(8,128)(2,1)S(1)}, bf16[256,384]{1,0:T(8,128)(2,1)S(1)}, u32[]{:S(2)}, u32[]{:S(2)}) collective-permute-start(bf16[256,384]{1,0:T(8,128)(2,1)S(1)} %get-tuple-element.86), channel_id=1, source_target_pairs={{0,16},{8,24},{16,0},{24,8},{1,17},{9,25},{17,1},{25,9},{2,18},{10... | collective-permute-start | bytes 589832 | tf_op jit(solution)/shard_map/ppermute | solution.py:35
  149.0 10.7 %collective-permute-start.27 = (bf16[256,384]{1,0:T(8,128)(2,1)S(1)}, bf16[256,384]{1,0:T(8,128)(2,1)S(1)}, u32[]{:S(2)}, u32[]{:S(2)}) collective-permute-start(bf16[256,384]{1,0:T(8,128)(2,1)S(1)} %get-tuple-element.87), channel_id=1, source_target_pairs={{0,24},{8,0},{16,8},{24,16},{1,25},{9,1},{17,9},{25,17},{2,26},{10... | collective-permute-start | bytes 589832 | tf_op jit(solution)/shard_map/ppermute | solution.py:35
  152.4 13.9 %collective-permute-start.22 = (bf16[512,384]{1,0:T(8,128)(2,1)S(1)}, bf16[512,384]{1,0:T(8,128)(2,1)S(1)}, u32[]{:S(2)}, u32[]{:S(2)}) collective-permute-start(bf16[512,384]{1,0:T(8,128)(2,1)S(1)} %get-tuple-element.57), channel_id=1, source_target_pairs={{0,8},{8,16},{16,24},{24,0},{1,9},{9,17},{17,25},{25,1},{2,10},{10... | collective-permute-start | bytes 1179656 | tf_op jit(solution)/shard_map/ppermute | solution.py:35
  152.5 15.7 %collective-permute-start.23 = (bf16[512,384]{1,0:T(8,128)(2,1)S(1)}, bf16[512,384]{1,0:T(8,128)(2,1)S(1)}, u32[]{:S(2)}, u32[]{:S(2)}) collective-permute-start(bf16[512,384]{1,0:T(8,128)(2,1)S(1)} %get-tuple-element.58), channel_id=1, source_target_pairs={{0,24},{8,0},{16,8},{24,16},{1,25},{9,1},{17,9},{25,17},{2,26},{10... | collective-permute-start | bytes 1179656 | tf_op jit(solution)/shard_map/ppermute | solution.py:35
  154.5 22.0 %collective-permute-start.24 = (bf16[512,384]{1,0:T(8,128)(2,1)S(1)}, bf16[512,384]{1,0:T(8,128)(2,1)S(1)}, u32[]{:S(2)}, u32[]{:S(2)}) collective-permute-start(bf16[512,384]{1,0:T(8,128)(2,1)S(1)} %get-tuple-element.59), channel_id=1, source_target_pairs={{0,16},{8,24},{16,0},{24,8},{1,17},{9,25},{17,1},{25,9},{2,18},{10... | collective-permute-start | bytes 1179656 | tf_op jit(solution)/shard_map/ppermute | solution.py:35
  177.5 6.9 %collective-permute-start.34 = (bf16[128,384]{1,0:T(8,128)(2,1)S(1)}, bf16[128,384]{1,0:T(8,128)(2,1)S(1)}, u32[]{:S(2)}, u32[]{:S(2)}) collective-permute-start(bf16[128,384]{1,0:T(8,128)(2,1)S(1)} %get-tuple-element.75.own), channel_id=1, source_target_pairs={{0,32},{32,64},{64,96},{96,0},{1,33},{33,65},{65,97},{97,1},{2,34}... | collective-permute-start | bytes 294920 | tf_op jit(solution)/shard_map/ppermute | solution.py:35
  178.8 7.0 %collective-permute-start.33 = (bf16[128,384]{1,0:T(8,128)(2,1)S(1)}, bf16[128,384]{1,0:T(8,128)(2,1)S(1)}, u32[]{:S(2)}, u32[]{:S(2)}) collective-permute-start(bf16[128,384]{1,0:T(8,128)(2,1)S(1)} %get-tuple-element.75.own), channel_id=1, source_target_pairs={{0,64},{32,96},{64,0},{96,32},{1,65},{33,97},{65,1},{97,33},{2,66}... | collective-permute-start | bytes 294920 | tf_op jit(solution)/shard_map/ppermute | solution.py:35
  182.1 4.6 %collective-permute-start.32 = (bf16[128,384]{1,0:T(8,128)(2,1)S(1)}, bf16[128,384]{1,0:T(8,128)(2,1)S(1)}, u32[]{:S(2)}, u32[]{:S(2)}) collective-permute-start(bf16[128,384]{1,0:T(8,128)(2,1)S(1)} %get-tuple-element.75.own), channel_id=1, source_target_pairs={{0,96},{32,0},{64,32},{96,64},{1,97},{33,1},{65,33},{97,65},{2,98}... | collective-permute-start | bytes 294920 | tf_op jit(solution)/shard_map/ppermute | solution.py:35

commit v3 on v2

--- a/solution.py
+++ b/solution.py
@@ -327,7 +327,7 @@
 
 
 def line_kernel(
-    part_ref, chip_ref, from_1, from_2, from_3, out_a_ref, out_b_ref, read_ref,
+    part_ref, chip_ref, from_1, from_2, from_3, out_a_ref, out_b_ref,
     stat_ref, mine_ref, theirs_ref,
 ):
     for side, o_ref in enumerate((out_a_ref, out_b_ref)):
@@ -344,16 +344,15 @@
                     mine_ref[i, :, head_cols(h)] = scaled
                 else:
                     theirs_ref[pl.ds(i * TOK, TOK), head_cols(h)] = scaled.astype(BF16)
-    theirs_ref[pl.ds(NY * TOK, HEAD_DIM)] = read_ref[...]
-
-
-def join_kernel(mine_ref, core_ref, read_ref, own_ref, pay_1, pay_2, pay_3):
+
+
+def join_kernel(mine_ref, core_ref, read_ref, pair_ref, own_ref, pay_1, pay_2, pay_3):
     own_ref[...] = mine_ref[0] + core_ref[pl.ds(0, TOK)].astype(F32)
     for o, pay in ((1, pay_1), (2, pay_2), (3, pay_3)):
         total = mine_ref[o] + core_ref[pl.ds(o * TOK, TOK)].astype(F32)
         pay[pl.ds(0, TOK)] = total.astype(BF16)
         pay[pl.ds(TOK, HEAD_DIM)] = read_ref[...]
-        pay[pl.ds(TOK + HEAD_DIM, HEAD_DIM)] = core_ref[pl.ds(NY * TOK, HEAD_DIM)]
+        pay[pl.ds(TOK + HEAD_DIM, HEAD_DIM)] = pair_ref[...]
 
 
 def triangle(upper):
@@ -362,8 +361,8 @@
     return row <= col if upper else row >= col
 
 
-def decay_columns(decay_ref):
-    return dot(triangle(False).astype(F32), decay_ref[...], 1, 1, HIGHEST)
+def decay_columns(decay):
+    return dot(triangle(False).astype(F32), decay[...], 1, 1, HIGHEST)
 
 
 def log_pieces(log):
@@ -439,7 +438,7 @@
     same = chain_members(lines[0])[1]
     own_start = least([jnp.where(s > 0, k, 99) for s, k in zip(same, lines[0])])
     earlier = [flag(s < own_start) for s in starts]
-    result = jnp.zeros((HEAD_DIM, WIDTH), F32)
+    result = 0.0
     for o in range(NX):
         exponent = prefix
         for i in range(NX):
@@ -538,11 +537,11 @@
 
 
 def back_kernel(
-    group_ref, index_ref, log_ref, read_ref, core_ref, from_1, from_2, from_3, handed_ref, part_ref
+    group_ref, index_ref, log_ref, read_ref, pair_ref, from_1, from_2, from_3, handed_ref, part_ref
 ):
     logs = [log_ref[pl.ds(j, 1)] for j in range(LINE)]
     sources = [(read_ref, 0), (from_1, TOK), (from_2, TOK), (from_3, TOK)]
-    sources += [(core_ref, NY * TOK)]
+    sources += [(pair_ref, 0)]
     sources += [(ref, TOK + HEAD_DIM) for ref in (from_1, from_2, from_3)]
     states = [
         functools.partial(lambda ref, row: ref[pl.ds(row, HEAD_DIM)].astype(F32), ref, row)
@@ -557,20 +556,25 @@
 
 def write_kernel(
     group_ref, index_ref, k_ref, v_ref, decay_ref, part_ref, log_ref, own, from_1, from_2, from_3,
-    dk_in, dv_in, dk_ref, dv_ref,
-):
-    leave_all = part_ref[pl.ds(0, HEAD_DIM)] + total_sums(
+    dk_in, dv_in, out_own, out_1, out_2, out_3, dkv_own, dkv_1, dkv_2, dkv_3,
+    dk_ref, dv_ref, soft_out_ref, soft_dk_ref, soft_dv_ref,
+):
+    leave = part_ref[pl.ds(0, HEAD_DIM)] + total_sums(
         group_ref, index_ref, False, [t[...] for t in (own, from_1, from_2, from_3)],
         [log_ref[pl.ds(o, 1)] for o in range(NX)], part_ref[pl.ds(HEAD_DIM, 1)],
     )
-    cumulative = decay_columns(decay_ref)
+    leave = leave.astype(BF16)
+    cumulative = decay_columns(decay_ref[pl.ds(pl.program_id(0), 1)])
     tail = jnp.exp(cumulative[TOK - 1 : TOK] - cumulative)
-    for h in range(HEADS):
-        cols = head_cols(h)
-        leave = leave_all[:, h * HEAD_DIM : (h + 1) * HEAD_DIM].astype(BF16)
-        scale = tail[:, h : h + 1]
-        dk_ref[:, cols] = dk_in[:, cols] + scale * dot(v_ref[:, cols], leave, 1, 1)
-        dv_ref[:, cols] = dv_in[:, cols] + scale * dot(k_ref[:, cols], leave, 1, 0)
+    dk_ref[...] = dk_in[...] + tail * dot(v_ref[...], leave, 1, 1)
+    dv_ref[...] = dv_in[...] + tail * dot(k_ref[...], leave, 1, 0)
+    soft_out_ref[...] = sum(
+        (r[...].astype(F32) for r in (out_1, out_2, out_3)), out_own[...]
+    ).astype(BF16)
+    for i, ref in enumerate((soft_dk_ref, soft_dv_ref)):
+        ref[...] = sum(
+            (r[i].astype(F32) for r in (dkv_1, dkv_2, dkv_3)), dkv_own[i]
+        ).astype(BF16)
 
 
 def in_vmem(n):
@@ -592,6 +596,7 @@
         shaped(PACK_ROWS, WIDTH, dtype=BF16),
         2**26,
         (soft_grad, lin_key, lin_value, decay),
+        vmem=60,
     )
     q_from = {0: soft_query, **{o: fetch(soft_query, "y", NY, o) for o in OFFSETS}}
     g_from = {0: packed, **{o: fetch(packed, "y", NY, o) for o in OFFSETS}}
@@ -647,19 +652,20 @@
         [
             shaped(2, NY, 8, TOK),
             shaped(NY, TOK, WIDTH),
-            shaped(NY * TOK + HEAD_DIM, WIDTH, dtype=BF16),
+            shaped(NY * TOK, WIDTH, dtype=BF16),
         ],
         2**22,
-        (part, chip, received[1], received[2], received[3], out_a, out_b, read_grad),
+        (part, chip, received[1], received[2], received[3], out_a, out_b),
     )
     from_core = fetch(theirs, "c", NC, 1)
+    pair_read = fetch(read_grad, "c", NC, 1)
 
     grads = far_backward(place, 0, 1, qa, qb, ga, gb, kvs[1:], stats)
     own_out, *pays = call(
         join_kernel,
         [rows] + [shaped(2 * TOK, WIDTH, dtype=BF16)] * 3,
         2**22,
-        (mine, from_core, read_grad),
+        (mine, from_core, read_grad, pair_read),
     )
     sent_out = {o: send(pays[o - 1], "y", NY, o) for o in OFFSETS}
     dq_a, dq_b, far_dkv = far_backward(place, 1, 2, qa, qb, ga, gb, kvs[1:], stats, tuple(grads))
@@ -671,7 +677,7 @@
         back_kernel,
         [shaped(HEAD_DIM, WIDTH, dtype=BF16), shaped(HEAD_DIM + 8, WIDTH)],
         2**24,
-        (*place, logs, read_grad, from_core, *(sent_out[NY - o] for o in (1, 2, 3))),
+        (*place, logs, read_grad, pair_read, *(sent_out[NY - o] for o in (1, 2, 3))),
         **placed(in_vmem(6), in_vmem(2)),
     )
     back_totals = [back_handed, *(fetch(back_handed, "x", NX, o) for o in (1, 2, 3))]
@@ -679,22 +685,32 @@
     soft_dq = chip_dq[0]
     for o in OFFSETS:
         soft_dq = soft_dq + send(chip_dq[o].astype(BF16), "y", NY, o).astype(F32)
-    lin_dk, lin_dv = call(
+    head_block = pl.BlockSpec((TOK, HEAD_DIM), lambda h, *_: (0, h))
+    lin_dk, lin_dv, soft_out, soft_dk, soft_dv = call(
         write_kernel,
-        [rows, rows],
+        [rows, rows] + [shaped(TOK, WIDTH, dtype=BF16)] * 3,
         2**26,
-        (*place, lin_key, lin_value, decay, leave_part, line_logs, *back_totals, dk_local, dv_local),
-        **placed(in_vmem(11), in_vmem(2)),
-    )
-    soft_out = own_out
-    for o in OFFSETS:
-        soft_out = soft_out + sent_out[o][:TOK].astype(F32)
-    dkv = near_dkv
-    for sent in sent_dkv:
-        dkv = dkv + sent.astype(F32)
+        (
+            *place, lin_key, lin_value, decay, leave_part, line_logs, *back_totals,
+            dk_local, dv_local, own_out, *(sent_out[o] for o in OFFSETS), near_dkv, *sent_dkv,
+        ),
+        **placed(
+            [
+                head_block,
+                head_block,
+                pl.BlockSpec((HEADS, TOK), lambda h, *_: (0, 0)),
+                pl.BlockSpec((HEAD_DIM + 8, HEAD_DIM), lambda h, *_: (0, h)),
+                pl.BlockSpec((8, HEAD_DIM), lambda h, *_: (0, h)),
+            ]
+            + [pl.BlockSpec((HEAD_DIM, HEAD_DIM), lambda h, *_: (0, h))] * NX
+            + [head_block] * 6
+            + [pair_spec()] * NX,
+            [head_block] * 5,
+            grid=(HEADS,),
+        ),
+    )
     return (
-        soft_out.astype(BF16), soft_dq.astype(BF16), dkv[0].astype(BF16), dkv[1].astype(BF16),
-        lin_out, lin_dq, lin_dk, lin_dv,
+        soft_out, soft_dq.astype(BF16), soft_dk, soft_dv, lin_out, lin_dq, lin_dk, lin_dv,
     )
 
 

time: 189 us -> 179 us (0.947)
  the two profiles are of different devices: /device:TPU:8 before, /device:TPU:1 now
where the time goes in v3:
time: 179 us; the launch traced here: 175 us
  waiting for transfers between devices  83.8 us (47%)
  Pallas kernels  52.1 us (29%)
  starting transfers between devices  35.2 us (20%)
  other arithmetic  3.07 us (2%)
    ppermute x36, waiting for transfers between devices, send(): lax.ppermute(block, axis, [(i, (i + offset) % size) for i in range(size)])  83.8 us
    pallas_call x15, Pallas kernels, call(): pl.pallas_call(kernel, out_shape=out_shape, cost_estimate=pl.CostEstimate...  52.1 us
    ppermute x36, starting transfers between devices, send(): lax.ppermute(block, axis, [(i, (i + offset) % size) for i in range(size)])  35.2 us
  transfers between devices with their start and end apart: 36, of which 24 were waited for; matrix products, arithmetic and copies ran while one was open for 2% of the time, Pallas kernels for 25%

profile of v3, /device:TPU:1, one launch (start us, length us, event | category | flops | bytes accessed | tf_op | source)
XLA Modules:
  0.0 175.3 jit_solution(8853196001505333526)
XLA Ops:
  0.6 2.7 %shard_map.161 = bf16[400,384]{1,0:T(8,128)(2,1)} custom-call(bf16[256,384]{1,0:T(8,128)(2,1)} %g_ref.3, bf16[256,384]{1,0:T(8,128)(2,1)} %k_ref.5, bf16[256,384]{1,0:T(8,128)(2,1)} %v_ref.5, f32[3,256]{1,0:T(4,128)} %bitcast.34), custom_call_target="tpu_custom_call" | custom-call | flops 67108864 | bytes 2097152 | tf_op jit(solution)/shard_map/pallas_call | solution.py:57
  3.3 3.6 %collective-permute-start = (bf16[400,384]{1,0:T(8,128)(2,1)}, bf16[400,384]{1,0:T(8,128)(2,1)S(1)}, u32[]{:S(2)}, u32[]{:S(2)}) collective-permute-start(bf16[400,384]{1,0:T(8,128)(2,1)} %shard_map.161), channel_id=1, source_target_pairs={{0,24},{8,0},{16,8},{24,16},{1,25},{9,1},{17,9},{25,17},{2,26},{10... | collective-permute-start | bytes 921608 | tf_op jit(solution)/shard_map/ppermute | solution.py:35
  7.9 2.0 %collective-permute-start.11 = (bf16[256,384]{1,0:T(8,128)(2,1)}, bf16[256,384]{1,0:T(8,128)(2,1)S(1)}, u32[]{:S(2)}, u32[]{:S(2)}) collective-permute-start(bf16[256,384]{1,0:T(8,128)(2,1)} %param.11), channel_id=1, source_target_pairs={{0,24},{8,0},{16,8},{24,16},{1,25},{9,1},{17,9},{25,17},{2,26},{10... | collective-permute-start | bytes 589832 | tf_op jit(solution)/shard_map/ppermute | solution.py:35
  9.9 1.4 collective-permute-start.12
  11.3 7.3 %collective-permute-done = bf16[400,384]{1,0:T(8,128)(2,1)S(1)} collective-permute-done((bf16[400,384]{1,0:T(8,128)(2,1)}, bf16[400,384]{1,0:T(8,128)(2,1)S(1)}, u32[]{:S(2)}, u32[]{:S(2)}) %collective-permute-start) | collective-permute-done | bytes 307232 | tf_op jit(solution)/shard_map/ppermute | solution.py:35
  18.6 7.0 %collective-permute-done.2 = bf16[400,384]{1,0:T(8,128)(2,1)S(1)} collective-permute-done((bf16[400,384]{1,0:T(8,128)(2,1)}, bf16[400,384]{1,0:T(8,128)(2,1)S(1)}, u32[]{:S(2)}, u32[]{:S(2)}) %collective-permute-start.2) | collective-permute-done | bytes 307232 | tf_op jit(solution)/shard_map/ppermute | solution.py:35
  25.6 1.2 pad_maximum_fusion.ga_ref.g_a
  26.8 0.8 collective-permute-start.3
  28.0 4.7 %collective-permute-done.13 = bf16[256,384]{1,0:T(8,128)(2,1)S(1)} collective-permute-done((bf16[256,384]{1,0:T(8,128)(2,1)}, bf16[256,384]{1,0:T(8,128)(2,1)S(1)}, u32[]{:S(2)}, u32[]{:S(2)}) %collective-permute-start.13) | collective-permute-done | bytes 196640 | tf_op jit(solution)/shard_map/ppermute | solution.py:35
  33.5 0.8 pad_maximum_fusion.2.kv_0.kv_ref
  34.3 2.5 %collective-permute-start.14 = (bf16[2,256,384]{2,1,0:T(8,128)(2,1)}, bf16[2,256,384]{2,1,0:T(8,128)(2,1)}, u32[]{:S(2)}, u32[]{:S(2)}) collective-permute-start(bf16[2,256,384]{2,1,0:T(8,128)(2,1)} %pad_maximum_fusion.2.kv_0.kv_ref), channel_id=1, source_target_pairs={{0,96},{32,0},{64,32},{96,64},{1,97},{33,1},{65,33},{97,65},{2,98}... | collective-permute-start | bytes 1179656 | tf_op jit(solution)/shard_map/ppermute | solution.py:35
  37.9 15.9 %collective-permute-done.14.kv_1 = bf16[2,256,384]{2,1,0:T(8,128)(2,1)} collective-permute-done((bf16[2,256,384]{2,1,0:T(8,128)(2,1)}, bf16[2,256,384]{2,1,0:T(8,128)(2,1)}, u32[]{:S(2)}, u32[]{:S(2)}) %collective-permute-start.14) | collective-permute-done | bytes 393248 | tf_op jit(solution)/shard_map/ppermute | solution.py:35
  53.8 4.2 %collective-permute-done.16.kv_3 = bf16[2,256,384]{2,1,0:T(8,128)(2,1)} collective-permute-done((bf16[2,256,384]{2,1,0:T(8,128)(2,1)}, bf16[2,256,384]{2,1,0:T(8,128)(2,1)}, u32[]{:S(2)}, u32[]{:S(2)}) %collective-permute-start.16) | collective-permute-done | bytes 393248 | tf_op jit(solution)/shard_map/ppermute | solution.py:35
  58.0 7.4 %shard_map.165 = (bf16[4,256,384]{2,1,0:T(8,128)(2,1)S(1)}, f32[4,8,256]{2,1,0:T(8,128)S(1)}) custom-call(s32[32]{0:T(128)S(1)} %copy-done.5, s32[1]{0:T(128)} %bitcast.index_ref, bf16[4,256,384]{2,1,0:T(8,128)(2,1)S(1)} %pad_maximum_fusion.1.q_ref.qa_ref, bf16[2,256,384]{2,1,0:T(8,128)(2,1)} %pad_maximum_fusion.2.kv_0.kv_ref, ...), custom_call_target="tpu_custom_call" | custom-call | flops 1610612736 | bytes 2097152 | tf_op jit(solution)/shard_map/pallas_call | solution.py:57
  65.5 7.4 %shard_map.166 = (bf16[4,256,384]{2,1,0:T(8,128)(2,1)S(1)}, f32[4,8,256]{2,1,0:T(8,128)S(1)}) custom-call(s32[32]{0:T(128)S(1)} %copy-done.5, s32[1]{0:T(128)} %bitcast.index_ref, bf16[4,256,384]{2,1,0:T(8,128)(2,1)} %collective-permute-done.17.q_ref.qb_ref, bf16[2,256,384]{2,1,0:T(8,128)(2,1)} %pad_maximum_fusion.2.kv_0.kv_ref, ...), custom_call_target="tpu_custom_call" | custom-call | flops 1610612736 | bytes 2097152 | tf_op jit(solution)/shard_map/pallas_call | solution.py:57
  72.9 1.7 shard_map.167.part_ref
  75.1 0.9 collective-permute-done.18.other_ref
  77.6 1.6 collective-permute-done.19.from_1
  79.2 1.9 %collective-permute-done.20.from_2 = f32[2,4,8,256]{3,2,1,0:T(8,128)S(1)} collective-permute-done((f32[2,4,8,256]{3,2,1,0:T(8,128)S(1)}, f32[2,4,8,256]{3,2,1,0:T(8,128)S(1)}, u32[]{:S(2)}, u32[]{:S(2)}) %collective-permute-start.20) | collective-permute-done | bytes 65568 | tf_op jit(solution)/shard_map/ppermute | solution.py:35
  81.1 2.0 %collective-permute-done.21.from_3 = f32[2,4,8,256]{3,2,1,0:T(8,128)S(1)} collective-permute-done((f32[2,4,8,256]{3,2,1,0:T(8,128)S(1)}, f32[2,4,8,256]{3,2,1,0:T(8,128)S(1)}, u32[]{:S(2)}, u32[]{:S(2)}) %collective-permute-start.21) | collective-permute-done | bytes 65568 | tf_op jit(solution)/shard_map/ppermute | solution.py:35
  83.1 1.3 shard_map.169
  84.4 1.0 collective-permute-start.22
  85.4 5.7 %shard_map.172 = (f32[4,3,128,256]{3,2,1,0:T(8,128)S(1)}, f32[4,3,128,256]{3,2,1,0:T(8,128)S(1)}, bf16[3,2,256,384]{3,2,1,0:T(8,128)(2,1)S(1)}) custom-call(s32[32]{0:T(128)S(1)} %copy-done.5, s32[1]{0:T(128)} %bitcast.index_ref, bf16[4,256,384]{2,1,0:T(8,128)(2,1)S(1)} %pad_maximum_fusion.1.q_ref.qa_ref, ...), custom_call_target="tpu_custom_call" | custom-call | flops 2013265920 | bytes 2097152 | tf_op jit(solution)/shard_map/pallas_call | solution.py:57
  91.1 9.9 %shard_map.173 = (f32[4,3,128,256]{3,2,1,0:T(8,128)S(1)}, f32[4,3,128,256]{3,2,1,0:T(8,128)S(1)}, bf16[3,2,256,384]{3,2,1,0:T(8,128)(2,1)S(1)}) custom-call(s32[32]{0:T(128)S(1)} %copy-done.5, s32[1]{0:T(128)} %bitcast.index_ref, ...), custom_call_target="tpu_custom_call", output_to_operand_aliasing={{0}: (10, {}), {1}: (11, {}), {2}: (12, {})} | custom-call | flops 4026531840 | bytes 2097152 | tf_op jit(solution)/shard_map/pallas_call | solution.py:57
  101.0 6.7 %shard_map.174 = (bf16[4,256,384]{2,1,0:T(8,128)(2,1)S(1)}, bf16[4,256,384]{2,1,0:T(8,128)(2,1)S(1)}, f32[2,256,384]{2,1,0:T(8,128)S(1)}) custom-call(s32[32]{0:T(128)S(1)} %copy-done.5, s32[1]{0:T(128)} %bitcast.index_ref, bf16[4,256,384]{2,1,0:T(8,128)(2,1)S(1)} %pad_maximum_fusion.1.q_ref.qa_ref, ...), custom_call_target="tpu_custom_call" | custom-call | flops 2013265920 | bytes 2097152 | tf_op jit(solution)/shard_map/pallas_call | solution.py:57
  107.9 1.0 shard_map.162
  110.5 2.7 %collective-permute-done.4.from_1 = bf16[144,384]{1,0:T(8,128)(2,1)S(1)} collective-permute-done((bf16[144,384]{1,0:T(8,128)(2,1)S(1)}, bf16[144,384]{1,0:T(8,128)(2,1)S(1)}, u32[]{:S(2)}, u32[]{:S(2)}) %collective-permute-start.4) | collective-permute-done | bytes 110624 | tf_op jit(solution)/shard_map/ppermute | solution.py:35
  113.1 1.4 collective-permute-done.5.from_2
  114.5 3.7 %collective-permute-done.6.from_3 = bf16[144,384]{1,0:T(8,128)(2,1)S(1)} collective-permute-done((bf16[144,384]{1,0:T(8,128)(2,1)S(1)}, bf16[144,384]{1,0:T(8,128)(2,1)S(1)}, u32[]{:S(2)}, u32[]{:S(2)}) %collective-permute-start.6) | collective-permute-done | bytes 110624 | tf_op jit(solution)/shard_map/ppermute | solution.py:35
  118.2 1.7 shard_map.163
  120.0 3.8 %collective-permute-start.7 = (f32[8,256]{1,0:T(8,128)S(1)}, f32[8,256]{1,0:T(8,128)S(1)}, u32[]{:S(2)}, u32[]{:S(2)}) collective-permute-start(f32[8,256]{1,0:T(8,128)S(1)} %get-tuple-element.52.sum_0), channel_id=1, source_target_pairs={{0,3},{1,0},{2,1},{3,2},{4,7},{5,4},{6,5},{7,6},{8,11},{9,8},{10,9... | collective-permute-start | bytes 24584 | tf_op jit(solution)/shard_map/ppermute | solution.py:35
  124.5 3.2 %collective-permute-done.8.sum_2 = f32[8,256]{1,0:T(8,128)S(1)} collective-permute-done((f32[8,256]{1,0:T(8,128)S(1)}, f32[8,256]{1,0:T(8,128)S(1)}, u32[]{:S(2)}, u32[]{:S(2)}) %collective-permute-start.8) | collective-permute-done | bytes 8224 | tf_op jit(solution)/shard_map/ppermute | solution.py:35
  127.8 2.2 %shard_map.164 = (f32[256,384]{1,0:T(8,128)}, f32[256,384]{1,0:T(8,128)}, f32[256,384]{1,0:T(8,128)S(1)}, f32[256,384]{1,0:T(8,128)S(1)}, bf16[128,384]{1,0:T(8,128)(2,1)S(1)}) custom-call(bf16[256,384]{1,0:T(8,128)(2,1)S(1)} %copy-done.2, bf16[256,384]{1,0:T(8,128)(2,1)S(1)} %copy-done, bf16[256,384]{1,0:T(8,128)(2,1)S(1)} %copy-done.1, ...), custom_call_target="tpu_custom_call" | custom-call | flops 268435456 | bytes 2097152 | tf_op jit(solution)/shard_map/pallas_call | solution.py:57
  129.9 1.9 %collective-permute-start.10 = (bf16[128,384]{1,0:T(8,128)(2,1)S(1)}, bf16[128,384]{1,0:T(8,128)(2,1)S(1)}, u32[]{:S(2)}, u32[]{:S(2)}) collective-permute-start(bf16[128,384]{1,0:T(8,128)(2,1)S(1)} %get-tuple-element.53.read_ref), channel_id=1, source_target_pairs={{0,4},{4,0},{1,5},{5,1},{2,6},{6,2},{3,7},{7,3},{8,12},{12,8},{9,1... | collective-permute-start | bytes 294920 | tf_op jit(solution)/shard_map/ppermute | solution.py:35
  133.0 1.3 collective-permute-start.23
  135.2 2.0 %collective-permute-start.33 = (bf16[256,384]{1,0:T(8,128)(2,1)S(1)}, bf16[256,384]{1,0:T(8,128)(2,1)S(1)}, u32[]{:S(2)}, u32[]{:S(2)}) collective-permute-start(bf16[256,384]{1,0:T(8,128)(2,1)S(1)} %get-tuple-element.91), channel_id=1, source_target_pairs={{0,8},{8,16},{16,24},{24,0},{1,9},{9,17},{17,25},{25,1},{2,10},{10... | collective-permute-start | bytes 589832 | tf_op jit(solution)/shard_map/ppermute | solution.py:35
  137.3 6.6 %collective-permute-done.29.dkv_1 = bf16[2,256,384]{2,1,0:T(8,128)(2,1)S(1)} collective-permute-done((bf16[2,256,384]{2,1,0:T(8,128)(2,1)S(1)}, bf16[2,256,384]{2,1,0:T(8,128)(2,1)S(1)}, u32[]{:S(2)}, u32[]{:S(2)}) %collective-permute-start.29) | collective-permute-done | bytes 393248 | tf_op jit(solution)/shard_map/ppermute | solution.py:35
  143.9 1.2 collective-permute-start.34
  145.9 2.0 %collective-permute-start.30 = (bf16[2,256,384]{2,1,0:T(8,128)(2,1)S(1)}, bf16[2,256,384]{2,1,0:T(8,128)(2,1)S(1)}, u32[]{:S(2)}, u32[]{:S(2)}) collective-permute-start(bf16[2,256,384]{2,1,0:T(8,128)(2,1)S(1)} %get-tuple-element.89), channel_id=1, source_target_pairs={{0,96},{32,0},{64,32},{96,64},{1,97},{33,1},{65,33},{97,65},{2,98}... | collective-permute-start | bytes 1179656 | tf_op jit(solution)/shard_map/ppermute | solution.py:35
  147.9 7.4 %collective-permute-done.25.from_3.out_1 = bf16[512,384]{1,0:T(8,128)(2,1)S(1)} collective-permute-done((bf16[512,384]{1,0:T(8,128)(2,1)S(1)}, bf16[512,384]{1,0:T(8,128)(2,1)S(1)}, u32[]{:S(2)}, u32[]{:S(2)}) %collective-permute-start.25) | collective-permute-done | bytes 393248 | tf_op jit(solution)/shard_map/ppermute | solution.py:35
  155.2 1.0 collective-permute-start.31
  156.2 1.0 shard_map.171
  157.2 3.2 %collective-permute-done.33 = bf16[256,384]{1,0:T(8,128)(2,1)S(1)} collective-permute-done((bf16[256,384]{1,0:T(8,128)(2,1)S(1)}, bf16[256,384]{1,0:T(8,128)(2,1)S(1)}, u32[]{:S(2)}, u32[]{:S(2)}) %collective-permute-start.33) | collective-permute-done | bytes 196640 | tf_op jit(solution)/shard_map/ppermute | solution.py:35
  160.4 1.9 %collective-permute-start.26 = (bf16[128,384]{1,0:T(8,128)(2,1)S(1)}, bf16[128,384]{1,0:T(8,128)(2,1)S(1)}, u32[]{:S(2)}, u32[]{:S(2)}) collective-permute-start(bf16[128,384]{1,0:T(8,128)(2,1)S(1)} %get-tuple-element.65.own), channel_id=1, source_target_pairs={{0,96},{32,0},{64,32},{96,64},{1,97},{33,1},{65,33},{97,65},{2,98}... | collective-permute-start | bytes 294920 | tf_op jit(solution)/shard_map/ppermute | solution.py:35
  163.6 3.2 %collective-permute-done.31.dkv_3 = bf16[2,256,384]{2,1,0:T(8,128)(2,1)S(1)} collective-permute-done((bf16[2,256,384]{2,1,0:T(8,128)(2,1)S(1)}, bf16[2,256,384]{2,1,0:T(8,128)(2,1)S(1)}, u32[]{:S(2)}, u32[]{:S(2)}) %collective-permute-start.31) | collective-permute-done | bytes 393248 | tf_op jit(solution)/shard_map/ppermute | solution.py:35
  166.8 2.3 %collective-permute-done.26.from_1 = bf16[128,384]{1,0:T(8,128)(2,1)S(1)} collective-permute-done((bf16[128,384]{1,0:T(8,128)(2,1)S(1)}, bf16[128,384]{1,0:T(8,128)(2,1)S(1)}, u32[]{:S(2)}, u32[]{:S(2)}) %collective-permute-start.26) | collective-permute-done | bytes 98336 | tf_op jit(solution)/shard_map/ppermute | solution.py:35
  169.2 2.8 %collective-permute-done.28.from_3 = bf16[128,384]{1,0:T(8,128)(2,1)S(1)} collective-permute-done((bf16[128,384]{1,0:T(8,128)(2,1)S(1)}, bf16[128,384]{1,0:T(8,128)(2,1)S(1)}, u32[]{:S(2)}, u32[]{:S(2)}) %collective-permute-start.28) | collective-permute-done | bytes 98336 | tf_op jit(solution)/shard_map/ppermute | solution.py:35
  172.0 3.4 %shard_map.175 = (f32[256,384]{1,0:T(8,128)}, f32[256,384]{1,0:T(8,128)}, bf16[256,384]{1,0:T(8,128)(2,1)}, bf16[256,384]{1,0:T(8,128)(2,1)}, bf16[256,384]{1,0:T(8,128)(2,1)}) custom-call(s32[32]{0:T(128)S(1)} %copy-done.5, s32[1]{0:T(128)} %bitcast.index_ref, bf16[256,384]{1,0:T(8,128)(2,1)S(1)} %copy-done, bf16[256,384]{1,0:T(8,128)(2,1)S(1)} %copy-done.1, ...), custom_call_target="tpu_custom_call" | custom-call | flops 67108864 | bytes 2097152 | tf_op jit(solution)/shard_map/pallas_call | solution.py:57
  (64 shorter events, 12.0 us)
Async XLA Ops:
  3.3 15.3 %collective-permute-start = (bf16[400,384]{1,0:T(8,128)(2,1)}, bf16[400,384]{1,0:T(8,128)(2,1)S(1)}, u32[]{:S(2)}, u32[]{:S(2)}) collective-permute-start(bf16[400,384]{1,0:T(8,128)(2,1)} %shard_map.161), channel_id=1, source_target_pairs={{0,24},{8,0},{16,8},{24,16},{1,25},{9,1},{17,9},{25,17},{2,26},{10... | collective-permute-start | bytes 921608 | tf_op jit(solution)/shard_map/ppermute | solution.py:35
  6.8 11.7 %collective-permute-start.1 = (bf16[400,384]{1,0:T(8,128)(2,1)}, bf16[400,384]{1,0:T(8,128)(2,1)S(1)}, u32[]{:S(2)}, u32[]{:S(2)}) collective-permute-start(bf16[400,384]{1,0:T(8,128)(2,1)} %shard_map.161), channel_id=1, source_target_pairs={{0,16},{8,24},{16,0},{24,8},{1,17},{9,25},{17,1},{25,9},{2,18},{10... | collective-permute-start | bytes 921608 | tf_op jit(solution)/shard_map/ppermute | solution.py:35
  7.2 18.4 %collective-permute-start.2 = (bf16[400,384]{1,0:T(8,128)(2,1)}, bf16[400,384]{1,0:T(8,128)(2,1)S(1)}, u32[]{:S(2)}, u32[]{:S(2)}) collective-permute-start(bf16[400,384]{1,0:T(8,128)(2,1)} %shard_map.161), channel_id=1, source_target_pairs={{0,8},{8,16},{16,24},{24,0},{1,9},{9,17},{17,25},{25,1},{2,10},{10... | collective-permute-start | bytes 921608 | tf_op jit(solution)/shard_map/ppermute | solution.py:35
  7.9 20.1 %collective-permute-start.11 = (bf16[256,384]{1,0:T(8,128)(2,1)}, bf16[256,384]{1,0:T(8,128)(2,1)S(1)}, u32[]{:S(2)}, u32[]{:S(2)}) collective-permute-start(bf16[256,384]{1,0:T(8,128)(2,1)} %param.11), channel_id=1, source_target_pairs={{0,24},{8,0},{16,8},{24,16},{1,25},{9,1},{17,9},{25,17},{2,26},{10... | collective-permute-start | bytes 589832 | tf_op jit(solution)/shard_map/ppermute | solution.py:35
  9.9 18.1 %collective-permute-start.12 = (bf16[256,384]{1,0:T(8,128)(2,1)}, bf16[256,384]{1,0:T(8,128)(2,1)S(1)}, u32[]{:S(2)}, u32[]{:S(2)}) collective-permute-start(bf16[256,384]{1,0:T(8,128)(2,1)} %param.11), channel_id=1, source_target_pairs={{0,16},{8,24},{16,0},{24,8},{1,17},{9,25},{17,1},{25,9},{2,18},{10... | collective-permute-start | bytes 589832 | tf_op jit(solution)/shard_map/ppermute | solution.py:35
  18.5 14.2 %collective-permute-start.13 = (bf16[256,384]{1,0:T(8,128)(2,1)}, bf16[256,384]{1,0:T(8,128)(2,1)S(1)}, u32[]{:S(2)}, u32[]{:S(2)}) collective-permute-start(bf16[256,384]{1,0:T(8,128)(2,1)} %param.11), channel_id=1, source_target_pairs={{0,8},{8,16},{16,24},{24,0},{1,9},{9,17},{17,25},{25,1},{2,10},{10... | collective-permute-start | bytes 589832 | tf_op jit(solution)/shard_map/ppermute | solution.py:35
  25.6 7.1 %copy-start.6 = (bf16[256,384]{1,0:T(8,128)(2,1)S(1)}, bf16[256,384]{1,0:T(8,128)(2,1)}, u32[]{:S(2)}) copy-start(bf16[256,384]{1,0:T(8,128)(2,1)} %param.11) | copy-start | bytes 589828
  26.8 6.7 %copy-start.7 = (bf16[256,384]{1,0:T(8,128)(2,1)S(1)}, bf16[256,384]{1,0:T(8,128)(2,1)}, u32[]{:S(2)}) copy-start(bf16[256,384]{1,0:T(8,128)(2,1)} %param.13) | copy-start | bytes 589828
  26.8 6.7 %copy-start.8 = (bf16[256,384]{1,0:T(8,128)(2,1)S(1)}, bf16[256,384]{1,0:T(8,128)(2,1)}, u32[]{:S(2)}) copy-start(bf16[256,384]{1,0:T(8,128)(2,1)} %param.12) | copy-start | bytes 589828
  26.8 31.2 %copy-start.5 = (s32[32]{0:T(128)S(1)}, s32[32]{0:T(128)}, u32[]{:S(2)}) copy-start(s32[32]{0:T(128)} %group_ref.17) | copy-start | bytes 388
  26.8 46.0 %collective-permute-start.3 = (bf16[4,400,384]{2,1,0:T(8,128)(2,1)S(1)}, bf16[4,400,384]{2,1,0:T(8,128)(2,1)S(1)}, u32[]{:S(2)}, u32[]{:S(2)}) collective-permute-start(bf16[4,400,384]{2,1,0:T(8,128)(2,1)S(1)} %pad_maximum_fusion.ga_ref.g_a), channel_id=1, source_target_pairs={{0,4},{4,0},{1,5},{5,1},{2,6},{6,2},{3,7},{7,3},{8,12},{12,8},{9,1... | collective-permute-start | bytes 3686408 | tf_op jit(solution)/shard_map/ppermute | solution.py:35
  32.8 32.6 %collective-permute-start.17 = (bf16[4,256,384]{2,1,0:T(8,128)(2,1)S(1)}, bf16[4,256,384]{2,1,0:T(8,128)(2,1)}, u32[]{:S(2)}, u32[]{:S(2)}) collective-permute-start(bf16[4,256,384]{2,1,0:T(8,128)(2,1)S(1)} %pad_maximum_fusion.1.q_ref.qa_ref), channel_id=1, source_target_pairs={{0,4},{4,0},{1,5},{5,1},{2,6},{6,2},{3,7},{7,3},{8,12},{12,8},{9,1... | collective-permute-start | bytes 2359304 | tf_op jit(solution)/shard_map/ppermute | solution.py:35
  34.3 19.5 %collective-permute-start.14 = (bf16[2,256,384]{2,1,0:T(8,128)(2,1)}, bf16[2,256,384]{2,1,0:T(8,128)(2,1)}, u32[]{:S(2)}, u32[]{:S(2)}) collective-permute-start(bf16[2,256,384]{2,1,0:T(8,128)(2,1)} %pad_maximum_fusion.2.kv_0.kv_ref), channel_id=1, source_target_pairs={{0,96},{32,0},{64,32},{96,64},{1,97},{33,1},{65,33},{97,65},{2,98}... | collective-permute-start | bytes 1179656 | tf_op jit(solution)/shard_map/ppermute | solution.py:35
  36.7 17.0 %collective-permute-start.15 = (bf16[2,256,384]{2,1,0:T(8,128)(2,1)}, bf16[2,256,384]{2,1,0:T(8,128)(2,1)}, u32[]{:S(2)}, u32[]{:S(2)}) collective-permute-start(bf16[2,256,384]{2,1,0:T(8,128)(2,1)} %pad_maximum_fusion.2.kv_0.kv_ref), channel_id=1, source_target_pairs={{0,64},{32,96},{64,0},{96,32},{1,65},{33,97},{65,1},{97,33},{2,66}... | collective-permute-start | bytes 1179656 | tf_op jit(solution)/shard_map/ppermute | solution.py:35
  37.3 20.8 %collective-permute-start.16 = (bf16[2,256,384]{2,1,0:T(8,128)(2,1)}, bf16[2,256,384]{2,1,0:T(8,128)(2,1)}, u32[]{:S(2)}, u32[]{:S(2)}) collective-permute-start(bf16[2,256,384]{2,1,0:T(8,128)(2,1)} %pad_maximum_fusion.2.kv_0.kv_ref), channel_id=1, source_target_pairs={{0,32},{32,64},{64,96},{96,0},{1,33},{33,65},{65,97},{97,1},{2,34}... | collective-permute-start | bytes 1179656 | tf_op jit(solution)/shard_map/ppermute | solution.py:35
  74.5 1.5 collective-permute-start.18
  76.1 3.2 %collective-permute-start.19 = (f32[2,4,8,256]{3,2,1,0:T(8,128)S(1)}, f32[2,4,8,256]{3,2,1,0:T(8,128)S(1)}, u32[]{:S(2)}, u32[]{:S(2)}) collective-permute-start(f32[2,4,8,256]{3,2,1,0:T(8,128)S(1)} %shard_map.168.chip_ref), channel_id=1, source_target_pairs={{0,24},{8,0},{16,8},{24,16},{1,25},{9,1},{17,9},{25,17},{2,26},{10... | collective-permute-start | bytes 196616 | tf_op jit(solution)/shard_map/ppermute | solution.py:35
  76.5 4.6 %collective-permute-start.20 = (f32[2,4,8,256]{3,2,1,0:T(8,128)S(1)}, f32[2,4,8,256]{3,2,1,0:T(8,128)S(1)}, u32[]{:S(2)}, u32[]{:S(2)}) collective-permute-start(f32[2,4,8,256]{3,2,1,0:T(8,128)S(1)} %shard_map.168.chip_ref), channel_id=1, source_target_pairs={{0,16},{8,24},{16,0},{24,8},{1,17},{9,25},{17,1},{25,9},{2,18},{10... | collective-permute-start | bytes 196616 | tf_op jit(solution)/shard_map/ppermute | solution.py:35
  76.9 6.3 %collective-permute-start.21 = (f32[2,4,8,256]{3,2,1,0:T(8,128)S(1)}, f32[2,4,8,256]{3,2,1,0:T(8,128)S(1)}, u32[]{:S(2)}, u32[]{:S(2)}) collective-permute-start(f32[2,4,8,256]{3,2,1,0:T(8,128)S(1)} %shard_map.168.chip_ref), channel_id=1, source_target_pairs={{0,8},{8,16},{16,24},{24,0},{1,9},{9,17},{17,25},{25,1},{2,10},{10... | collective-permute-start | bytes 196616 | tf_op jit(solution)/shard_map/ppermute | solution.py:35
  84.4 48.4 %collective-permute-start.22 = (bf16[1024,384]{1,0:T(8,128)(2,1)S(1)}, bf16[1024,384]{1,0:T(8,128)(2,1)S(1)}, u32[]{:S(2)}, u32[]{:S(2)}) collective-permute-start(bf16[1024,384]{1,0:T(8,128)(2,1)S(1)} %get-tuple-element.59), channel_id=1, source_target_pairs={{0,4},{4,0},{1,5},{5,1},{2,6},{6,2},{3,7},{7,3},{8,12},{12,8},{9,1... | collective-permute-start | bytes 2359304 | tf_op jit(solution)/shard_map/ppermute | solution.py:35
  107.7 10.5 %copy-start = (bf16[256,384]{1,0:T(8,128)(2,1)S(1)}, bf16[256,384]{1,0:T(8,128)(2,1)}, u32[]{:S(2)}) copy-start(bf16[256,384]{1,0:T(8,128)(2,1)} %k_ref.5) | copy-start | bytes 589828
  107.7 10.5 %copy-start.1 = (bf16[256,384]{1,0:T(8,128)(2,1)S(1)}, bf16[256,384]{1,0:T(8,128)(2,1)}, u32[]{:S(2)}) copy-start(bf16[256,384]{1,0:T(8,128)(2,1)} %v_ref.5) | copy-start | bytes 589828
  107.8 10.5 %copy-start.2 = (bf16[256,384]{1,0:T(8,128)(2,1)S(1)}, bf16[256,384]{1,0:T(8,128)(2,1)}, u32[]{:S(2)}) copy-start(bf16[256,384]{1,0:T(8,128)(2,1)} %q_ref.3) | copy-start | bytes 589828
  107.8 10.5 %copy-start.3 = (bf16[256,384]{1,0:T(8,128)(2,1)S(1)}, bf16[256,384]{1,0:T(8,128)(2,1)}, u32[]{:S(2)}) copy-start(bf16[256,384]{1,0:T(8,128)(2,1)} %g_ref.5) | copy-start | bytes 589828
  107.8 10.5 %copy-start.4 = (f32[256,3]{0,1:T(4,128)S(1)}, f32[256,3]{0,1:T(4,128)}, u32[]{:S(2)}) copy-start(f32[256,3]{0,1:T(4,128)} %param.18) | copy-start | bytes 9220
  107.8 27.1 %collective-permute-start.32 = (bf16[4,256,384]{2,1,0:T(8,128)(2,1)S(1)}, bf16[4,256,384]{2,1,0:T(8,128)(2,1)S(1)}, u32[]{:S(2)}, u32[]{:S(2)}) collective-permute-start(bf16[4,256,384]{2,1,0:T(8,128)(2,1)S(1)} %get-tuple-element.79), channel_id=1, source_target_pairs={{0,4},{4,0},{1,5},{5,1},{2,6},{6,2},{3,7},{7,3},{8,12},{12,8},{9,1... | collective-permute-start | bytes 2359304 | tf_op jit(solution)/shard_map/ppermute | solution.py:35
  108.9 4.2 %collective-permute-start.4 = (bf16[144,384]{1,0:T(8,128)(2,1)S(1)}, bf16[144,384]{1,0:T(8,128)(2,1)S(1)}, u32[]{:S(2)}, u32[]{:S(2)}) collective-permute-start(bf16[144,384]{1,0:T(8,128)(2,1)S(1)} %get-tuple-element.49.own), channel_id=1, source_target_pairs={{0,96},{32,0},{64,32},{96,64},{1,97},{33,1},{65,33},{97,65},{2,98}... | collective-permute-start | bytes 331784 | tf_op jit(solution)/shard_map/ppermute | solution.py:35
  109.4 5.2 %collective-permute-start.5 = (bf16[144,384]{1,0:T(8,128)(2,1)S(1)}, bf16[144,384]{1,0:T(8,128)(2,1)S(1)}, u32[]{:S(2)}, u32[]{:S(2)}) collective-permute-start(bf16[144,384]{1,0:T(8,128)(2,1)S(1)} %get-tuple-element.49.own), channel_id=1, source_target_pairs={{0,64},{32,96},{64,0},{96,32},{1,65},{33,97},{65,1},{97,33},{2,66}... | collective-permute-start | bytes 331784 | tf_op jit(solution)/shard_map/ppermute | solution.py:35
  109.9 8.3 %collective-permute-start.6 = (bf16[144,384]{1,0:T(8,128)(2,1)S(1)}, bf16[144,384]{1,0:T(8,128)(2,1)S(1)}, u32[]{:S(2)}, u32[]{:S(2)}) collective-permute-start(bf16[144,384]{1,0:T(8,128)(2,1)S(1)} %get-tuple-element.49.own), channel_id=1, source_target_pairs={{0,32},{32,64},{64,96},{96,0},{1,33},{33,65},{65,97},{97,1},{2,34}... | collective-permute-start | bytes 331784 | tf_op jit(solution)/shard_map/ppermute | solution.py:35
  120.0 4.6 %collective-permute-start.7 = (f32[8,256]{1,0:T(8,128)S(1)}, f32[8,256]{1,0:T(8,128)S(1)}, u32[]{:S(2)}, u32[]{:S(2)}) collective-permute-start(f32[8,256]{1,0:T(8,128)S(1)} %get-tuple-element.52.sum_0), channel_id=1, source_target_pairs={{0,3},{1,0},{2,1},{3,2},{4,7},{5,4},{6,5},{7,6},{8,11},{9,8},{10,9... | collective-permute-start | bytes 24584 | tf_op jit(solution)/shard_map/ppermute | solution.py:35
  123.7 4.0 %collective-permute-start.8 = (f32[8,256]{1,0:T(8,128)S(1)}, f32[8,256]{1,0:T(8,128)S(1)}, u32[]{:S(2)}, u32[]{:S(2)}) collective-permute-start(f32[8,256]{1,0:T(8,128)S(1)} %get-tuple-element.52.sum_0), channel_id=1, source_target_pairs={{0,2},{1,3},{2,0},{3,1},{4,6},{5,7},{6,4},{7,5},{8,10},{9,11},{10,... | collective-permute-start | bytes 24584 | tf_op jit(solution)/shard_map/ppermute | solution.py:35
  123.7 4.0 %collective-permute-start.9 = (f32[8,256]{1,0:T(8,128)S(1)}, f32[8,256]{1,0:T(8,128)S(1)}, u32[]{:S(2)}, u32[]{:S(2)}) collective-permute-start(f32[8,256]{1,0:T(8,128)S(1)} %get-tuple-element.52.sum_0), channel_id=1, source_target_pairs={{0,1},{1,2},{2,3},{3,0},{4,5},{5,6},{6,7},{7,4},{8,9},{9,10},{10,1... | collective-permute-start | bytes 24584 | tf_op jit(solution)/shard_map/ppermute | solution.py:35
  129.9 2.9 %collective-permute-start.10 = (bf16[128,384]{1,0:T(8,128)(2,1)S(1)}, bf16[128,384]{1,0:T(8,128)(2,1)S(1)}, u32[]{:S(2)}, u32[]{:S(2)}) collective-permute-start(bf16[128,384]{1,0:T(8,128)(2,1)S(1)} %get-tuple-element.53.read_ref), channel_id=1, source_target_pairs={{0,4},{4,0},{1,5},{5,1},{2,6},{6,2},{3,7},{7,3},{8,12},{12,8},{9,1... | collective-permute-start | bytes 294920 | tf_op jit(solution)/shard_map/ppermute | solution.py:35
  132.0 11.9 %collective-permute-start.29 = (bf16[2,256,384]{2,1,0:T(8,128)(2,1)S(1)}, bf16[2,256,384]{2,1,0:T(8,128)(2,1)S(1)}, u32[]{:S(2)}, u32[]{:S(2)}) collective-permute-start(bf16[2,256,384]{2,1,0:T(8,128)(2,1)S(1)} %get-tuple-element.90), channel_id=1, source_target_pairs={{0,32},{32,64},{64,96},{96,0},{1,33},{33,65},{65,97},{97,1},{2,34}... | collective-permute-start | bytes 1179656 | tf_op jit(solution)/shard_map/ppermute | solution.py:35
  133.0 12.2 %collective-permute-start.23 = (bf16[512,384]{1,0:T(8,128)(2,1)S(1)}, bf16[512,384]{1,0:T(8,128)(2,1)S(1)}, u32[]{:S(2)}, u32[]{:S(2)}) collective-permute-start(bf16[512,384]{1,0:T(8,128)(2,1)S(1)} %get-tuple-element.60), channel_id=1, source_target_pairs={{0,24},{8,0},{16,8},{24,16},{1,25},{9,1},{17,9},{25,17},{2,26},{10... | collective-permute-start | bytes 1179656 | tf_op jit(solution)/shard_map/ppermute | solution.py:35
  134.3 11.6 %collective-permute-start.24 = (bf16[512,384]{1,0:T(8,128)(2,1)S(1)}, bf16[512,384]{1,0:T(8,128)(2,1)S(1)}, u32[]{:S(2)}, u32[]{:S(2)}) collective-permute-start(bf16[512,384]{1,0:T(8,128)(2,1)S(1)} %get-tuple-element.61), channel_id=1, source_target_pairs={{0,16},{8,24},{16,0},{24,8},{1,17},{9,25},{17,1},{25,9},{2,18},{10... | collective-permute-start | bytes 1179656 | tf_op jit(solution)/shard_map/ppermute | solution.py:35
  134.9 20.3 %collective-permute-start.25 = (bf16[512,384]{1,0:T(8,128)(2,1)S(1)}, bf16[512,384]{1,0:T(8,128)(2,1)S(1)}, u32[]{:S(2)}, u32[]{:S(2)}) collective-permute-start(bf16[512,384]{1,0:T(8,128)(2,1)S(1)} %get-tuple-element.62), channel_id=1, source_target_pairs={{0,8},{8,16},{16,24},{24,0},{1,9},{9,17},{17,25},{25,1},{2,10},{10... | collective-permute-start | bytes 1179656 | tf_op jit(solution)/shard_map/ppermute | solution.py:35
  135.2 25.2 %collective-permute-start.33 = (bf16[256,384]{1,0:T(8,128)(2,1)S(1)}, bf16[256,384]{1,0:T(8,128)(2,1)S(1)}, u32[]{:S(2)}, u32[]{:S(2)}) collective-permute-start(bf16[256,384]{1,0:T(8,128)(2,1)S(1)} %get-tuple-element.91), channel_id=1, source_target_pairs={{0,8},{8,16},{16,24},{24,0},{1,9},{9,17},{17,25},{25,1},{2,10},{10... | collective-permute-start | bytes 589832 | tf_op jit(solution)/shard_map/ppermute | solution.py:35
  143.9 18.4 %collective-permute-start.34 = (bf16[256,384]{1,0:T(8,128)(2,1)S(1)}, bf16[256,384]{1,0:T(8,128)(2,1)S(1)}, u32[]{:S(2)}, u32[]{:S(2)}) collective-permute-start(bf16[256,384]{1,0:T(8,128)(2,1)S(1)} %get-tuple-element.93), channel_id=1, source_target_pairs={{0,24},{8,0},{16,8},{24,16},{1,25},{9,1},{17,9},{25,17},{2,26},{10... | collective-permute-start | bytes 589832 | tf_op jit(solution)/shard_map/ppermute | solution.py:35
  145.2 17.6 %collective-permute-start.35 = (bf16[256,384]{1,0:T(8,128)(2,1)S(1)}, bf16[256,384]{1,0:T(8,128)(2,1)S(1)}, u32[]{:S(2)}, u32[]{:S(2)}) collective-permute-start(bf16[256,384]{1,0:T(8,128)(2,1)S(1)} %get-tuple-element.92), channel_id=1, source_target_pairs={{0,16},{8,24},{16,0},{24,8},{1,17},{9,25},{17,1},{25,9},{2,18},{10... | collective-permute-start | bytes 589832 | tf_op jit(solution)/shard_map/ppermute | solution.py:35
  145.9 17.8 %collective-permute-start.30 = (bf16[2,256,384]{2,1,0:T(8,128)(2,1)S(1)}, bf16[2,256,384]{2,1,0:T(8,128)(2,1)S(1)}, u32[]{:S(2)}, u32[]{:S(2)}) collective-permute-start(bf16[2,256,384]{2,1,0:T(8,128)(2,1)S(1)} %get-tuple-element.89), channel_id=1, source_target_pairs={{0,96},{32,0},{64,32},{96,64},{1,97},{33,1},{65,33},{97,65},{2,98}... | collective-permute-start | bytes 1179656 | tf_op jit(solution)/shard_map/ppermute | solution.py:35
  155.2 11.6 %collective-permute-start.31 = (bf16[2,256,384]{2,1,0:T(8,128)(2,1)S(1)}, bf16[2,256,384]{2,1,0:T(8,128)(2,1)S(1)}, u32[]{:S(2)}, u32[]{:S(2)}) collective-permute-start(bf16[2,256,384]{2,1,0:T(8,128)(2,1)S(1)} %get-tuple-element.88), channel_id=1, source_target_pairs={{0,64},{32,96},{64,0},{96,32},{1,65},{33,97},{65,1},{97,33},{2,66}... | collective-permute-start | bytes 1179656 | tf_op jit(solution)/shard_map/ppermute | solution.py:35
  160.4 8.7 %collective-permute-start.26 = (bf16[128,384]{1,0:T(8,128)(2,1)S(1)}, bf16[128,384]{1,0:T(8,128)(2,1)S(1)}, u32[]{:S(2)}, u32[]{:S(2)}) collective-permute-start(bf16[128,384]{1,0:T(8,128)(2,1)S(1)} %get-tuple-element.65.own), channel_id=1, source_target_pairs={{0,96},{32,0},{64,32},{96,64},{1,97},{33,1},{65,33},{97,65},{2,98}... | collective-permute-start | bytes 294920 | tf_op jit(solution)/shard_map/ppermute | solution.py:35
  162.3 6.9 %collective-permute-start.27 = (bf16[128,384]{1,0:T(8,128)(2,1)S(1)}, bf16[128,384]{1,0:T(8,128)(2,1)S(1)}, u32[]{:S(2)}, u32[]{:S(2)}) collective-permute-start(bf16[128,384]{1,0:T(8,128)(2,1)S(1)} %get-tuple-element.65.own), channel_id=1, source_target_pairs={{0,64},{32,96},{64,0},{96,32},{1,65},{33,97},{65,1},{97,33},{2,66}... | collective-permute-start | bytes 294920 | tf_op jit(solution)/shard_map/ppermute | solution.py:35
  162.7 9.3 %collective-permute-start.28 = (bf16[128,384]{1,0:T(8,128)(2,1)S(1)}, bf16[128,384]{1,0:T(8,128)(2,1)S(1)}, u32[]{:S(2)}, u32[]{:S(2)}) collective-permute-start(bf16[128,384]{1,0:T(8,128)(2,1)S(1)} %get-tuple-element.65.own), channel_id=1, source_target_pairs={{0,32},{32,64},{64,96},{96,0},{1,33},{33,65},{65,97},{97,1},{2,34}... | collective-permute-start | bytes 294920 | tf_op jit(solution)/shard_map/ppermute | solution.py:35

commit v4 on v2

--- a/solution.py
+++ b/solution.py
@@ -327,7 +327,7 @@
 
 
 def line_kernel(
-    part_ref, chip_ref, from_1, from_2, from_3, out_a_ref, out_b_ref, read_ref,
+    part_ref, chip_ref, from_1, from_2, from_3, out_a_ref, out_b_ref,
     stat_ref, mine_ref, theirs_ref,
 ):
     for side, o_ref in enumerate((out_a_ref, out_b_ref)):
@@ -344,16 +344,15 @@
                     mine_ref[i, :, head_cols(h)] = scaled
                 else:
                     theirs_ref[pl.ds(i * TOK, TOK), head_cols(h)] = scaled.astype(BF16)
-    theirs_ref[pl.ds(NY * TOK, HEAD_DIM)] = read_ref[...]
-
-
-def join_kernel(mine_ref, core_ref, read_ref, own_ref, pay_1, pay_2, pay_3):
+
+
+def join_kernel(mine_ref, core_ref, read_ref, pair_ref, own_ref, pay_1, pay_2, pay_3):
     own_ref[...] = mine_ref[0] + core_ref[pl.ds(0, TOK)].astype(F32)
     for o, pay in ((1, pay_1), (2, pay_2), (3, pay_3)):
         total = mine_ref[o] + core_ref[pl.ds(o * TOK, TOK)].astype(F32)
         pay[pl.ds(0, TOK)] = total.astype(BF16)
         pay[pl.ds(TOK, HEAD_DIM)] = read_ref[...]
-        pay[pl.ds(TOK + HEAD_DIM, HEAD_DIM)] = core_ref[pl.ds(NY * TOK, HEAD_DIM)]
+        pay[pl.ds(TOK + HEAD_DIM, HEAD_DIM)] = pair_ref[...]
 
 
 def triangle(upper):
@@ -362,8 +361,8 @@
     return row <= col if upper else row >= col
 
 
-def decay_columns(decay_ref):
-    return dot(triangle(False).astype(F32), decay_ref[...], 1, 1, HIGHEST)
+def decay_columns(decay):
+    return dot(triangle(False).astype(F32), decay[...], 1, 1, HIGHEST)
 
 
 def log_pieces(log):
@@ -439,7 +438,7 @@
     same = chain_members(lines[0])[1]
     own_start = least([jnp.where(s > 0, k, 99) for s, k in zip(same, lines[0])])
     earlier = [flag(s < own_start) for s in starts]
-    result = jnp.zeros((HEAD_DIM, WIDTH), F32)
+    result = 0.0
     for o in range(NX):
         exponent = prefix
         for i in range(NX):
@@ -538,11 +537,11 @@
 
 
 def back_kernel(
-    group_ref, index_ref, log_ref, read_ref, core_ref, from_1, from_2, from_3, handed_ref, part_ref
+    group_ref, index_ref, log_ref, read_ref, pair_ref, from_1, from_2, from_3, handed_ref, part_ref
 ):
     logs = [log_ref[pl.ds(j, 1)] for j in range(LINE)]
     sources = [(read_ref, 0), (from_1, TOK), (from_2, TOK), (from_3, TOK)]
-    sources += [(core_ref, NY * TOK)]
+    sources += [(pair_ref, 0)]
     sources += [(ref, TOK + HEAD_DIM) for ref in (from_1, from_2, from_3)]
     states = [
         functools.partial(lambda ref, row: ref[pl.ds(row, HEAD_DIM)].astype(F32), ref, row)
@@ -647,19 +646,20 @@
         [
             shaped(2, NY, 8, TOK),
             shaped(NY, TOK, WIDTH),
-            shaped(NY * TOK + HEAD_DIM, WIDTH, dtype=BF16),
+            shaped(NY * TOK, WIDTH, dtype=BF16),
         ],
         2**22,
-        (part, chip, received[1], received[2], received[3], out_a, out_b, read_grad),
+        (part, chip, received[1], received[2], received[3], out_a, out_b),
     )
     from_core = fetch(theirs, "c", NC, 1)
+    pair_read = fetch(read_grad, "c", NC, 1)
 
     grads = far_backward(place, 0, 1, qa, qb, ga, gb, kvs[1:], stats)
     own_out, *pays = call(
         join_kernel,
         [rows] + [shaped(2 * TOK, WIDTH, dtype=BF16)] * 3,
         2**22,
-        (mine, from_core, read_grad),
+        (mine, from_core, read_grad, pair_read),
     )
     sent_out = {o: send(pays[o - 1], "y", NY, o) for o in OFFSETS}
     dq_a, dq_b, far_dkv = far_backward(place, 1, 2, qa, qb, ga, gb, kvs[1:], stats, tuple(grads))
@@ -671,7 +671,7 @@
         back_kernel,
         [shaped(HEAD_DIM, WIDTH, dtype=BF16), shaped(HEAD_DIM + 8, WIDTH)],
         2**24,
-        (*place, logs, read_grad, from_core, *(sent_out[NY - o] for o in (1, 2, 3))),
+        (*place, logs, read_grad, pair_read, *(sent_out[NY - o] for o in (1, 2, 3))),
         **placed(in_vmem(6), in_vmem(2)),
     )
     back_totals = [back_handed, *(fetch(back_handed, "x", NX, o) for o in (1, 2, 3))]
@@ -689,12 +689,13 @@
     soft_out = own_out
     for o in OFFSETS:
         soft_out = soft_out + sent_out[o][:TOK].astype(F32)
+    soft_out = soft_out.astype(BF16)
     dkv = near_dkv
     for sent in sent_dkv:
         dkv = dkv + sent.astype(F32)
+    soft_dk, soft_dv = dkv[0].astype(BF16), dkv[1].astype(BF16)
     return (
-        soft_out.astype(BF16), soft_dq.astype(BF16), dkv[0].astype(BF16), dkv[1].astype(BF16),
-        lin_out, lin_dq, lin_dk, lin_dv,
+        soft_out, soft_dq.astype(BF16), soft_dk, soft_dv, lin_out, lin_dq, lin_dk, lin_dv,
     )
 
 

time: 189 us -> 193 us (1.021)
  the two profiles are of different devices: /device:TPU:8 before, /device:TPU:1 now
where the time goes in v4:
time: 193 us; the launch traced here: 192 us
  waiting for transfers between devices  78.8 us (41%)
  starting transfers between devices  55.7 us (29%)
  Pallas kernels  49.1 us (25%)
  local copies, waits for them, and re-layouts  4.48 us (2%)
  other arithmetic  3.06 us (2%)
    ppermute x36, waiting for transfers between devices, send(): lax.ppermute(block, axis, [(i, (i + offset) % size) for i in range(size)])  78.8 us
    ppermute x36, starting transfers between devices, send(): lax.ppermute(block, axis, [(i, (i + offset) % size) for i in range(size)])  55.7 us
    pallas_call x15, Pallas kernels, call(): pl.pallas_call(kernel, out_shape=out_shape, cost_estimate=pl.CostEstimate...  49.1 us
  transfers between devices with their start and end apart: 36, of which 20 were waited for; matrix products, arithmetic and copies ran while one was open for 2% of the time, Pallas kernels for 10%

profile of v4, /device:TPU:1, one launch (start us, length us, event | category | flops | bytes accessed | tf_op | source)
XLA Modules:
  0.0 192.0 jit_solution(1622955749731257240)
XLA Ops:
  4.9 2.2 %collective-permute-start.2 = (bf16[400,384]{1,0:T(8,128)(2,1)S(1)}, bf16[400,384]{1,0:T(8,128)(2,1)S(1)}, u32[]{:S(2)}, u32[]{:S(2)}) collective-permute-start(bf16[400,384]{1,0:T(8,128)(2,1)S(1)} %shard_map.161), channel_id=1, source_target_pairs={{0,8},{8,16},{16,24},{24,0},{1,9},{9,17},{17,25},{25,1},{2,10},{10... | collective-permute-start | bytes 921608 | tf_op jit(solution)/shard_map/ppermute | solution.py:35
  7.1 2.6 %collective-permute-start.1 = (bf16[400,384]{1,0:T(8,128)(2,1)S(1)}, bf16[400,384]{1,0:T(8,128)(2,1)S(1)}, u32[]{:S(2)}, u32[]{:S(2)}) collective-permute-start(bf16[400,384]{1,0:T(8,128)(2,1)S(1)} %shard_map.161), channel_id=1, source_target_pairs={{0,16},{8,24},{16,0},{24,8},{1,17},{9,25},{17,1},{25,9},{2,18},{10... | collective-permute-start | bytes 921608 | tf_op jit(solution)/shard_map/ppermute | solution.py:35
  10.8 1.4 collective-permute-start.6
  12.3 3.2 %collective-permute-done.2 = bf16[400,384]{1,0:T(8,128)(2,1)S(1)} collective-permute-done((bf16[400,384]{1,0:T(8,128)(2,1)S(1)}, bf16[400,384]{1,0:T(8,128)(2,1)S(1)}, u32[]{:S(2)}, u32[]{:S(2)}) %collective-permute-start.2) | collective-permute-done | bytes 307232 | tf_op jit(solution)/shard_map/ppermute | solution.py:35
  15.4 1.6 collective-permute-start.5
  17.0 6.1 %collective-permute-done.1 = bf16[400,384]{1,0:T(8,128)(2,1)S(1)} collective-permute-done((bf16[400,384]{1,0:T(8,128)(2,1)S(1)}, bf16[400,384]{1,0:T(8,128)(2,1)S(1)}, u32[]{:S(2)}, u32[]{:S(2)}) %collective-permute-start.1) | collective-permute-done | bytes 307232 | tf_op jit(solution)/shard_map/ppermute | solution.py:35
  23.3 3.4 %collective-permute-start.3 = (bf16[4,400,384]{2,1,0:T(8,128)(2,1)S(1)}, bf16[4,400,384]{2,1,0:T(8,128)(2,1)S(1)}, u32[]{:S(2)}, u32[]{:S(2)}) collective-permute-start(bf16[4,400,384]{2,1,0:T(8,128)(2,1)S(1)} %pad_maximum_fusion.g_a.ga_ref), channel_id=1, source_target_pairs={{0,4},{4,0},{1,5},{5,1},{2,6},{6,2},{3,7},{7,3},{8,12},{12,8},{9,1... | collective-permute-start | bytes 3686408 | tf_op jit(solution)/shard_map/ppermute | solution.py:35
  27.3 4.1 %collective-permute-done.5 = bf16[256,384]{1,0:T(8,128)(2,1)S(1)} collective-permute-done((bf16[256,384]{1,0:T(8,128)(2,1)}, bf16[256,384]{1,0:T(8,128)(2,1)S(1)}, u32[]{:S(2)}, u32[]{:S(2)}) %collective-permute-start.5) | collective-permute-done | bytes 196640 | tf_op jit(solution)/shard_map/ppermute | solution.py:35
  31.6 1.6 collective-permute-start.10
  34.0 1.2 collective-permute-start.9
  35.2 2.5 %collective-permute-start.8 = (bf16[2,256,384]{2,1,0:T(8,128)(2,1)}, bf16[2,256,384]{2,1,0:T(8,128)(2,1)}, u32[]{:S(2)}, u32[]{:S(2)}) collective-permute-start(bf16[2,256,384]{2,1,0:T(8,128)(2,1)} %pad_maximum_fusion.2.kv_0.kv_ref), channel_id=1, source_target_pairs={{0,64},{32,96},{64,0},{96,32},{1,65},{33,97},{65,1},{97,33},{2,66}... | collective-permute-start | bytes 1179656 | tf_op jit(solution)/shard_map/ppermute | solution.py:35
  38.8 7.4 %collective-permute-done.9.kv_3 = bf16[2,256,384]{2,1,0:T(8,128)(2,1)} collective-permute-done((bf16[2,256,384]{2,1,0:T(8,128)(2,1)}, bf16[2,256,384]{2,1,0:T(8,128)(2,1)}, u32[]{:S(2)}, u32[]{:S(2)}) %collective-permute-start.9) | collective-permute-done | bytes 393248 | tf_op jit(solution)/shard_map/ppermute | solution.py:35
  46.2 9.4 %collective-permute-done.8.kv_2 = bf16[2,256,384]{2,1,0:T(8,128)(2,1)} collective-permute-done((bf16[2,256,384]{2,1,0:T(8,128)(2,1)}, bf16[2,256,384]{2,1,0:T(8,128)(2,1)}, u32[]{:S(2)}, u32[]{:S(2)}) %collective-permute-start.8) | collective-permute-done | bytes 393248 | tf_op jit(solution)/shard_map/ppermute | solution.py:35
  55.6 7.4 %shard_map.162 = (bf16[4,256,384]{2,1,0:T(8,128)(2,1)S(1)}, f32[4,8,256]{2,1,0:T(8,128)S(1)}) custom-call(s32[32]{0:T(128)S(1)} %copy-done.9, s32[1]{0:T(128)} %bitcast.5.index_ref, bf16[4,256,384]{2,1,0:T(8,128)(2,1)S(1)} %pad_maximum_fusion.1.q_ref.qa_ref, bf16[2,256,384]{2,1,0:T(8,128)(2,1)} %pad_maximum_fusion.2.kv_0.kv_ref, ...), custom_call_target="tpu_custom_call" | custom-call | flops 1610612736 | bytes 2097152 | tf_op jit(solution)/shard_map/pallas_call | solution.py:57
  63.0 7.4 %shard_map.163 = (bf16[4,256,384]{2,1,0:T(8,128)(2,1)S(1)}, f32[4,8,256]{2,1,0:T(8,128)S(1)}) custom-call(s32[32]{0:T(128)S(1)} %copy-done.9, s32[1]{0:T(128)} %bitcast.5.index_ref, bf16[4,256,384]{2,1,0:T(8,128)(2,1)} %collective-permute-done.10.q_ref.qb_ref, bf16[2,256,384]{2,1,0:T(8,128)(2,1)} %pad_maximum_fusion.2.kv_0.kv_ref, ...), custom_call_target="tpu_custom_call" | custom-call | flops 1610612736 | bytes 2097152 | tf_op jit(solution)/shard_map/pallas_call | solution.py:57
  70.4 1.7 shard_map.164.part_ref
  74.0 1.7 collective-permute-start.14
  75.7 1.4 collective-permute-start.13
  78.4 1.9 %collective-permute-done.13.from_2 = f32[2,4,8,256]{3,2,1,0:T(8,128)S(1)} collective-permute-done((f32[2,4,8,256]{3,2,1,0:T(8,128)S(1)}, f32[2,4,8,256]{3,2,1,0:T(8,128)S(1)}, u32[]{:S(2)}, u32[]{:S(2)}) %collective-permute-start.13) | collective-permute-done | bytes 65568 | tf_op jit(solution)/shard_map/ppermute | solution.py:35
  81.1 1.3 shard_map.166
  82.3 5.7 %shard_map.171 = (f32[4,3,128,256]{3,2,1,0:T(8,128)S(1)}, f32[4,3,128,256]{3,2,1,0:T(8,128)S(1)}, bf16[3,2,256,384]{3,2,1,0:T(8,128)(2,1)S(1)}) custom-call(s32[32]{0:T(128)S(1)} %copy-done.9, s32[1]{0:T(128)} %bitcast.5.index_ref, bf16[4,256,384]{2,1,0:T(8,128)(2,1)S(1)} %pad_maximum_fusion.1.q_ref.qa_ref, ...), custom_call_target="tpu_custom_call" | custom-call | flops 2013265920 | bytes 2097152 | tf_op jit(solution)/shard_map/pallas_call | solution.py:57
  88.0 9.9 %shard_map.172 = (f32[4,3,128,256]{3,2,1,0:T(8,128)S(1)}, f32[4,3,128,256]{3,2,1,0:T(8,128)S(1)}, bf16[3,2,256,384]{3,2,1,0:T(8,128)(2,1)S(1)}) custom-call(s32[32]{0:T(128)S(1)} %copy-done.9, s32[1]{0:T(128)} %bitcast.5.index_ref, ...), custom_call_target="tpu_custom_call", output_to_operand_aliasing={{0}: (10, {}), {1}: (11, {}), {2}: (12, {})} | custom-call | flops 4026531840 | bytes 2097152 | tf_op jit(solution)/shard_map/pallas_call | solution.py:57
  97.9 6.7 %shard_map.173 = (bf16[4,256,384]{2,1,0:T(8,128)(2,1)S(1)}, bf16[4,256,384]{2,1,0:T(8,128)(2,1)S(1)}, f32[2,256,384]{2,1,0:T(8,128)S(1)}) custom-call(s32[32]{0:T(128)S(1)} %copy-done.9, s32[1]{0:T(128)} %bitcast.5.index_ref, bf16[4,256,384]{2,1,0:T(8,128)(2,1)S(1)} %pad_maximum_fusion.1.q_ref.qa_ref, ...), custom_call_target="tpu_custom_call" | custom-call | flops 2013265920 | bytes 2097152 | tf_op jit(solution)/shard_map/pallas_call | solution.py:57
  104.7 1.3 collective-permute-start.26
  107.1 1.3 collective-permute-start.18
  108.5 2.1 %collective-permute-start.17 = (bf16[144,384]{1,0:T(8,128)(2,1)S(1)}, bf16[144,384]{1,0:T(8,128)(2,1)S(1)}, u32[]{:S(2)}, u32[]{:S(2)}) collective-permute-start(bf16[144,384]{1,0:T(8,128)(2,1)S(1)} %get-tuple-element.51.own), channel_id=1, source_target_pairs={{0,64},{32,96},{64,0},{96,32},{1,65},{33,97},{65,1},{97,33},{2,66}... | collective-permute-start | bytes 331784 | tf_op jit(solution)/shard_map/ppermute | solution.py:35
  110.6 1.3 collective-permute-start.16
  111.8 1.4 collective-permute-done.18.from_3
  113.2 2.9 %collective-permute-done.17.from_2 = bf16[144,384]{1,0:T(8,128)(2,1)S(1)} collective-permute-done((bf16[144,384]{1,0:T(8,128)(2,1)S(1)}, bf16[144,384]{1,0:T(8,128)(2,1)S(1)}, u32[]{:S(2)}, u32[]{:S(2)}) %collective-permute-start.17) | collective-permute-done | bytes 110624 | tf_op jit(solution)/shard_map/ppermute | solution.py:35
  116.1 1.7 shard_map.168
  117.8 1.7 collective-permute-start.21
  119.5 3.3 %collective-permute-start.20 = (f32[8,256]{1,0:T(8,128)S(1)}, f32[8,256]{1,0:T(8,128)S(1)}, u32[]{:S(2)}, u32[]{:S(2)}) collective-permute-start(f32[8,256]{1,0:T(8,128)S(1)} %get-tuple-element.54.sum_0), channel_id=1, source_target_pairs={{0,2},{1,3},{2,0},{3,1},{4,6},{5,7},{6,4},{7,5},{8,10},{9,11},{10,... | collective-permute-start | bytes 24584 | tf_op jit(solution)/shard_map/ppermute | solution.py:35
  123.9 1.7 collective-permute-done.19.sum_1
  125.6 2.2 %shard_map.169 = (f32[256,384]{1,0:T(8,128)}, f32[256,384]{1,0:T(8,128)}, f32[256,384]{1,0:T(8,128)S(1)}, f32[256,384]{1,0:T(8,128)S(1)}, bf16[128,384]{1,0:T(8,128)(2,1)S(1)}) custom-call(bf16[256,384]{1,0:T(8,128)(2,1)S(1)} %copy-done.4, bf16[256,384]{1,0:T(8,128)(2,1)S(1)} %copy-done.1, bf16[256,384]{1,0:T(8,128)(2,1)S(1)} %copy-done.3, ...), custom_call_target="tpu_custom_call" | custom-call | flops 268435456 | bytes 2097152 | tf_op jit(solution)/shard_map/pallas_call | solution.py:57
  127.8 2.4 %collective-permute-start.22 = (bf16[128,384]{1,0:T(8,128)(2,1)S(1)}, bf16[128,384]{1,0:T(8,128)(2,1)S(1)}, u32[]{:S(2)}, u32[]{:S(2)}) collective-permute-start(bf16[128,384]{1,0:T(8,128)(2,1)S(1)} %get-tuple-element.55.read_ref), channel_id=1, source_target_pairs={{0,4},{4,0},{1,5},{5,1},{2,6},{6,2},{3,7},{7,3},{8,12},{12,8},{9,1... | collective-permute-start | bytes 294920 | tf_op jit(solution)/shard_map/ppermute | solution.py:35
  130.3 1.5 collective-permute-start.30
  131.8 2.1 %collective-permute-start.32 = (bf16[2,256,384]{2,1,0:T(8,128)(2,1)S(1)}, bf16[2,256,384]{2,1,0:T(8,128)(2,1)S(1)}, u32[]{:S(2)}, u32[]{:S(2)}) collective-permute-start(bf16[2,256,384]{2,1,0:T(8,128)(2,1)S(1)} %get-tuple-element.83), channel_id=1, source_target_pairs={{0,64},{32,96},{64,0},{96,32},{1,65},{33,97},{65,1},{97,33},{2,66}... | collective-permute-start | bytes 1179656 | tf_op jit(solution)/shard_map/ppermute | solution.py:35
  135.1 6.6 %collective-permute-done.30 = bf16[2,256,384]{2,1,0:T(8,128)(2,1)S(1)} collective-permute-done((bf16[2,256,384]{2,1,0:T(8,128)(2,1)S(1)}, bf16[2,256,384]{2,1,0:T(8,128)(2,1)S(1)}, u32[]{:S(2)}, u32[]{:S(2)}) %collective-permute-start.30) | collective-permute-done | bytes 393248 | tf_op jit(solution)/shard_map/ppermute | solution.py:35
  142.6 8.4 %collective-permute-done.32 = bf16[2,256,384]{2,1,0:T(8,128)(2,1)S(1)} collective-permute-done((bf16[2,256,384]{2,1,0:T(8,128)(2,1)S(1)}, bf16[2,256,384]{2,1,0:T(8,128)(2,1)S(1)}, u32[]{:S(2)}, u32[]{:S(2)}) %collective-permute-start.32) | collective-permute-done | bytes 393248 | tf_op jit(solution)/shard_map/ppermute | solution.py:35
  152.5 1.8 collective-permute-start.24
  155.0 2.2 %collective-permute-start.29 = (bf16[256,384]{1,0:T(8,128)(2,1)S(1)}, bf16[256,384]{1,0:T(8,128)(2,1)S(1)}, u32[]{:S(2)}, u32[]{:S(2)}) collective-permute-start(bf16[256,384]{1,0:T(8,128)(2,1)S(1)} %get-tuple-element.86), channel_id=1, source_target_pairs={{0,16},{8,24},{16,0},{24,8},{1,17},{9,25},{17,1},{25,9},{2,18},{10... | collective-permute-start | bytes 589832 | tf_op jit(solution)/shard_map/ppermute | solution.py:35
  159.0 16.4 %collective-permute-done.29 = bf16[256,384]{1,0:T(8,128)(2,1)S(1)} collective-permute-done((bf16[256,384]{1,0:T(8,128)(2,1)S(1)}, bf16[256,384]{1,0:T(8,128)(2,1)S(1)}, u32[]{:S(2)}, u32[]{:S(2)}) %collective-permute-start.29) | collective-permute-done | bytes 196640 | tf_op jit(solution)/shard_map/ppermute | solution.py:35
  175.5 2.6 %collective-permute-done.28 = bf16[256,384]{1,0:T(8,128)(2,1)S(1)} collective-permute-done((bf16[256,384]{1,0:T(8,128)(2,1)S(1)}, bf16[256,384]{1,0:T(8,128)(2,1)S(1)}, u32[]{:S(2)}, u32[]{:S(2)}) %collective-permute-start.28) | collective-permute-done | bytes 196640 | tf_op jit(solution)/shard_map/ppermute | solution.py:35
  179.9 2.5 %collective-permute-start.35 = (bf16[128,384]{1,0:T(8,128)(2,1)S(1)}, bf16[128,384]{1,0:T(8,128)(2,1)S(1)}, u32[]{:S(2)}, u32[]{:S(2)}) collective-permute-start(bf16[128,384]{1,0:T(8,128)(2,1)S(1)} %get-tuple-element.75.own), channel_id=1, source_target_pairs={{0,32},{32,64},{64,96},{96,0},{1,33},{33,65},{65,97},{97,1},{2,34}... | collective-permute-start | bytes 294920 | tf_op jit(solution)/shard_map/ppermute | solution.py:35
  182.4 2.8 %collective-permute-start.34 = (bf16[128,384]{1,0:T(8,128)(2,1)S(1)}, bf16[128,384]{1,0:T(8,128)(2,1)S(1)}, u32[]{:S(2)}, u32[]{:S(2)}) collective-permute-start(bf16[128,384]{1,0:T(8,128)(2,1)S(1)} %get-tuple-element.75.own), channel_id=1, source_target_pairs={{0,64},{32,96},{64,0},{96,32},{1,65},{33,97},{65,1},{97,33},{2,66}... | collective-permute-start | bytes 294920 | tf_op jit(solution)/shard_map/ppermute | solution.py:35
  186.1 2.3 %collective-permute-done.34.from_2 = bf16[128,384]{1,0:T(8,128)(2,1)S(1)} collective-permute-done((bf16[128,384]{1,0:T(8,128)(2,1)S(1)}, bf16[128,384]{1,0:T(8,128)(2,1)S(1)}, u32[]{:S(2)}, u32[]{:S(2)}) %collective-permute-start.34) | collective-permute-done | bytes 98336 | tf_op jit(solution)/shard_map/ppermute | solution.py:35
  188.4 1.5 collective-permute-done.33.from_1
  190.0 2.0 %shard_map.175 = (f32[256,384]{1,0:T(8,128)}, f32[256,384]{1,0:T(8,128)}) custom-call(s32[32]{0:T(128)S(1)} %copy-done.9, s32[1]{0:T(128)} %bitcast.5.index_ref, bf16[256,384]{1,0:T(8,128)(2,1)S(1)} %copy-done.1, bf16[256,384]{1,0:T(8,128)(2,1)S(1)} %copy-done.3, f32[3,256]{1,0:T(4,128)S(1)} %bitcast.42, f32[136,384]{1,0:T(8,128)S(1)} %get-tuple-element.73.part_ref, ...), custom_call_target="tpu_custom_call" | custom-call | flops 67108864 | bytes 2097152 | tf_op jit(solution)/shard_map/pallas_call | solution.py:57
  (75 shorter events, 23.2 us)
Async XLA Ops:
  0.6 0.9 copy-start
  1.6 0.9 copy-start.2
  2.5 0.9 copy-start.6
  4.9 10.5 %collective-permute-start.2 = (bf16[400,384]{1,0:T(8,128)(2,1)S(1)}, bf16[400,384]{1,0:T(8,128)(2,1)S(1)}, u32[]{:S(2)}, u32[]{:S(2)}) collective-permute-start(bf16[400,384]{1,0:T(8,128)(2,1)S(1)} %shard_map.161), channel_id=1, source_target_pairs={{0,8},{8,16},{16,24},{24,0},{1,9},{9,17},{17,25},{25,1},{2,10},{10... | collective-permute-start | bytes 921608 | tf_op jit(solution)/shard_map/ppermute | solution.py:35
  7.1 15.9 %collective-permute-start.1 = (bf16[400,384]{1,0:T(8,128)(2,1)S(1)}, bf16[400,384]{1,0:T(8,128)(2,1)S(1)}, u32[]{:S(2)}, u32[]{:S(2)}) collective-permute-start(bf16[400,384]{1,0:T(8,128)(2,1)S(1)} %shard_map.161), channel_id=1, source_target_pairs={{0,16},{8,24},{16,0},{24,8},{1,17},{9,25},{17,1},{25,9},{2,18},{10... | collective-permute-start | bytes 921608 | tf_op jit(solution)/shard_map/ppermute | solution.py:35
  9.7 13.3 %collective-permute-start = (bf16[400,384]{1,0:T(8,128)(2,1)S(1)}, bf16[400,384]{1,0:T(8,128)(2,1)S(1)}, u32[]{:S(2)}, u32[]{:S(2)}) collective-permute-start(bf16[400,384]{1,0:T(8,128)(2,1)S(1)} %shard_map.161), channel_id=1, source_target_pairs={{0,24},{8,0},{16,8},{24,16},{1,25},{9,1},{17,9},{25,17},{2,26},{10... | collective-permute-start | bytes 921608 | tf_op jit(solution)/shard_map/ppermute | solution.py:35
  10.8 16.5 %collective-permute-start.4 = (bf16[256,384]{1,0:T(8,128)(2,1)}, bf16[256,384]{1,0:T(8,128)(2,1)S(1)}, u32[]{:S(2)}, u32[]{:S(2)}) collective-permute-start(bf16[256,384]{1,0:T(8,128)(2,1)} %param.11), channel_id=1, source_target_pairs={{0,24},{8,0},{16,8},{24,16},{1,25},{9,1},{17,9},{25,17},{2,26},{10... | collective-permute-start | bytes 589832 | tf_op jit(solution)/shard_map/ppermute | solution.py:35
  10.8 16.5 %collective-permute-start.6 = (bf16[256,384]{1,0:T(8,128)(2,1)}, bf16[256,384]{1,0:T(8,128)(2,1)S(1)}, u32[]{:S(2)}, u32[]{:S(2)}) collective-permute-start(bf16[256,384]{1,0:T(8,128)(2,1)} %param.11), channel_id=1, source_target_pairs={{0,8},{8,16},{16,24},{24,0},{1,9},{9,17},{17,25},{25,1},{2,10},{10... | collective-permute-start | bytes 589832 | tf_op jit(solution)/shard_map/ppermute | solution.py:35
  15.4 16.1 %collective-permute-start.5 = (bf16[256,384]{1,0:T(8,128)(2,1)}, bf16[256,384]{1,0:T(8,128)(2,1)S(1)}, u32[]{:S(2)}, u32[]{:S(2)}) collective-permute-start(bf16[256,384]{1,0:T(8,128)(2,1)} %param.11), channel_id=1, source_target_pairs={{0,16},{8,24},{16,0},{24,8},{1,17},{9,25},{17,1},{25,9},{2,18},{10... | collective-permute-start | bytes 589832 | tf_op jit(solution)/shard_map/ppermute | solution.py:35
  23.0 8.4 %copy-start.10 = (bf16[256,384]{1,0:T(8,128)(2,1)S(1)}, bf16[256,384]{1,0:T(8,128)(2,1)}, u32[]{:S(2)}) copy-start(bf16[256,384]{1,0:T(8,128)(2,1)} %param.11) | copy-start | bytes 589828
  23.2 10.0 %copy-start.11 = (bf16[256,384]{1,0:T(8,128)(2,1)S(1)}, bf16[256,384]{1,0:T(8,128)(2,1)}, u32[]{:S(2)}) copy-start(bf16[256,384]{1,0:T(8,128)(2,1)} %param.13) | copy-start | bytes 589828
  23.3 10.0 %copy-start.12 = (bf16[256,384]{1,0:T(8,128)(2,1)S(1)}, bf16[256,384]{1,0:T(8,128)(2,1)}, u32[]{:S(2)}) copy-start(bf16[256,384]{1,0:T(8,128)(2,1)} %param.12) | copy-start | bytes 589828
  23.3 32.3 %copy-start.9 = (s32[32]{0:T(128)S(1)}, s32[32]{0:T(128)}, u32[]{:S(2)}) copy-start(s32[32]{0:T(128)} %group_ref.17) | copy-start | bytes 388
  23.3 47.1 %collective-permute-start.3 = (bf16[4,400,384]{2,1,0:T(8,128)(2,1)S(1)}, bf16[4,400,384]{2,1,0:T(8,128)(2,1)S(1)}, u32[]{:S(2)}, u32[]{:S(2)}) collective-permute-start(bf16[4,400,384]{2,1,0:T(8,128)(2,1)S(1)} %pad_maximum_fusion.g_a.ga_ref), channel_id=1, source_target_pairs={{0,4},{4,0},{1,5},{5,1},{2,6},{6,2},{3,7},{7,3},{8,12},{12,8},{9,1... | collective-permute-start | bytes 3686408 | tf_op jit(solution)/shard_map/ppermute | solution.py:35
  31.6 31.4 %collective-permute-start.10 = (bf16[4,256,384]{2,1,0:T(8,128)(2,1)S(1)}, bf16[4,256,384]{2,1,0:T(8,128)(2,1)}, u32[]{:S(2)}, u32[]{:S(2)}) collective-permute-start(bf16[4,256,384]{2,1,0:T(8,128)(2,1)S(1)} %pad_maximum_fusion.1.q_ref.qa_ref), channel_id=1, source_target_pairs={{0,4},{4,0},{1,5},{5,1},{2,6},{6,2},{3,7},{7,3},{8,12},{12,8},{9,1... | collective-permute-start | bytes 2359304 | tf_op jit(solution)/shard_map/ppermute | solution.py:35
  34.0 12.2 %collective-permute-start.9 = (bf16[2,256,384]{2,1,0:T(8,128)(2,1)}, bf16[2,256,384]{2,1,0:T(8,128)(2,1)}, u32[]{:S(2)}, u32[]{:S(2)}) collective-permute-start(bf16[2,256,384]{2,1,0:T(8,128)(2,1)} %pad_maximum_fusion.2.kv_0.kv_ref), channel_id=1, source_target_pairs={{0,32},{32,64},{64,96},{96,0},{1,33},{33,65},{65,97},{97,1},{2,34}... | collective-permute-start | bytes 1179656 | tf_op jit(solution)/shard_map/ppermute | solution.py:35
  35.2 20.4 %collective-permute-start.8 = (bf16[2,256,384]{2,1,0:T(8,128)(2,1)}, bf16[2,256,384]{2,1,0:T(8,128)(2,1)}, u32[]{:S(2)}, u32[]{:S(2)}) collective-permute-start(bf16[2,256,384]{2,1,0:T(8,128)(2,1)} %pad_maximum_fusion.2.kv_0.kv_ref), channel_id=1, source_target_pairs={{0,64},{32,96},{64,0},{96,32},{1,65},{33,97},{65,1},{97,33},{2,66}... | collective-permute-start | bytes 1179656 | tf_op jit(solution)/shard_map/ppermute | solution.py:35
  37.7 17.9 %collective-permute-start.7 = (bf16[2,256,384]{2,1,0:T(8,128)(2,1)}, bf16[2,256,384]{2,1,0:T(8,128)(2,1)}, u32[]{:S(2)}, u32[]{:S(2)}) collective-permute-start(bf16[2,256,384]{2,1,0:T(8,128)(2,1)} %pad_maximum_fusion.2.kv_0.kv_ref), channel_id=1, source_target_pairs={{0,96},{32,0},{64,32},{96,64},{1,97},{33,1},{65,33},{97,65},{2,98}... | collective-permute-start | bytes 1179656 | tf_op jit(solution)/shard_map/ppermute | solution.py:35
  72.1 1.9 collective-permute-start.11
  74.0 4.4 %collective-permute-start.14 = (f32[2,4,8,256]{3,2,1,0:T(8,128)S(1)}, f32[2,4,8,256]{3,2,1,0:T(8,128)S(1)}, u32[]{:S(2)}, u32[]{:S(2)}) collective-permute-start(f32[2,4,8,256]{3,2,1,0:T(8,128)S(1)} %shard_map.165.chip_ref), channel_id=1, source_target_pairs={{0,8},{8,16},{16,24},{24,0},{1,9},{9,17},{17,25},{25,1},{2,10},{10... | collective-permute-start | bytes 196616 | tf_op jit(solution)/shard_map/ppermute | solution.py:35
  75.7 4.6 %collective-permute-start.13 = (f32[2,4,8,256]{3,2,1,0:T(8,128)S(1)}, f32[2,4,8,256]{3,2,1,0:T(8,128)S(1)}, u32[]{:S(2)}, u32[]{:S(2)}) collective-permute-start(f32[2,4,8,256]{3,2,1,0:T(8,128)S(1)} %shard_map.165.chip_ref), channel_id=1, source_target_pairs={{0,16},{8,24},{16,0},{24,8},{1,17},{9,25},{17,1},{25,9},{2,18},{10... | collective-permute-start | bytes 196616 | tf_op jit(solution)/shard_map/ppermute | solution.py:35
  77.1 3.9 %collective-permute-start.12 = (f32[2,4,8,256]{3,2,1,0:T(8,128)S(1)}, f32[2,4,8,256]{3,2,1,0:T(8,128)S(1)}, u32[]{:S(2)}, u32[]{:S(2)}) collective-permute-start(f32[2,4,8,256]{3,2,1,0:T(8,128)S(1)} %shard_map.165.chip_ref), channel_id=1, source_target_pairs={{0,24},{8,0},{16,8},{24,16},{1,25},{9,1},{17,9},{25,17},{2,26},{10... | collective-permute-start | bytes 196616 | tf_op jit(solution)/shard_map/ppermute | solution.py:35
  104.7 11.4 %copy-start.1 = (bf16[256,384]{1,0:T(8,128)(2,1)S(1)}, bf16[256,384]{1,0:T(8,128)(2,1)}, u32[]{:S(2)}) copy-start(bf16[256,384]{1,0:T(8,128)(2,1)} %k_ref.5) | copy-start | bytes 589828
  104.7 11.4 %copy-start.3 = (bf16[256,384]{1,0:T(8,128)(2,1)S(1)}, bf16[256,384]{1,0:T(8,128)(2,1)}, u32[]{:S(2)}) copy-start(bf16[256,384]{1,0:T(8,128)(2,1)} %v_ref.5) | copy-start | bytes 589828
  104.7 11.4 %copy-start.4 = (bf16[256,384]{1,0:T(8,128)(2,1)S(1)}, bf16[256,384]{1,0:T(8,128)(2,1)}, u32[]{:S(2)}) copy-start(bf16[256,384]{1,0:T(8,128)(2,1)} %q_ref.3) | copy-start | bytes 589828
  104.7 11.4 %copy-start.5 = (bf16[256,384]{1,0:T(8,128)(2,1)S(1)}, bf16[256,384]{1,0:T(8,128)(2,1)}, u32[]{:S(2)}) copy-start(bf16[256,384]{1,0:T(8,128)(2,1)} %g_ref.5) | copy-start | bytes 589828
  104.7 11.4 %copy-start.8 = (f32[256,3]{0,1:T(4,128)S(1)}, f32[256,3]{0,1:T(4,128)}, u32[]{:S(2)}) copy-start(f32[256,3]{0,1:T(4,128)} %param.18) | copy-start | bytes 9220
  104.7 29.2 %collective-permute-start.26 = (bf16[4,256,384]{2,1,0:T(8,128)(2,1)S(1)}, bf16[4,256,384]{2,1,0:T(8,128)(2,1)S(1)}, u32[]{:S(2)}, u32[]{:S(2)}) collective-permute-start(bf16[4,256,384]{2,1,0:T(8,128)(2,1)S(1)} %get-tuple-element.67), channel_id=1, source_target_pairs={{0,4},{4,0},{1,5},{5,1},{2,6},{6,2},{3,7},{7,3},{8,12},{12,8},{9,1... | collective-permute-start | bytes 2359304 | tf_op jit(solution)/shard_map/ppermute | solution.py:35
  107.1 6.1 %collective-permute-start.18 = (bf16[144,384]{1,0:T(8,128)(2,1)S(1)}, bf16[144,384]{1,0:T(8,128)(2,1)S(1)}, u32[]{:S(2)}, u32[]{:S(2)}) collective-permute-start(bf16[144,384]{1,0:T(8,128)(2,1)S(1)} %get-tuple-element.51.own), channel_id=1, source_target_pairs={{0,32},{32,64},{64,96},{96,0},{1,33},{33,65},{65,97},{97,1},{2,34}... | collective-permute-start | bytes 331784 | tf_op jit(solution)/shard_map/ppermute | solution.py:35
  108.5 7.6 %collective-permute-start.17 = (bf16[144,384]{1,0:T(8,128)(2,1)S(1)}, bf16[144,384]{1,0:T(8,128)(2,1)S(1)}, u32[]{:S(2)}, u32[]{:S(2)}) collective-permute-start(bf16[144,384]{1,0:T(8,128)(2,1)S(1)} %get-tuple-element.51.own), channel_id=1, source_target_pairs={{0,64},{32,96},{64,0},{96,32},{1,65},{33,97},{65,1},{97,33},{2,66}... | collective-permute-start | bytes 331784 | tf_op jit(solution)/shard_map/ppermute | solution.py:35
  110.6 5.5 %collective-permute-start.16 = (bf16[144,384]{1,0:T(8,128)(2,1)S(1)}, bf16[144,384]{1,0:T(8,128)(2,1)S(1)}, u32[]{:S(2)}, u32[]{:S(2)}) collective-permute-start(bf16[144,384]{1,0:T(8,128)(2,1)S(1)} %get-tuple-element.51.own), channel_id=1, source_target_pairs={{0,96},{32,0},{64,32},{96,64},{1,97},{33,1},{65,33},{97,65},{2,98}... | collective-permute-start | bytes 331784 | tf_op jit(solution)/shard_map/ppermute | solution.py:35
  117.8 5.7 %collective-permute-start.21 = (f32[8,256]{1,0:T(8,128)S(1)}, f32[8,256]{1,0:T(8,128)S(1)}, u32[]{:S(2)}, u32[]{:S(2)}) collective-permute-start(f32[8,256]{1,0:T(8,128)S(1)} %get-tuple-element.54.sum_0), channel_id=1, source_target_pairs={{0,1},{1,2},{2,3},{3,0},{4,5},{5,6},{6,7},{7,4},{8,9},{9,10},{10,1... | collective-permute-start | bytes 24584 | tf_op jit(solution)/shard_map/ppermute | solution.py:35
  119.5 4.4 %collective-permute-start.20 = (f32[8,256]{1,0:T(8,128)S(1)}, f32[8,256]{1,0:T(8,128)S(1)}, u32[]{:S(2)}, u32[]{:S(2)}) collective-permute-start(f32[8,256]{1,0:T(8,128)S(1)} %get-tuple-element.54.sum_0), channel_id=1, source_target_pairs={{0,2},{1,3},{2,0},{3,1},{4,6},{5,7},{6,4},{7,5},{8,10},{9,11},{10,... | collective-permute-start | bytes 24584 | tf_op jit(solution)/shard_map/ppermute | solution.py:35
  122.8 2.8 %collective-permute-start.19 = (f32[8,256]{1,0:T(8,128)S(1)}, f32[8,256]{1,0:T(8,128)S(1)}, u32[]{:S(2)}, u32[]{:S(2)}) collective-permute-start(f32[8,256]{1,0:T(8,128)S(1)} %get-tuple-element.54.sum_0), channel_id=1, source_target_pairs={{0,3},{1,0},{2,1},{3,2},{4,7},{5,4},{6,5},{7,6},{8,11},{9,8},{10,9... | collective-permute-start | bytes 24584 | tf_op jit(solution)/shard_map/ppermute | solution.py:35
  127.8 23.5 %collective-permute-start.22 = (bf16[128,384]{1,0:T(8,128)(2,1)S(1)}, bf16[128,384]{1,0:T(8,128)(2,1)S(1)}, u32[]{:S(2)}, u32[]{:S(2)}) collective-permute-start(bf16[128,384]{1,0:T(8,128)(2,1)S(1)} %get-tuple-element.55.read_ref), channel_id=1, source_target_pairs={{0,4},{4,0},{1,5},{5,1},{2,6},{6,2},{3,7},{7,3},{8,12},{12,8},{9,1... | collective-permute-start | bytes 294920 | tf_op jit(solution)/shard_map/ppermute | solution.py:35
  130.1 21.1 %collective-permute-start.15 = (bf16[1024,384]{1,0:T(8,128)(2,1)S(1)}, bf16[1024,384]{1,0:T(8,128)(2,1)S(1)}, u32[]{:S(2)}, u32[]{:S(2)}) collective-permute-start(bf16[1024,384]{1,0:T(8,128)(2,1)S(1)} %get-tuple-element.49), channel_id=1, source_target_pairs={{0,4},{4,0},{1,5},{5,1},{2,6},{6,2},{3,7},{7,3},{8,12},{12,8},{9,1... | collective-permute-start | bytes 2359304 | tf_op jit(solution)/shard_map/ppermute | solution.py:35
  130.3 11.4 %collective-permute-start.30 = (bf16[2,256,384]{2,1,0:T(8,128)(2,1)S(1)}, bf16[2,256,384]{2,1,0:T(8,128)(2,1)S(1)}, u32[]{:S(2)}, u32[]{:S(2)}) collective-permute-start(bf16[2,256,384]{2,1,0:T(8,128)(2,1)S(1)} %get-tuple-element.82), channel_id=1, source_target_pairs={{0,32},{32,64},{64,96},{96,0},{1,33},{33,65},{65,97},{97,1},{2,34}... | collective-permute-start | bytes 1179656 | tf_op jit(solution)/shard_map/ppermute | solution.py:35
  131.8 19.2 %collective-permute-start.32 = (bf16[2,256,384]{2,1,0:T(8,128)(2,1)S(1)}, bf16[2,256,384]{2,1,0:T(8,128)(2,1)S(1)}, u32[]{:S(2)}, u32[]{:S(2)}) collective-permute-start(bf16[2,256,384]{2,1,0:T(8,128)(2,1)S(1)} %get-tuple-element.83), channel_id=1, source_target_pairs={{0,64},{32,96},{64,0},{96,32},{1,65},{33,97},{65,1},{97,33},{2,66}... | collective-permute-start | bytes 1179656 | tf_op jit(solution)/shard_map/ppermute | solution.py:35
  133.9 17.1 %collective-permute-start.31 = (bf16[2,256,384]{2,1,0:T(8,128)(2,1)S(1)}, bf16[2,256,384]{2,1,0:T(8,128)(2,1)S(1)}, u32[]{:S(2)}, u32[]{:S(2)}) collective-permute-start(bf16[2,256,384]{2,1,0:T(8,128)(2,1)S(1)} %get-tuple-element.84), channel_id=1, source_target_pairs={{0,96},{32,0},{64,32},{96,64},{1,97},{33,1},{65,33},{97,65},{2,98}... | collective-permute-start | bytes 1179656 | tf_op jit(solution)/shard_map/ppermute | solution.py:35
  141.7 15.5 %collective-permute-start.27 = (bf16[256,384]{1,0:T(8,128)(2,1)S(1)}, bf16[256,384]{1,0:T(8,128)(2,1)S(1)}, u32[]{:S(2)}, u32[]{:S(2)}) collective-permute-start(bf16[256,384]{1,0:T(8,128)(2,1)S(1)} %get-tuple-element.85), channel_id=1, source_target_pairs={{0,8},{8,16},{16,24},{24,0},{1,9},{9,17},{17,25},{25,1},{2,10},{10... | collective-permute-start | bytes 589832 | tf_op jit(solution)/shard_map/ppermute | solution.py:35
  151.5 27.4 %collective-permute-start.23 = (bf16[512,384]{1,0:T(8,128)(2,1)S(1)}, bf16[512,384]{1,0:T(8,128)(2,1)S(1)}, u32[]{:S(2)}, u32[]{:S(2)}) collective-permute-start(bf16[512,384]{1,0:T(8,128)(2,1)S(1)} %get-tuple-element.57), channel_id=1, source_target_pairs={{0,8},{8,16},{16,24},{24,0},{1,9},{9,17},{17,25},{25,1},{2,10},{10... | collective-permute-start | bytes 1179656 | tf_op jit(solution)/shard_map/ppermute | solution.py:35
  152.5 26.4 %collective-permute-start.24 = (bf16[512,384]{1,0:T(8,128)(2,1)S(1)}, bf16[512,384]{1,0:T(8,128)(2,1)S(1)}, u32[]{:S(2)}, u32[]{:S(2)}) collective-permute-start(bf16[512,384]{1,0:T(8,128)(2,1)S(1)} %get-tuple-element.58), channel_id=1, source_target_pairs={{0,24},{8,0},{16,8},{24,16},{1,25},{9,1},{17,9},{25,17},{2,26},{10... | collective-permute-start | bytes 1179656 | tf_op jit(solution)/shard_map/ppermute | solution.py:35
  154.3 24.7 %collective-permute-start.25 = (bf16[512,384]{1,0:T(8,128)(2,1)S(1)}, bf16[512,384]{1,0:T(8,128)(2,1)S(1)}, u32[]{:S(2)}, u32[]{:S(2)}) collective-permute-start(bf16[512,384]{1,0:T(8,128)(2,1)S(1)} %get-tuple-element.59), channel_id=1, source_target_pairs={{0,16},{8,24},{16,0},{24,8},{1,17},{9,25},{17,1},{25,9},{2,18},{10... | collective-permute-start | bytes 1179656 | tf_op jit(solution)/shard_map/ppermute | solution.py:35
  155.0 20.5 %collective-permute-start.29 = (bf16[256,384]{1,0:T(8,128)(2,1)S(1)}, bf16[256,384]{1,0:T(8,128)(2,1)S(1)}, u32[]{:S(2)}, u32[]{:S(2)}) collective-permute-start(bf16[256,384]{1,0:T(8,128)(2,1)S(1)} %get-tuple-element.86), channel_id=1, source_target_pairs={{0,16},{8,24},{16,0},{24,8},{1,17},{9,25},{17,1},{25,9},{2,18},{10... | collective-permute-start | bytes 589832 | tf_op jit(solution)/shard_map/ppermute | solution.py:35
  157.2 20.9 %collective-permute-start.28 = (bf16[256,384]{1,0:T(8,128)(2,1)S(1)}, bf16[256,384]{1,0:T(8,128)(2,1)S(1)}, u32[]{:S(2)}, u32[]{:S(2)}) collective-permute-start(bf16[256,384]{1,0:T(8,128)(2,1)S(1)} %get-tuple-element.87), channel_id=1, source_target_pairs={{0,24},{8,0},{16,8},{24,16},{1,25},{9,1},{17,9},{25,17},{2,26},{10... | collective-permute-start | bytes 589832 | tf_op jit(solution)/shard_map/ppermute | solution.py:35
  179.9 6.2 %collective-permute-start.35 = (bf16[128,384]{1,0:T(8,128)(2,1)S(1)}, bf16[128,384]{1,0:T(8,128)(2,1)S(1)}, u32[]{:S(2)}, u32[]{:S(2)}) collective-permute-start(bf16[128,384]{1,0:T(8,128)(2,1)S(1)} %get-tuple-element.75.own), channel_id=1, source_target_pairs={{0,32},{32,64},{64,96},{96,0},{1,33},{33,65},{65,97},{97,1},{2,34}... | collective-permute-start | bytes 294920 | tf_op jit(solution)/shard_map/ppermute | solution.py:35
  182.4 6.0 %collective-permute-start.34 = (bf16[128,384]{1,0:T(8,128)(2,1)S(1)}, bf16[128,384]{1,0:T(8,128)(2,1)S(1)}, u32[]{:S(2)}, u32[]{:S(2)}) collective-permute-start(bf16[128,384]{1,0:T(8,128)(2,1)S(1)} %get-tuple-element.75.own), channel_id=1, source_target_pairs={{0,64},{32,96},{64,0},{96,32},{1,65},{33,97},{65,1},{97,33},{2,66}... | collective-permute-start | bytes 294920 | tf_op jit(solution)/shard_map/ppermute | solution.py:35
  185.3 4.7 %collective-permute-start.33 = (bf16[128,384]{1,0:T(8,128)(2,1)S(1)}, bf16[128,384]{1,0:T(8,128)(2,1)S(1)}, u32[]{:S(2)}, u32[]{:S(2)}) collective-permute-start(bf16[128,384]{1,0:T(8,128)(2,1)S(1)} %get-tuple-element.75.own), channel_id=1, source_target_pairs={{0,96},{32,0},{64,32},{96,64},{1,97},{33,1},{65,33},{97,65},{2,98}... | collective-permute-start | bytes 294920 | tf_op jit(solution)/shard_map/ppermute | solution.py:35
  (1 other events, 0.7 us)

commit v5 on v4

--- a/solution.py
+++ b/solution.py
@@ -103,18 +103,26 @@
         current = following
 
 
-def forward_kernel(
-    side, group_ref, index_ref, q_ref, kv_0, kv_1, kv_2, kv_3, out_ref, stat_ref, k_ref, vt_ref
-):
-    h = pl.program_id(0)
+def forward_a_kernel(
+    group_ref, index_ref, q_ref, kv_0, kv_1, kv_2, kv_3, out_ref, stat_ref, k_ref, vt_ref
+):
     for o, kv_ref in enumerate((kv_0, kv_1, kv_2, kv_3)):
         k_ref[pl.ds(o * TOK, TOK)] = kv_ref[0]
-        vt_ref[pl.ds(0, HEAD_DIM), pl.ds(o * TOK, TOK)] = kv_ref[1].T
+        vt_ref[0, pl.ds(0, HEAD_DIM), pl.ds(o * TOK, TOK)] = kv_ref[1].T
+    vt_ref[0, pl.ds(HEAD_DIM, 16)] = jnp.ones((16, NX * TOK), BF16)
+    forward_blocks(0, group_ref, index_ref, q_ref, k_ref, vt_ref, out_ref, stat_ref)
+
+
+def forward_b_kernel(group_ref, index_ref, q_ref, k_ref, vt_ref, out_ref, stat_ref):
+    forward_blocks(1, group_ref, index_ref, q_ref, k_ref, vt_ref, out_ref, stat_ref)
+
+
+def forward_blocks(side, group_ref, index_ref, q_ref, k_ref, vt_ref, out_ref, stat_ref):
+    h = pl.program_id(0)
 
     @pl.when(h == 0)
     def _():
         stat_ref[...] = jnp.zeros_like(stat_ref)
-        vt_ref[pl.ds(HEAD_DIM, 16)] = jnp.ones((16, NX * TOK), BF16)
 
     key_pos = [position(group_ref, index_ref, o, 0, 0) for o in range(NX)]
 
@@ -131,7 +139,7 @@
         probs = [
             jnp.exp2((s - (top + x)) * (SCALE * LOG2E)).astype(BF16) for s, x in zip(parts, hide)
         ]
-        acc = dot(vt_ref[...], jnp.concatenate(probs), 1, 0)
+        acc = dot(vt_ref[0], jnp.concatenate(probs), 1, 0)
         total = acc[HEAD_DIM : HEAD_DIM + 1]
         seen = top > 0.5 * NEG
         out_ref[i] = jnp.where(seen, acc[:HEAD_DIM] * (1.0 / total), 0.0).T.astype(BF16)
@@ -149,20 +157,20 @@
     return pl.BlockSpec((2, TOK, HEAD_DIM), lambda h, *_: (0, 0, h + first))
 
 
-def soft_forward(place, side, q, kvs):
+KEYS_SPEC = pl.BlockSpec((NX * TOK, HEAD_DIM), lambda h, *_: (0, h))
+TURNED_SPEC = pl.BlockSpec((1, HEAD_DIM + 16, NX * TOK), lambda h, *_: (h, 0, 0))
+
+
+def soft_forward(place, kernel, q, keys, key_specs, extra_shapes=(), extra_specs=()):
     return call(
-        functools.partial(forward_kernel, side),
-        [shaped(NY, TOK, WIDTH, dtype=BF16), shaped(NY, 8, TOK)],
+        kernel,
+        [shaped(NY, TOK, WIDTH, dtype=BF16), shaped(NY, 8, TOK), *extra_shapes],
         NY * NX * HEADS * 4 * TOK * TOK * HEAD_DIM,
-        (*place, q, *kvs),
+        (*place, q, *keys),
         **placed(
-            [rows_spec()] + [pair_spec()] * NX,
-            [rows_spec(), pl.BlockSpec((NY, 8, TOK), lambda h, *_: (0, 0, 0))],
-            [
-                pltpu.VMEM((NX * TOK, HEAD_DIM), BF16),
-                pltpu.VMEM((HEAD_DIM + 16, NX * TOK), BF16),
-            ],
-            (HEADS,),
+            [rows_spec(), *key_specs],
+            [rows_spec(), pl.BlockSpec((NY, 8, TOK), lambda h, *_: (0, 0, 0)), *extra_specs],
+            grid=(HEADS,),
         ),
     )
 
@@ -473,14 +481,23 @@
     return dot(decay_ref[...], triangle(True).astype(F32), 1, 0, HIGHEST)
 
 
-def inner_terms(q, k, rows, cumulative, h):
+def inner_decay(rows, cumulative, h):
     gap = cumulative[:, h : h + 1] - rows[h : h + 1]
-    decay = jnp.where(triangle(False), jnp.exp(jnp.minimum(gap, 0.0)), 0.0)
-    return decay, (dot(q, k, 1, 1) * decay).astype(BF16)
+    return jnp.where(triangle(False), jnp.exp(jnp.minimum(gap, 0.0)), 0.0)
+
+
+def local_kernel(q_ref, k_ref, v_ref, decay_ref, local_ref, score_ref):
+    cumulative, decay_in_rows = decay_columns(decay_ref), decay_rows(decay_ref)
+    for h in range(HEADS):
+        cols = head_cols(h)
+        decay = inner_decay(decay_in_rows, cumulative, h)
+        scores = (dot(q_ref[:, cols], k_ref[:, cols], 1, 1) * decay).astype(BF16)
+        score_ref[h] = scores
+        local_ref[:, cols] = dot(scores, v_ref[:, cols], 1, 0)
 
 
 def read_kernel(
-    group_ref, index_ref, q_ref, k_ref, v_ref, g_ref, decay_ref, part_ref, own, from_1, from_2,
+    group_ref, index_ref, q_ref, local_ref, g_ref, decay_ref, part_ref, own, from_1, from_2,
     from_3, raw_ref, sum_ref, entry_ref, log_ref,
 ):
     all_totals = (own, from_1, from_2, from_3)
@@ -493,15 +510,13 @@
         part_ref[pl.ds(HEAD_DIM, 1)],
     )
     entry_ref[...] = entry.astype(BF16)
-    cumulative, decay_in_rows = decay_columns(decay_ref), decay_rows(decay_ref)
+    cumulative = decay_columns(decay_ref)
     squares = jnp.zeros((TOK, 1), F32)
     inner = jnp.zeros((TOK, 1), F32)
     for h in range(HEADS):
         cols = head_cols(h)
-        q = q_ref[:, cols]
-        scores = inner_terms(q, k_ref[:, cols], decay_in_rows, cumulative, h)[1]
-        carried = dot(q, entry_ref[:, cols], 1, 0)
-        raw = dot(scores, v_ref[:, cols], 1, 0) + jnp.exp(cumulative[:, h : h + 1]) * carried
+        carried = dot(q_ref[:, cols], entry_ref[:, cols], 1, 0)
+        raw = local_ref[:, cols] + jnp.exp(cumulative[:, h : h + 1]) * carried
         raw_ref[:, cols] = raw
         squares = squares + jnp.sum(raw * raw, axis=1, keepdims=True)
         inner = inner + jnp.sum(raw * g_ref[:, cols].astype(F32), axis=1, keepdims=True)
@@ -511,7 +526,7 @@
 
 
 def grad_kernel(
-    q_ref, k_ref, v_ref, g_ref, decay_ref, entry_ref, raw_ref, sum_0, sum_1, sum_2, sum_3,
+    q_ref, k_ref, v_ref, g_ref, decay_ref, score_ref, entry_ref, raw_ref, sum_0, sum_1, sum_2, sum_3,
     out_ref, dq_ref, dk_ref, dv_ref, read_ref,
 ):
     cumulative, decay_in_rows = decay_columns(decay_ref), decay_rows(decay_ref)
@@ -525,13 +540,13 @@
         out = raw_ref[:, cols] * inverse
         out_ref[:, cols] = out
         raw_grad = ((g_ref[:, cols].astype(F32) - out * aligned) * inverse).astype(BF16)
-        decay, scores = inner_terms(q, k, decay_in_rows, cumulative, h)
+        decay = inner_decay(decay_in_rows, cumulative, h)
         head_decay = jnp.exp(cumulative[:, h : h + 1])
         inner_grad = (dot(raw_grad, v_ref[:, cols], 1, 1) * decay).astype(BF16)
         carried = dot(raw_grad, entry_ref[:, cols], 1, 1)
         dq_ref[:, cols] = dot(inner_grad, k, 1, 0) + head_decay * carried
         dk_ref[:, cols] = dot(inner_grad, q, 0, 0)
-        dv_ref[:, cols] = dot(scores, raw_grad, 0, 0)
+        dv_ref[:, cols] = dot(score_ref[h], raw_grad, 0, 0)
         scaled = (q.astype(F32) * head_decay).astype(BF16)
         read_ref[:, cols] = dot(scaled, raw_grad, 0, 0).astype(BF16)
 
@@ -599,7 +614,14 @@
     ga = jnp.stack([g_from[o] for o in range(NY)])
     gb = fetch(ga, "c", NC, 1)
 
-    out_a, stat_a = soft_forward(place, 0, qa, kvs)
+    out_a, stat_a, keys, values_turned = soft_forward(
+        place, forward_a_kernel, qa, kvs, [pair_spec()] * NX,
+        [
+            shaped(NX * TOK, WIDTH, dtype=BF16),
+            shaped(HEADS, HEAD_DIM + 16, NX * TOK, dtype=BF16),
+        ],
+        [KEYS_SPEC, TURNED_SPEC],
+    )
     handed, entry_part, logs = call(
         states_kernel,
         [
@@ -612,7 +634,9 @@
         **placed(in_vmem(2), in_vmem(3)),
     )
     totals = [handed, *(fetch(handed, "x", NX, o) for o in (1, 2, 3))]
-    out_b, stat_b = soft_forward(place, 1, qb, kvs)
+    out_b, stat_b = soft_forward(
+        place, forward_b_kernel, qb, (keys, values_turned), [KEYS_SPEC, TURNED_SPEC]
+    )
     part = call(
         delta_kernel,
         shaped(2, NY, 8, TOK),
@@ -625,12 +649,18 @@
     other = fetch(part, "c", NC, 1)
 
     rows = shaped(TOK, WIDTH)
+    local_out, inner_scores = call(
+        local_kernel,
+        [rows, shaped(HEADS, TOK, TOK, dtype=BF16)],
+        2**27,
+        (lin_query, lin_key, lin_value, decay),
+    )
     raw, sums, entry, line_logs = call(
         read_kernel,
         [rows, shaped(8, TOK), shaped(HEAD_DIM, WIDTH, dtype=BF16), shaped(8, WIDTH)],
         2**27,
-        (*place, lin_query, lin_key, lin_value, lin_grad, decay, entry_part, *totals),
-        **placed(in_vmem(10), in_vmem(4)),
+        (*place, lin_query, local_out, lin_grad, decay, entry_part, *totals),
+        **placed(in_vmem(9), in_vmem(4)),
     )
     all_sums = [sums, *(fetch(sums, "head", NZ, o) for o in (1, 2, 3))]
     chip = call(chip_kernel, shaped(2, NY, 8, TOK), 2**20, (part, other))
@@ -639,7 +669,7 @@
         grad_kernel,
         [rows] * 4 + [shaped(HEAD_DIM, WIDTH, dtype=BF16)],
         2**28,
-        (lin_query, lin_key, lin_value, lin_grad, decay, entry, raw, *all_sums),
+        (lin_query, lin_key, lin_value, lin_grad, decay, inner_scores, entry, raw, *all_sums),
     )
     stats, mine, theirs = call(
         line_kernel,

time: 193 us -> 192 us (level)
    pallas_call x15 -> x16, Pallas kernels: 49.1 us -> 49.3 us  [call(): pl.pallas_call(kernel, out_shape=out_shape, cost_estimate=pl.CostEstimate...]
  transfers between devices with their start and end apart: 36 -> 36, of which waited for: 20 -> 20; matrix products, arithmetic and copies ran while one was open for 2% -> 2% of each run, Pallas kernels for 10% -> 11%
where the time goes in v5:
time: 192 us; the launch traced here: 191 us
  waiting for transfers between devices  77.8 us (41%)
  starting transfers between devices  55.7 us (29%)
  Pallas kernels  49.3 us (26%)
  local copies, waits for them, and re-layouts  4.48 us (2%)
  other arithmetic  3.05 us (2%)
    ppermute x36, waiting for transfers between devices, send(): lax.ppermute(block, axis, [(i, (i + offset) % size) for i in range(size)])  77.8 us
    ppermute x36, starting transfers between devices, send(): lax.ppermute(block, axis, [(i, (i + offset) % size) for i in range(size)])  55.7 us
    pallas_call x16, Pallas kernels, call(): pl.pallas_call(kernel, out_shape=out_shape, cost_estimate=pl.CostEstimate...  49.3 us
  transfers between devices with their start and end apart: 36, of which 20 were waited for; matrix products, arithmetic and copies ran while one was open for 2% of the time, Pallas kernels for 11%

profile of v5, /device:TPU:1, one launch (start us, length us, event | category | flops | bytes accessed | tf_op | source)
XLA Modules:
  0.0 191.2 jit_solution(12449638679027801571)
XLA Ops:
  4.9 2.2 %collective-permute-start.2 = (bf16[400,384]{1,0:T(8,128)(2,1)S(1)}, bf16[400,384]{1,0:T(8,128)(2,1)S(1)}, u32[]{:S(2)}, u32[]{:S(2)}) collective-permute-start(bf16[400,384]{1,0:T(8,128)(2,1)S(1)} %shard_map.161), channel_id=1, source_target_pairs={{0,8},{8,16},{16,24},{24,0},{1,9},{9,17},{17,25},{25,1},{2,10},{10... | collective-permute-start | bytes 921608 | tf_op jit(solution)/shard_map/ppermute | solution.py:35
  7.1 2.6 %collective-permute-start.1 = (bf16[400,384]{1,0:T(8,128)(2,1)S(1)}, bf16[400,384]{1,0:T(8,128)(2,1)S(1)}, u32[]{:S(2)}, u32[]{:S(2)}) collective-permute-start(bf16[400,384]{1,0:T(8,128)(2,1)S(1)} %shard_map.161), channel_id=1, source_target_pairs={{0,16},{8,24},{16,0},{24,8},{1,17},{9,25},{17,1},{25,9},{2,18},{10... | collective-permute-start | bytes 921608 | tf_op jit(solution)/shard_map/ppermute | solution.py:35
  10.8 1.4 collective-permute-start.6
  12.3 3.2 %collective-permute-done.2 = bf16[400,384]{1,0:T(8,128)(2,1)S(1)} collective-permute-done((bf16[400,384]{1,0:T(8,128)(2,1)S(1)}, bf16[400,384]{1,0:T(8,128)(2,1)S(1)}, u32[]{:S(2)}, u32[]{:S(2)}) %collective-permute-start.2) | collective-permute-done | bytes 307232 | tf_op jit(solution)/shard_map/ppermute | solution.py:35
  15.4 1.6 collective-permute-start.5
  17.0 6.1 %collective-permute-done.1 = bf16[400,384]{1,0:T(8,128)(2,1)S(1)} collective-permute-done((bf16[400,384]{1,0:T(8,128)(2,1)S(1)}, bf16[400,384]{1,0:T(8,128)(2,1)S(1)}, u32[]{:S(2)}, u32[]{:S(2)}) %collective-permute-start.1) | collective-permute-done | bytes 307232 | tf_op jit(solution)/shard_map/ppermute | solution.py:35
  23.3 3.4 %collective-permute-start.3 = (bf16[4,400,384]{2,1,0:T(8,128)(2,1)S(1)}, bf16[4,400,384]{2,1,0:T(8,128)(2,1)S(1)}, u32[]{:S(2)}, u32[]{:S(2)}) collective-permute-start(bf16[4,400,384]{2,1,0:T(8,128)(2,1)S(1)} %pad_maximum_fusion.g_a.ga_ref), channel_id=1, source_target_pairs={{0,4},{4,0},{1,5},{5,1},{2,6},{6,2},{3,7},{7,3},{8,12},{12,8},{9,1... | collective-permute-start | bytes 3686408 | tf_op jit(solution)/shard_map/ppermute | solution.py:35
  27.3 4.1 %collective-permute-done.5 = bf16[256,384]{1,0:T(8,128)(2,1)S(1)} collective-permute-done((bf16[256,384]{1,0:T(8,128)(2,1)}, bf16[256,384]{1,0:T(8,128)(2,1)S(1)}, u32[]{:S(2)}, u32[]{:S(2)}) %collective-permute-start.5) | collective-permute-done | bytes 196640 | tf_op jit(solution)/shard_map/ppermute | solution.py:35
  31.6 1.6 collective-permute-start.10
  34.0 1.2 collective-permute-start.9
  35.2 2.5 %collective-permute-start.8 = (bf16[2,256,384]{2,1,0:T(8,128)(2,1)}, bf16[2,256,384]{2,1,0:T(8,128)(2,1)}, u32[]{:S(2)}, u32[]{:S(2)}) collective-permute-start(bf16[2,256,384]{2,1,0:T(8,128)(2,1)} %pad_maximum_fusion.2.kv_0.kv_ref), channel_id=1, source_target_pairs={{0,64},{32,96},{64,0},{96,32},{1,65},{33,97},{65,1},{97,33},{2,66}... | collective-permute-start | bytes 1179656 | tf_op jit(solution)/shard_map/ppermute | solution.py:35
  37.7 1.2 collective-permute-start.7
  38.8 7.4 %collective-permute-done.9.kv_3 = bf16[2,256,384]{2,1,0:T(8,128)(2,1)} collective-permute-done((bf16[2,256,384]{2,1,0:T(8,128)(2,1)}, bf16[2,256,384]{2,1,0:T(8,128)(2,1)}, u32[]{:S(2)}, u32[]{:S(2)}) %collective-permute-start.9) | collective-permute-done | bytes 393248 | tf_op jit(solution)/shard_map/ppermute | solution.py:35
  46.2 9.4 %collective-permute-done.8.kv_2 = bf16[2,256,384]{2,1,0:T(8,128)(2,1)} collective-permute-done((bf16[2,256,384]{2,1,0:T(8,128)(2,1)}, bf16[2,256,384]{2,1,0:T(8,128)(2,1)}, u32[]{:S(2)}, u32[]{:S(2)}) %collective-permute-start.8) | collective-permute-done | bytes 393248 | tf_op jit(solution)/shard_map/ppermute | solution.py:35
  55.6 7.6 %shard_map.162 = (bf16[4,256,384]{2,1,0:T(8,128)(2,1)S(1)}, f32[4,8,256]{2,1,0:T(8,128)S(1)}, bf16[1024,384]{1,0:T(8,128)(2,1)S(1)}, bf16[3,144,1024]{2,1,0:T(8,128)(2,1)S(1)}) custom-call(s32[32]{0:T(128)S(1)} %copy-done.9, s32[1]{0:T(128)} %bitcast.5.index_ref, bf16[4,256,384]{2,1,0:T(8,128)(2,1)S(1)} %pad_maximum_fusion.1.q_ref.qa_ref, ...), custom_call_target="tpu_custom_call" | custom-call | flops 1610612736 | bytes 2097152 | tf_op jit(solution)/shard_map/pallas_call | solution.py:57
  63.2 6.9 %shard_map.163 = (bf16[4,256,384]{2,1,0:T(8,128)(2,1)S(1)}, f32[4,8,256]{2,1,0:T(8,128)S(1)}) custom-call(s32[32]{0:T(128)S(1)} %copy-done.9, s32[1]{0:T(128)} %bitcast.5.index_ref, bf16[4,256,384]{2,1,0:T(8,128)(2,1)} %collective-permute-done.10.q_ref.qb_ref, bf16[1024,384]{1,0:T(8,128)(2,1)S(1)} %get-tuple-element.49.k_ref, ...), custom_call_target="tpu_custom_call" | custom-call | flops 1610612736 | bytes 2097152 | tf_op jit(solution)/shard_map/pallas_call | solution.py:57
  70.1 1.7 shard_map.164.part_ref
  73.7 1.7 collective-permute-start.14
  75.5 1.4 collective-permute-start.13
  78.1 2.0 %collective-permute-done.13.from_2 = f32[2,4,8,256]{3,2,1,0:T(8,128)S(1)} collective-permute-done((f32[2,4,8,256]{3,2,1,0:T(8,128)S(1)}, f32[2,4,8,256]{3,2,1,0:T(8,128)S(1)}, u32[]{:S(2)}, u32[]{:S(2)}) %collective-permute-start.13) | collective-permute-done | bytes 65568 | tf_op jit(solution)/shard_map/ppermute | solution.py:35
  80.8 1.3 shard_map.166
  82.1 5.7 %shard_map.172 = (f32[4,3,128,256]{3,2,1,0:T(8,128)S(1)}, f32[4,3,128,256]{3,2,1,0:T(8,128)S(1)}, bf16[3,2,256,384]{3,2,1,0:T(8,128)(2,1)S(1)}) custom-call(s32[32]{0:T(128)S(1)} %copy-done.9, s32[1]{0:T(128)} %bitcast.5.index_ref, bf16[4,256,384]{2,1,0:T(8,128)(2,1)S(1)} %pad_maximum_fusion.1.q_ref.qa_ref, ...), custom_call_target="tpu_custom_call" | custom-call | flops 2013265920 | bytes 2097152 | tf_op jit(solution)/shard_map/pallas_call | solution.py:57
  87.8 9.9 %shard_map.173 = (f32[4,3,128,256]{3,2,1,0:T(8,128)S(1)}, f32[4,3,128,256]{3,2,1,0:T(8,128)S(1)}, bf16[3,2,256,384]{3,2,1,0:T(8,128)(2,1)S(1)}) custom-call(s32[32]{0:T(128)S(1)} %copy-done.9, s32[1]{0:T(128)} %bitcast.5.index_ref, ...), custom_call_target="tpu_custom_call", output_to_operand_aliasing={{0}: (10, {}), {1}: (11, {}), {2}: (12, {})} | custom-call | flops 4026531840 | bytes 2097152 | tf_op jit(solution)/shard_map/pallas_call | solution.py:57
  97.7 6.7 %shard_map.174 = (bf16[4,256,384]{2,1,0:T(8,128)(2,1)S(1)}, bf16[4,256,384]{2,1,0:T(8,128)(2,1)S(1)}, f32[2,256,384]{2,1,0:T(8,128)S(1)}) custom-call(s32[32]{0:T(128)S(1)} %copy-done.9, s32[1]{0:T(128)} %bitcast.5.index_ref, bf16[4,256,384]{2,1,0:T(8,128)(2,1)S(1)} %pad_maximum_fusion.1.q_ref.qa_ref, ...), custom_call_target="tpu_custom_call" | custom-call | flops 2013265920 | bytes 2097152 | tf_op jit(solution)/shard_map/pallas_call | solution.py:57
  104.5 1.3 collective-permute-start.26
  106.9 1.3 collective-permute-start.18
  108.2 2.1 %collective-permute-start.17 = (bf16[144,384]{1,0:T(8,128)(2,1)S(1)}, bf16[144,384]{1,0:T(8,128)(2,1)S(1)}, u32[]{:S(2)}, u32[]{:S(2)}) collective-permute-start(bf16[144,384]{1,0:T(8,128)(2,1)S(1)} %get-tuple-element.59.own), channel_id=1, source_target_pairs={{0,64},{32,96},{64,0},{96,32},{1,65},{33,97},{65,1},{97,33},{2,66}... | collective-permute-start | bytes 331784 | tf_op jit(solution)/shard_map/ppermute | solution.py:35
  110.3 1.3 collective-permute-start.16
  113.0 2.9 %collective-permute-done.17.from_2 = bf16[144,384]{1,0:T(8,128)(2,1)S(1)} collective-permute-done((bf16[144,384]{1,0:T(8,128)(2,1)S(1)}, bf16[144,384]{1,0:T(8,128)(2,1)S(1)}, u32[]{:S(2)}, u32[]{:S(2)}) %collective-permute-start.17) | collective-permute-done | bytes 110624 | tf_op jit(solution)/shard_map/ppermute | solution.py:35
  115.8 1.4 shard_map.169
  117.2 1.7 collective-permute-start.21
  118.9 3.3 %collective-permute-start.20 = (f32[8,256]{1,0:T(8,128)S(1)}, f32[8,256]{1,0:T(8,128)S(1)}, u32[]{:S(2)}, u32[]{:S(2)}) collective-permute-start(f32[8,256]{1,0:T(8,128)S(1)} %get-tuple-element.62.sum_0), channel_id=1, source_target_pairs={{0,2},{1,3},{2,0},{3,1},{4,6},{5,7},{6,4},{7,5},{8,10},{9,11},{10,... | collective-permute-start | bytes 24584 | tf_op jit(solution)/shard_map/ppermute | solution.py:35
  123.3 1.7 collective-permute-done.19.sum_1
  125.0 2.0 %shard_map.170 = (f32[256,384]{1,0:T(8,128)}, f32[256,384]{1,0:T(8,128)}, f32[256,384]{1,0:T(8,128)S(1)}, f32[256,384]{1,0:T(8,128)S(1)}, bf16[128,384]{1,0:T(8,128)(2,1)S(1)}) custom-call(bf16[256,384]{1,0:T(8,128)(2,1)S(1)} %copy-done.4, bf16[256,384]{1,0:T(8,128)(2,1)S(1)} %copy-done.1, bf16[256,384]{1,0:T(8,128)(2,1)S(1)} %copy-done.3, ...), custom_call_target="tpu_custom_call" | custom-call | flops 268435456 | bytes 2097152 | tf_op jit(solution)/shard_map/pallas_call | solution.py:57
  127.0 2.4 %collective-permute-start.22 = (bf16[128,384]{1,0:T(8,128)(2,1)S(1)}, bf16[128,384]{1,0:T(8,128)(2,1)S(1)}, u32[]{:S(2)}, u32[]{:S(2)}) collective-permute-start(bf16[128,384]{1,0:T(8,128)(2,1)S(1)} %get-tuple-element.63.read_ref), channel_id=1, source_target_pairs={{0,4},{4,0},{1,5},{5,1},{2,6},{6,2},{3,7},{7,3},{8,12},{12,8},{9,1... | collective-permute-start | bytes 294920 | tf_op jit(solution)/shard_map/ppermute | solution.py:35
  129.5 1.5 collective-permute-start.30
  131.0 2.1 %collective-permute-start.32 = (bf16[2,256,384]{2,1,0:T(8,128)(2,1)S(1)}, bf16[2,256,384]{2,1,0:T(8,128)(2,1)S(1)}, u32[]{:S(2)}, u32[]{:S(2)}) collective-permute-start(bf16[2,256,384]{2,1,0:T(8,128)(2,1)S(1)} %get-tuple-element.91), channel_id=1, source_target_pairs={{0,64},{32,96},{64,0},{96,32},{1,65},{33,97},{65,1},{97,33},{2,66}... | collective-permute-start | bytes 1179656 | tf_op jit(solution)/shard_map/ppermute | solution.py:35
  134.3 6.6 %collective-permute-done.30 = bf16[2,256,384]{2,1,0:T(8,128)(2,1)S(1)} collective-permute-done((bf16[2,256,384]{2,1,0:T(8,128)(2,1)S(1)}, bf16[2,256,384]{2,1,0:T(8,128)(2,1)S(1)}, u32[]{:S(2)}, u32[]{:S(2)}) %collective-permute-start.30) | collective-permute-done | bytes 393248 | tf_op jit(solution)/shard_map/ppermute | solution.py:35
  141.9 8.4 %collective-permute-done.32 = bf16[2,256,384]{2,1,0:T(8,128)(2,1)S(1)} collective-permute-done((bf16[2,256,384]{2,1,0:T(8,128)(2,1)S(1)}, bf16[2,256,384]{2,1,0:T(8,128)(2,1)S(1)}, u32[]{:S(2)}, u32[]{:S(2)}) %collective-permute-start.32) | collective-permute-done | bytes 393248 | tf_op jit(solution)/shard_map/ppermute | solution.py:35
  151.7 1.7 collective-permute-start.24
  154.2 2.2 %collective-permute-start.29 = (bf16[256,384]{1,0:T(8,128)(2,1)S(1)}, bf16[256,384]{1,0:T(8,128)(2,1)S(1)}, u32[]{:S(2)}, u32[]{:S(2)}) collective-permute-start(bf16[256,384]{1,0:T(8,128)(2,1)S(1)} %get-tuple-element.94), channel_id=1, source_target_pairs={{0,16},{8,24},{16,0},{24,8},{1,17},{9,25},{17,1},{25,9},{2,18},{10... | collective-permute-start | bytes 589832 | tf_op jit(solution)/shard_map/ppermute | solution.py:35
  158.3 16.4 %collective-permute-done.29 = bf16[256,384]{1,0:T(8,128)(2,1)S(1)} collective-permute-done((bf16[256,384]{1,0:T(8,128)(2,1)S(1)}, bf16[256,384]{1,0:T(8,128)(2,1)S(1)}, u32[]{:S(2)}, u32[]{:S(2)}) %collective-permute-start.29) | collective-permute-done | bytes 196640 | tf_op jit(solution)/shard_map/ppermute | solution.py:35
  174.7 2.6 %collective-permute-done.28 = bf16[256,384]{1,0:T(8,128)(2,1)S(1)} collective-permute-done((bf16[256,384]{1,0:T(8,128)(2,1)S(1)}, bf16[256,384]{1,0:T(8,128)(2,1)S(1)}, u32[]{:S(2)}, u32[]{:S(2)}) %collective-permute-start.28) | collective-permute-done | bytes 196640 | tf_op jit(solution)/shard_map/ppermute | solution.py:35
  179.1 2.5 %collective-permute-start.35 = (bf16[128,384]{1,0:T(8,128)(2,1)S(1)}, bf16[128,384]{1,0:T(8,128)(2,1)S(1)}, u32[]{:S(2)}, u32[]{:S(2)}) collective-permute-start(bf16[128,384]{1,0:T(8,128)(2,1)S(1)} %get-tuple-element.83.own), channel_id=1, source_target_pairs={{0,32},{32,64},{64,96},{96,0},{1,33},{33,65},{65,97},{97,1},{2,34}... | collective-permute-start | bytes 294920 | tf_op jit(solution)/shard_map/ppermute | solution.py:35
  181.6 2.8 %collective-permute-start.34 = (bf16[128,384]{1,0:T(8,128)(2,1)S(1)}, bf16[128,384]{1,0:T(8,128)(2,1)S(1)}, u32[]{:S(2)}, u32[]{:S(2)}) collective-permute-start(bf16[128,384]{1,0:T(8,128)(2,1)S(1)} %get-tuple-element.83.own), channel_id=1, source_target_pairs={{0,64},{32,96},{64,0},{96,32},{1,65},{33,97},{65,1},{97,33},{2,66}... | collective-permute-start | bytes 294920 | tf_op jit(solution)/shard_map/ppermute | solution.py:35
  185.3 2.3 %collective-permute-done.34.from_2 = bf16[128,384]{1,0:T(8,128)(2,1)S(1)} collective-permute-done((bf16[128,384]{1,0:T(8,128)(2,1)S(1)}, bf16[128,384]{1,0:T(8,128)(2,1)S(1)}, u32[]{:S(2)}, u32[]{:S(2)}) %collective-permute-start.34) | collective-permute-done | bytes 98336 | tf_op jit(solution)/shard_map/ppermute | solution.py:35
  187.6 1.5 collective-permute-done.33.from_1
  189.2 2.0 %shard_map.176 = (f32[256,384]{1,0:T(8,128)}, f32[256,384]{1,0:T(8,128)}) custom-call(s32[32]{0:T(128)S(1)} %copy-done.9, s32[1]{0:T(128)} %bitcast.5.index_ref, bf16[256,384]{1,0:T(8,128)(2,1)S(1)} %copy-done.1, bf16[256,384]{1,0:T(8,128)(2,1)S(1)} %copy-done.3, f32[3,256]{1,0:T(4,128)S(1)} %bitcast.43, f32[136,384]{1,0:T(8,128)S(1)} %get-tuple-element.81.part_ref, ...), custom_call_target="tpu_custom_call" | custom-call | flops 67108864 | bytes 2097152 | tf_op jit(solution)/shard_map/pallas_call | solution.py:57
  (76 shorter events, 23.4 us)
Async XLA Ops:
  0.6 0.9 copy-start
  1.6 0.9 copy-start.2
  2.5 0.9 copy-start.6
  4.9 10.5 %collective-permute-start.2 = (bf16[400,384]{1,0:T(8,128)(2,1)S(1)}, bf16[400,384]{1,0:T(8,128)(2,1)S(1)}, u32[]{:S(2)}, u32[]{:S(2)}) collective-permute-start(bf16[400,384]{1,0:T(8,128)(2,1)S(1)} %shard_map.161), channel_id=1, source_target_pairs={{0,8},{8,16},{16,24},{24,0},{1,9},{9,17},{17,25},{25,1},{2,10},{10... | collective-permute-start | bytes 921608 | tf_op jit(solution)/shard_map/ppermute | solution.py:35
  7.1 15.9 %collective-permute-start.1 = (bf16[400,384]{1,0:T(8,128)(2,1)S(1)}, bf16[400,384]{1,0:T(8,128)(2,1)S(1)}, u32[]{:S(2)}, u32[]{:S(2)}) collective-permute-start(bf16[400,384]{1,0:T(8,128)(2,1)S(1)} %shard_map.161), channel_id=1, source_target_pairs={{0,16},{8,24},{16,0},{24,8},{1,17},{9,25},{17,1},{25,9},{2,18},{10... | collective-permute-start | bytes 921608 | tf_op jit(solution)/shard_map/ppermute | solution.py:35
  9.7 13.3 %collective-permute-start = (bf16[400,384]{1,0:T(8,128)(2,1)S(1)}, bf16[400,384]{1,0:T(8,128)(2,1)S(1)}, u32[]{:S(2)}, u32[]{:S(2)}) collective-permute-start(bf16[400,384]{1,0:T(8,128)(2,1)S(1)} %shard_map.161), channel_id=1, source_target_pairs={{0,24},{8,0},{16,8},{24,16},{1,25},{9,1},{17,9},{25,17},{2,26},{10... | collective-permute-start | bytes 921608 | tf_op jit(solution)/shard_map/ppermute | solution.py:35
  10.8 16.5 %collective-permute-start.4 = (bf16[256,384]{1,0:T(8,128)(2,1)}, bf16[256,384]{1,0:T(8,128)(2,1)S(1)}, u32[]{:S(2)}, u32[]{:S(2)}) collective-permute-start(bf16[256,384]{1,0:T(8,128)(2,1)} %param.11), channel_id=1, source_target_pairs={{0,24},{8,0},{16,8},{24,16},{1,25},{9,1},{17,9},{25,17},{2,26},{10... | collective-permute-start | bytes 589832 | tf_op jit(solution)/shard_map/ppermute | solution.py:35
  10.8 16.5 %collective-permute-start.6 = (bf16[256,384]{1,0:T(8,128)(2,1)}, bf16[256,384]{1,0:T(8,128)(2,1)S(1)}, u32[]{:S(2)}, u32[]{:S(2)}) collective-permute-start(bf16[256,384]{1,0:T(8,128)(2,1)} %param.11), channel_id=1, source_target_pairs={{0,8},{8,16},{16,24},{24,0},{1,9},{9,17},{17,25},{25,1},{2,10},{10... | collective-permute-start | bytes 589832 | tf_op jit(solution)/shard_map/ppermute | solution.py:35
  15.4 16.1 %collective-permute-start.5 = (bf16[256,384]{1,0:T(8,128)(2,1)}, bf16[256,384]{1,0:T(8,128)(2,1)S(1)}, u32[]{:S(2)}, u32[]{:S(2)}) collective-permute-start(bf16[256,384]{1,0:T(8,128)(2,1)} %param.11), channel_id=1, source_target_pairs={{0,16},{8,24},{16,0},{24,8},{1,17},{9,25},{17,1},{25,9},{2,18},{10... | collective-permute-start | bytes 589832 | tf_op jit(solution)/shard_map/ppermute | solution.py:35
  23.0 8.4 %copy-start.10 = (bf16[256,384]{1,0:T(8,128)(2,1)S(1)}, bf16[256,384]{1,0:T(8,128)(2,1)}, u32[]{:S(2)}) copy-start(bf16[256,384]{1,0:T(8,128)(2,1)} %param.11) | copy-start | bytes 589828
  23.2 10.0 %copy-start.11 = (bf16[256,384]{1,0:T(8,128)(2,1)S(1)}, bf16[256,384]{1,0:T(8,128)(2,1)}, u32[]{:S(2)}) copy-start(bf16[256,384]{1,0:T(8,128)(2,1)} %param.13) | copy-start | bytes 589828
  23.3 10.0 %copy-start.12 = (bf16[256,384]{1,0:T(8,128)(2,1)S(1)}, bf16[256,384]{1,0:T(8,128)(2,1)}, u32[]{:S(2)}) copy-start(bf16[256,384]{1,0:T(8,128)(2,1)} %param.12) | copy-start | bytes 589828
  23.3 32.3 %copy-start.9 = (s32[32]{0:T(128)S(1)}, s32[32]{0:T(128)}, u32[]{:S(2)}) copy-start(s32[32]{0:T(128)} %group_ref.17) | copy-start | bytes 388
  23.3 46.9 %collective-permute-start.3 = (bf16[4,400,384]{2,1,0:T(8,128)(2,1)S(1)}, bf16[4,400,384]{2,1,0:T(8,128)(2,1)S(1)}, u32[]{:S(2)}, u32[]{:S(2)}) collective-permute-start(bf16[4,400,384]{2,1,0:T(8,128)(2,1)S(1)} %pad_maximum_fusion.g_a.ga_ref), channel_id=1, source_target_pairs={{0,4},{4,0},{1,5},{5,1},{2,6},{6,2},{3,7},{7,3},{8,12},{12,8},{9,1... | collective-permute-start | bytes 3686408 | tf_op jit(solution)/shard_map/ppermute | solution.py:35
  31.6 31.6 %collective-permute-start.10 = (bf16[4,256,384]{2,1,0:T(8,128)(2,1)S(1)}, bf16[4,256,384]{2,1,0:T(8,128)(2,1)}, u32[]{:S(2)}, u32[]{:S(2)}) collective-permute-start(bf16[4,256,384]{2,1,0:T(8,128)(2,1)S(1)} %pad_maximum_fusion.1.q_ref.qa_ref), channel_id=1, source_target_pairs={{0,4},{4,0},{1,5},{5,1},{2,6},{6,2},{3,7},{7,3},{8,12},{12,8},{9,1... | collective-permute-start | bytes 2359304 | tf_op jit(solution)/shard_map/ppermute | solution.py:35
  34.0 12.2 %collective-permute-start.9 = (bf16[2,256,384]{2,1,0:T(8,128)(2,1)}, bf16[2,256,384]{2,1,0:T(8,128)(2,1)}, u32[]{:S(2)}, u32[]{:S(2)}) collective-permute-start(bf16[2,256,384]{2,1,0:T(8,128)(2,1)} %pad_maximum_fusion.2.kv_0.kv_ref), channel_id=1, source_target_pairs={{0,32},{32,64},{64,96},{96,0},{1,33},{33,65},{65,97},{97,1},{2,34}... | collective-permute-start | bytes 1179656 | tf_op jit(solution)/shard_map/ppermute | solution.py:35
  35.2 20.4 %collective-permute-start.8 = (bf16[2,256,384]{2,1,0:T(8,128)(2,1)}, bf16[2,256,384]{2,1,0:T(8,128)(2,1)}, u32[]{:S(2)}, u32[]{:S(2)}) collective-permute-start(bf16[2,256,384]{2,1,0:T(8,128)(2,1)} %pad_maximum_fusion.2.kv_0.kv_ref), channel_id=1, source_target_pairs={{0,64},{32,96},{64,0},{96,32},{1,65},{33,97},{65,1},{97,33},{2,66}... | collective-permute-start | bytes 1179656 | tf_op jit(solution)/shard_map/ppermute | solution.py:35
  37.7 17.9 %collective-permute-start.7 = (bf16[2,256,384]{2,1,0:T(8,128)(2,1)}, bf16[2,256,384]{2,1,0:T(8,128)(2,1)}, u32[]{:S(2)}, u32[]{:S(2)}) collective-permute-start(bf16[2,256,384]{2,1,0:T(8,128)(2,1)} %pad_maximum_fusion.2.kv_0.kv_ref), channel_id=1, source_target_pairs={{0,96},{32,0},{64,32},{96,64},{1,97},{33,1},{65,33},{97,65},{2,98}... | collective-permute-start | bytes 1179656 | tf_op jit(solution)/shard_map/ppermute | solution.py:35
  71.8 1.9 collective-permute-start.11
  73.7 4.4 %collective-permute-start.14 = (f32[2,4,8,256]{3,2,1,0:T(8,128)S(1)}, f32[2,4,8,256]{3,2,1,0:T(8,128)S(1)}, u32[]{:S(2)}, u32[]{:S(2)}) collective-permute-start(f32[2,4,8,256]{3,2,1,0:T(8,128)S(1)} %shard_map.165.chip_ref), channel_id=1, source_target_pairs={{0,8},{8,16},{16,24},{24,0},{1,9},{9,17},{17,25},{25,1},{2,10},{10... | collective-permute-start | bytes 196616 | tf_op jit(solution)/shard_map/ppermute | solution.py:35
  75.5 4.6 %collective-permute-start.13 = (f32[2,4,8,256]{3,2,1,0:T(8,128)S(1)}, f32[2,4,8,256]{3,2,1,0:T(8,128)S(1)}, u32[]{:S(2)}, u32[]{:S(2)}) collective-permute-start(f32[2,4,8,256]{3,2,1,0:T(8,128)S(1)} %shard_map.165.chip_ref), channel_id=1, source_target_pairs={{0,16},{8,24},{16,0},{24,8},{1,17},{9,25},{17,1},{25,9},{2,18},{10... | collective-permute-start | bytes 196616 | tf_op jit(solution)/shard_map/ppermute | solution.py:35
  76.9 3.9 %collective-permute-start.12 = (f32[2,4,8,256]{3,2,1,0:T(8,128)S(1)}, f32[2,4,8,256]{3,2,1,0:T(8,128)S(1)}, u32[]{:S(2)}, u32[]{:S(2)}) collective-permute-start(f32[2,4,8,256]{3,2,1,0:T(8,128)S(1)} %shard_map.165.chip_ref), channel_id=1, source_target_pairs={{0,24},{8,0},{16,8},{24,16},{1,25},{9,1},{17,9},{25,17},{2,26},{10... | collective-permute-start | bytes 196616 | tf_op jit(solution)/shard_map/ppermute | solution.py:35
  104.4 7.2 %copy-start.1 = (bf16[256,384]{1,0:T(8,128)(2,1)S(1)}, bf16[256,384]{1,0:T(8,128)(2,1)}, u32[]{:S(2)}) copy-start(bf16[256,384]{1,0:T(8,128)(2,1)} %k_ref.5) | copy-start | bytes 589828
  104.4 7.2 %copy-start.3 = (bf16[256,384]{1,0:T(8,128)(2,1)S(1)}, bf16[256,384]{1,0:T(8,128)(2,1)}, u32[]{:S(2)}) copy-start(bf16[256,384]{1,0:T(8,128)(2,1)} %v_ref.5) | copy-start | bytes 589828
  104.4 7.2 %copy-start.4 = (bf16[256,384]{1,0:T(8,128)(2,1)S(1)}, bf16[256,384]{1,0:T(8,128)(2,1)}, u32[]{:S(2)}) copy-start(bf16[256,384]{1,0:T(8,128)(2,1)} %q_ref.5) | copy-start | bytes 589828
  104.5 7.2 %copy-start.8 = (f32[256,3]{0,1:T(4,128)S(1)}, f32[256,3]{0,1:T(4,128)}, u32[]{:S(2)}) copy-start(f32[256,3]{0,1:T(4,128)} %param.18) | copy-start | bytes 9220
  104.5 11.4 %copy-start.5 = (bf16[256,384]{1,0:T(8,128)(2,1)S(1)}, bf16[256,384]{1,0:T(8,128)(2,1)}, u32[]{:S(2)}) copy-start(bf16[256,384]{1,0:T(8,128)(2,1)} %g_ref.5) | copy-start | bytes 589828
  104.5 28.7 %collective-permute-start.26 = (bf16[4,256,384]{2,1,0:T(8,128)(2,1)S(1)}, bf16[4,256,384]{2,1,0:T(8,128)(2,1)S(1)}, u32[]{:S(2)}, u32[]{:S(2)}) collective-permute-start(bf16[4,256,384]{2,1,0:T(8,128)(2,1)S(1)} %get-tuple-element.75), channel_id=1, source_target_pairs={{0,4},{4,0},{1,5},{5,1},{2,6},{6,2},{3,7},{7,3},{8,12},{12,8},{9,1... | collective-permute-start | bytes 2359304 | tf_op jit(solution)/shard_map/ppermute | solution.py:35
  106.9 6.1 %collective-permute-start.18 = (bf16[144,384]{1,0:T(8,128)(2,1)S(1)}, bf16[144,384]{1,0:T(8,128)(2,1)S(1)}, u32[]{:S(2)}, u32[]{:S(2)}) collective-permute-start(bf16[144,384]{1,0:T(8,128)(2,1)S(1)} %get-tuple-element.59.own), channel_id=1, source_target_pairs={{0,32},{32,64},{64,96},{96,0},{1,33},{33,65},{65,97},{97,1},{2,34}... | collective-permute-start | bytes 331784 | tf_op jit(solution)/shard_map/ppermute | solution.py:35
  108.2 7.6 %collective-permute-start.17 = (bf16[144,384]{1,0:T(8,128)(2,1)S(1)}, bf16[144,384]{1,0:T(8,128)(2,1)S(1)}, u32[]{:S(2)}, u32[]{:S(2)}) collective-permute-start(bf16[144,384]{1,0:T(8,128)(2,1)S(1)} %get-tuple-element.59.own), channel_id=1, source_target_pairs={{0,64},{32,96},{64,0},{96,32},{1,65},{33,97},{65,1},{97,33},{2,66}... | collective-permute-start | bytes 331784 | tf_op jit(solution)/shard_map/ppermute | solution.py:35
  110.3 5.5 %collective-permute-start.16 = (bf16[144,384]{1,0:T(8,128)(2,1)S(1)}, bf16[144,384]{1,0:T(8,128)(2,1)S(1)}, u32[]{:S(2)}, u32[]{:S(2)}) collective-permute-start(bf16[144,384]{1,0:T(8,128)(2,1)S(1)} %get-tuple-element.59.own), channel_id=1, source_target_pairs={{0,96},{32,0},{64,32},{96,64},{1,97},{33,1},{65,33},{97,65},{2,98}... | collective-permute-start | bytes 331784 | tf_op jit(solution)/shard_map/ppermute | solution.py:35
  117.2 5.7 %collective-permute-start.21 = (f32[8,256]{1,0:T(8,128)S(1)}, f32[8,256]{1,0:T(8,128)S(1)}, u32[]{:S(2)}, u32[]{:S(2)}) collective-permute-start(f32[8,256]{1,0:T(8,128)S(1)} %get-tuple-element.62.sum_0), channel_id=1, source_target_pairs={{0,1},{1,2},{2,3},{3,0},{4,5},{5,6},{6,7},{7,4},{8,9},{9,10},{10,1... | collective-permute-start | bytes 24584 | tf_op jit(solution)/shard_map/ppermute | solution.py:35
  118.9 4.4 %collective-permute-start.20 = (f32[8,256]{1,0:T(8,128)S(1)}, f32[8,256]{1,0:T(8,128)S(1)}, u32[]{:S(2)}, u32[]{:S(2)}) collective-permute-start(f32[8,256]{1,0:T(8,128)S(1)} %get-tuple-element.62.sum_0), channel_id=1, source_target_pairs={{0,2},{1,3},{2,0},{3,1},{4,6},{5,7},{6,4},{7,5},{8,10},{9,11},{10,... | collective-permute-start | bytes 24584 | tf_op jit(solution)/shard_map/ppermute | solution.py:35
  122.2 2.8 %collective-permute-start.19 = (f32[8,256]{1,0:T(8,128)S(1)}, f32[8,256]{1,0:T(8,128)S(1)}, u32[]{:S(2)}, u32[]{:S(2)}) collective-permute-start(f32[8,256]{1,0:T(8,128)S(1)} %get-tuple-element.62.sum_0), channel_id=1, source_target_pairs={{0,3},{1,0},{2,1},{3,2},{4,7},{5,4},{6,5},{7,6},{8,11},{9,8},{10,9... | collective-permute-start | bytes 24584 | tf_op jit(solution)/shard_map/ppermute | solution.py:35
  127.0 23.5 %collective-permute-start.22 = (bf16[128,384]{1,0:T(8,128)(2,1)S(1)}, bf16[128,384]{1,0:T(8,128)(2,1)S(1)}, u32[]{:S(2)}, u32[]{:S(2)}) collective-permute-start(bf16[128,384]{1,0:T(8,128)(2,1)S(1)} %get-tuple-element.63.read_ref), channel_id=1, source_target_pairs={{0,4},{4,0},{1,5},{5,1},{2,6},{6,2},{3,7},{7,3},{8,12},{12,8},{9,1... | collective-permute-start | bytes 294920 | tf_op jit(solution)/shard_map/ppermute | solution.py:35
  129.4 21.1 %collective-permute-start.15 = (bf16[1024,384]{1,0:T(8,128)(2,1)S(1)}, bf16[1024,384]{1,0:T(8,128)(2,1)S(1)}, u32[]{:S(2)}, u32[]{:S(2)}) collective-permute-start(bf16[1024,384]{1,0:T(8,128)(2,1)S(1)} %get-tuple-element.55), channel_id=1, source_target_pairs={{0,4},{4,0},{1,5},{5,1},{2,6},{6,2},{3,7},{7,3},{8,12},{12,8},{9,1... | collective-permute-start | bytes 2359304 | tf_op jit(solution)/shard_map/ppermute | solution.py:35
  129.5 11.4 %collective-permute-start.30 = (bf16[2,256,384]{2,1,0:T(8,128)(2,1)S(1)}, bf16[2,256,384]{2,1,0:T(8,128)(2,1)S(1)}, u32[]{:S(2)}, u32[]{:S(2)}) collective-permute-start(bf16[2,256,384]{2,1,0:T(8,128)(2,1)S(1)} %get-tuple-element.90), channel_id=1, source_target_pairs={{0,32},{32,64},{64,96},{96,0},{1,33},{33,65},{65,97},{97,1},{2,34}... | collective-permute-start | bytes 1179656 | tf_op jit(solution)/shard_map/ppermute | solution.py:35
  131.0 19.2 %collective-permute-start.32 = (bf16[2,256,384]{2,1,0:T(8,128)(2,1)S(1)}, bf16[2,256,384]{2,1,0:T(8,128)(2,1)S(1)}, u32[]{:S(2)}, u32[]{:S(2)}) collective-permute-start(bf16[2,256,384]{2,1,0:T(8,128)(2,1)S(1)} %get-tuple-element.91), channel_id=1, source_target_pairs={{0,64},{32,96},{64,0},{96,32},{1,65},{33,97},{65,1},{97,33},{2,66}... | collective-permute-start | bytes 1179656 | tf_op jit(solution)/shard_map/ppermute | solution.py:35
  133.1 17.1 %collective-permute-start.31 = (bf16[2,256,384]{2,1,0:T(8,128)(2,1)S(1)}, bf16[2,256,384]{2,1,0:T(8,128)(2,1)S(1)}, u32[]{:S(2)}, u32[]{:S(2)}) collective-permute-start(bf16[2,256,384]{2,1,0:T(8,128)(2,1)S(1)} %get-tuple-element.92), channel_id=1, source_target_pairs={{0,96},{32,0},{64,32},{96,64},{1,97},{33,1},{65,33},{97,65},{2,98}... | collective-permute-start | bytes 1179656 | tf_op jit(solution)/shard_map/ppermute | solution.py:35
  140.9 15.5 %collective-permute-start.27 = (bf16[256,384]{1,0:T(8,128)(2,1)S(1)}, bf16[256,384]{1,0:T(8,128)(2,1)S(1)}, u32[]{:S(2)}, u32[]{:S(2)}) collective-permute-start(bf16[256,384]{1,0:T(8,128)(2,1)S(1)} %get-tuple-element.93), channel_id=1, source_target_pairs={{0,8},{8,16},{16,24},{24,0},{1,9},{9,17},{17,25},{25,1},{2,10},{10... | collective-permute-start | bytes 589832 | tf_op jit(solution)/shard_map/ppermute | solution.py:35
  150.7 27.4 %collective-permute-start.23 = (bf16[512,384]{1,0:T(8,128)(2,1)S(1)}, bf16[512,384]{1,0:T(8,128)(2,1)S(1)}, u32[]{:S(2)}, u32[]{:S(2)}) collective-permute-start(bf16[512,384]{1,0:T(8,128)(2,1)S(1)} %get-tuple-element.65), channel_id=1, source_target_pairs={{0,8},{8,16},{16,24},{24,0},{1,9},{9,17},{17,25},{25,1},{2,10},{10... | collective-permute-start | bytes 1179656 | tf_op jit(solution)/shard_map/ppermute | solution.py:35
  151.7 26.4 %collective-permute-start.24 = (bf16[512,384]{1,0:T(8,128)(2,1)S(1)}, bf16[512,384]{1,0:T(8,128)(2,1)S(1)}, u32[]{:S(2)}, u32[]{:S(2)}) collective-permute-start(bf16[512,384]{1,0:T(8,128)(2,1)S(1)} %get-tuple-element.66), channel_id=1, source_target_pairs={{0,24},{8,0},{16,8},{24,16},{1,25},{9,1},{17,9},{25,17},{2,26},{10... | collective-permute-start | bytes 1179656 | tf_op jit(solution)/shard_map/ppermute | solution.py:35
  153.5 24.7 %collective-permute-start.25 = (bf16[512,384]{1,0:T(8,128)(2,1)S(1)}, bf16[512,384]{1,0:T(8,128)(2,1)S(1)}, u32[]{:S(2)}, u32[]{:S(2)}) collective-permute-start(bf16[512,384]{1,0:T(8,128)(2,1)S(1)} %get-tuple-element.67), channel_id=1, source_target_pairs={{0,16},{8,24},{16,0},{24,8},{1,17},{9,25},{17,1},{25,9},{2,18},{10... | collective-permute-start | bytes 1179656 | tf_op jit(solution)/shard_map/ppermute | solution.py:35
  154.2 20.5 %collective-permute-start.29 = (bf16[256,384]{1,0:T(8,128)(2,1)S(1)}, bf16[256,384]{1,0:T(8,128)(2,1)S(1)}, u32[]{:S(2)}, u32[]{:S(2)}) collective-permute-start(bf16[256,384]{1,0:T(8,128)(2,1)S(1)} %get-tuple-element.94), channel_id=1, source_target_pairs={{0,16},{8,24},{16,0},{24,8},{1,17},{9,25},{17,1},{25,9},{2,18},{10... | collective-permute-start | bytes 589832 | tf_op jit(solution)/shard_map/ppermute | solution.py:35
  156.4 20.9 %collective-permute-start.28 = (bf16[256,384]{1,0:T(8,128)(2,1)S(1)}, bf16[256,384]{1,0:T(8,128)(2,1)S(1)}, u32[]{:S(2)}, u32[]{:S(2)}) collective-permute-start(bf16[256,384]{1,0:T(8,128)(2,1)S(1)} %get-tuple-element.95), channel_id=1, source_target_pairs={{0,24},{8,0},{16,8},{24,16},{1,25},{9,1},{17,9},{25,17},{2,26},{10... | collective-permute-start | bytes 589832 | tf_op jit(solution)/shard_map/ppermute | solution.py:35
  179.1 6.2 %collective-permute-start.35 = (bf16[128,384]{1,0:T(8,128)(2,1)S(1)}, bf16[128,384]{1,0:T(8,128)(2,1)S(1)}, u32[]{:S(2)}, u32[]{:S(2)}) collective-permute-start(bf16[128,384]{1,0:T(8,128)(2,1)S(1)} %get-tuple-element.83.own), channel_id=1, source_target_pairs={{0,32},{32,64},{64,96},{96,0},{1,33},{33,65},{65,97},{97,1},{2,34}... | collective-permute-start | bytes 294920 | tf_op jit(solution)/shard_map/ppermute | solution.py:35
  181.6 6.0 %collective-permute-start.34 = (bf16[128,384]{1,0:T(8,128)(2,1)S(1)}, bf16[128,384]{1,0:T(8,128)(2,1)S(1)}, u32[]{:S(2)}, u32[]{:S(2)}) collective-permute-start(bf16[128,384]{1,0:T(8,128)(2,1)S(1)} %get-tuple-element.83.own), channel_id=1, source_target_pairs={{0,64},{32,96},{64,0},{96,32},{1,65},{33,97},{65,1},{97,33},{2,66}... | collective-permute-start | bytes 294920 | tf_op jit(solution)/shard_map/ppermute | solution.py:35
  184.5 4.7 %collective-permute-start.33 = (bf16[128,384]{1,0:T(8,128)(2,1)S(1)}, bf16[128,384]{1,0:T(8,128)(2,1)S(1)}, u32[]{:S(2)}, u32[]{:S(2)}) collective-permute-start(bf16[128,384]{1,0:T(8,128)(2,1)S(1)} %get-tuple-element.83.own), channel_id=1, source_target_pairs={{0,96},{32,0},{64,32},{96,64},{1,97},{33,1},{65,33},{97,65},{2,98}... | collective-permute-start | bytes 294920 | tf_op jit(solution)/shard_map/ppermute | solution.py:35
  (1 other events, 0.7 us)
